TPU v7x, 32 devices: a whole 2x2x4 slice. The times are simulated.
32 devices in a mesh: dp: 8 (over z, y), chan: 4 (over x, core).
Axes of the slice: x: 2, y: 2, z: 4, core: 2. Of those that a mesh axis runs over, the one named last changes fastest.
Arguments:
- inputs: bfloat16 [16, 16, 16, 512], P('dp', None, None, 'chan'), may hold values from -6 to 6
- affine: float32 [3, 2, 512], P(None, None, 'chan'), may hold values from 0.3 to 1.3
- image_sizes: int32 [16, 2], P('dp'), may hold values from 8 to 16
- labels: int32 [16, 16, 16, 7], P('dp'), may hold values from 0 to 20
- label_mask: int32 [16, 16, 16, 7], P('dp'), may hold values 0 or 1
- unit_slots: int32 [54], replicated, may hold values from 0 to 55, as said below
- conv_master: float32 [56, 256, 512], P('dp', None, 'chan'), may hold values from -0.09375 to 0.09375
- conv_first: float32 [56, 256, 512], P('dp', None, 'chan'), may hold values from -0.00390625 to 0.00390625
- conv_second: float32 [56, 256, 512], P('dp', None, 'chan'), may hold values from 2.746582e-09 to 4.3945313e-08
- head_master: float32 [7, 256, 512], P(None, 'chan'), may hold values from -0.25 to 0.25
- head_first: float32 [7, 256, 512], P(None, 'chan'), may hold values from -0.0048828125 to 0.0048828125
- head_second: float32 [7, 256, 512], P(None, 'chan'), may hold values from 4.8828124e-09 to 7.8125e-08
- join_master: float32 [7, 256, 21], P(None, 'chan'), may hold values from -4 to 4
- join_first: float32 [7, 256, 21], P(None, 'chan'), may hold values from -0.0012207031 to 0.0012207031
- join_second: float32 [7, 256, 21], P(None, 'chan'), may hold values from 3.0517577e-10 to 4.8828124e-09
- scale_master: float32 [7, 256], P(None, 'chan'), may hold values from 1 to 4
- scale_first: float32 [7, 256], P(None, 'chan'), may hold values from -0.0024414062 to 0.0024414062
- scale_second: float32 [7, 256], P(None, 'chan'), may hold values from 1.2207031e-09 to 1.953125e-08
- step_count: int32 [1], replicated, may hold values from 2 to 20
Outputs:
- loss: float32 [1], replicated
- conv_new: float32 [56, 256, 512], P('dp', None, 'chan')
- conv_first_new: float32 [56, 256, 512], P('dp', None, 'chan')
- conv_second_new: float32 [56, 256, 512], P('dp', None, 'chan')
- head_new: float32 [7, 256, 512], P(None, 'chan')
- head_first_new: float32 [7, 256, 512], P(None, 'chan')
- head_second_new: float32 [7, 256, 512], P(None, 'chan')
- join_new: float32 [7, 256, 21], P(None, 'chan')
- join_first_new: float32 [7, 256, 21], P(None, 'chan')
- join_second_new: float32 [7, 256, 21], P(None, 'chan')
- scale_new: float32 [7, 256], P(None, 'chan')
- scale_first_new: float32 [7, 256], P(None, 'chan')
- scale_second_new: float32 [7, 256], P(None, 'chan')
Inputs may be any that keep to these rules, and one draw needn't show every extreme that they name: `unit_slots`: distinct slots; slot s belongs to index s // 7 of dp, so an index holds at most 7 blocks; slot 55 is always used.
All inputs are finite; a program needn't handle non-finite values. No bound on the sum of `label_mask` on one device may be relied on, other than what follows from the above.
Results may differ from a plain program's by a relative error of at most 0.0035.
The roundings to bfloat16 on the way count: a program that leaves them out, or rounds other values in their place, can miss the bound.
Values may be sent and summed in bfloat16 or wider, within the bound.
A program may use at most 128 MiB of HBM per device.

v0:
```python
import jax
import jax.numpy as jnp
from jax import lax
from jax.sharding import PartitionSpec as P

C = 512
K = 21
TASKS = 7
LAYERS = 3
H = 16
W = 16


beta_one = 0.9
beta_two = 0.999
eps_adam = 1e-08
decay_rate = 0.01
eps_norm = 1e-06


def valid_pixels(image_sizes):
    row_ids = jnp.arange(H)[None, :, None] < image_sizes[:, 0][:, None, None]
    col_ids = jnp.arange(W)[None, None, :] < image_sizes[:, 1][:, None, None]
    return (row_ids & col_ids).astype(jnp.float32)[..., None]


def adamw(weight, gradient, moment_one, moment_two, step_rate, step_count):
    step_float = step_count[0].astype(jnp.float32)
    moment_one = beta_one * moment_one + (1.0 - beta_one) * gradient
    moment_two = beta_two * moment_two + (1.0 - beta_two) * gradient * gradient
    first_hat = moment_one / (1.0 - beta_one**step_float)
    second_hat = moment_two / (1.0 - beta_two**step_float)
    weight = weight - step_rate * (
        first_hat / (jnp.sqrt(second_hat) + eps_adam) + decay_rate * weight
    )
    return (weight, moment_one, moment_two)


def pad_image(values):
    return jnp.pad(values, ((0, 0), (1, 1), (1, 1), (0, 0)))


def gather_channels(local_part):
    return lax.all_gather(local_part, "chan", axis=3, tiled=True)


def channel_sum(partial_term):
    return lax.psum_scatter(partial_term, "chan", scatter_dimension=3, tiled=True)


def conv_forward(gathered, kernels):
    padded = pad_image(gathered)
    summed = jnp.zeros(gathered.shape[:3] + (kernels.shape[2],), jnp.float32)
    for tap_index in range(9):
        row_shift, col_shift = divmod(tap_index, 3)
        window = padded[:, row_shift : row_shift + H, col_shift : col_shift + W, :]
        summed = summed + jnp.einsum(
            "ihwc,cd->ihwd", window, kernels[tap_index], preferred_element_type=jnp.float32
        )
    return summed


def conv_backward(gathered, grad_linear, kernels, need_input):
    padded = pad_image(gathered)
    grad_padded = pad_image(grad_linear)
    weight_grads = []
    spread_sum = jnp.zeros(gathered.shape, jnp.float32)
    for tap_index in range(9):
        row_shift, col_shift = divmod(tap_index, 3)
        window = padded[:, row_shift : row_shift + H, col_shift : col_shift + W, :]
        weight_grads.append(
            jnp.einsum("ihwc,ihwd->cd", window, grad_linear, preferred_element_type=jnp.float32)
        )
        if need_input:
            back_window = grad_padded[
                :, 2 - row_shift : 2 - row_shift + H, 2 - col_shift : 2 - col_shift + W, :
            ]
            spread_sum = spread_sum + jnp.einsum(
                "ihwd,cd->ihwc", back_window, kernels[tap_index], preferred_element_type=jnp.float32
            )
    input_grad = channel_sum(spread_sum) if need_input else None
    return (jnp.stack(weight_grads), input_grad)


def per_device(
    inputs,
    affine,
    image_sizes,
    labels,
    label_mask,
    unit_slots,
    conv_master,
    conv_first,
    conv_second,
    head_master,
    head_first,
    head_second,
    join_master,
    join_first,
    join_second,
    scale_master,
    scale_first,
    scale_second,
    step_count,
):
    inside = valid_pixels(image_sizes)
    slot_count = conv_master.shape[0]
    every_slot = lax.all_gather(conv_master.astype(jnp.bfloat16), "dp", axis=0, tiled=True)
    blocks = jnp.take(every_slot, unit_slots, axis=0)
    kernels = blocks.reshape(LAYERS, 9, C, blocks.shape[2])
    head_low = head_master.astype(jnp.bfloat16)
    join_low = join_master.astype(jnp.bfloat16)
    label_keep = label_mask.astype(jnp.float32) * inside
    counts = jnp.maximum(lax.psum(jnp.sum(label_keep, axis=(0, 1, 2)), "dp"), 1.0)
    current = (inputs.astype(jnp.float32) * inside).astype(jnp.bfloat16)
    gathered_list, linear_list, local_list = ([], [], [])
    for layer_index in range(LAYERS):
        gathered = gather_channels(current)
        linear = conv_forward(gathered, kernels[layer_index])
        output = (jax.nn.relu(linear) * affine[layer_index, 0] + affine[layer_index, 1]) * inside
        gathered_list.append(gathered)
        linear_list.append(linear)
        local_list.append(current)
        current = output.astype(jnp.bfloat16)
    features = gather_channels(current)
    flat_features = features.reshape(-1, C)
    hidden = jnp.einsum("pc,tdc->ptd", flat_features, head_low, preferred_element_type=jnp.float32)
    squares = lax.psum(jnp.sum(hidden * hidden, axis=2), "chan")
    inverse = lax.rsqrt(squares + eps_norm)[:, :, None]
    normed = hidden * inverse
    scaled = (scale_master[None] * normed).astype(jnp.bfloat16)
    partial_logits = jnp.einsum(
        "ptd,tdk->ptk", scaled, join_low, preferred_element_type=jnp.float32
    )
    logits = lax.psum(partial_logits, "chan")
    largest = jnp.max(logits, axis=2, keepdims=True)
    shifted = jnp.exp(logits - largest)
    totals = jnp.sum(shifted, axis=2, keepdims=True)
    log_norm = largest[..., 0] + jnp.log(totals[..., 0])
    onehot = (labels.reshape(-1, TASKS)[:, :, None] == jnp.arange(K)[None, None, :]).astype(
        jnp.float32
    )
    picked = jnp.sum(onehot * logits, axis=2)
    pixel_weight = label_keep.reshape(-1, TASKS) / counts[None, :]
    loss_local = jnp.sum(pixel_weight * (log_norm - picked))
    grad_logits = (pixel_weight[:, :, None] * (shifted / totals - onehot)).astype(jnp.bfloat16)
    grad_scaled = jnp.einsum(
        "ptk,tdk->ptd", grad_logits, join_low, preferred_element_type=jnp.float32
    )
    join_grad = jnp.einsum("ptd,ptk->tdk", scaled, grad_logits, preferred_element_type=jnp.float32)
    scale_grad = jnp.sum(grad_scaled * normed, axis=0)
    grad_normed = grad_scaled * scale_master[None]
    along_norm = lax.psum(jnp.sum(normed * grad_normed, axis=2), "chan")[:, :, None]
    grad_hidden = ((grad_normed - normed * along_norm) * inverse).astype(jnp.bfloat16)
    head_grad = jnp.einsum(
        "ptd,pc->tdc", grad_hidden, flat_features, preferred_element_type=jnp.float32
    )
    grad_flat = jnp.einsum("ptd,tdc->pc", grad_hidden, head_low, preferred_element_type=jnp.float32)
    grad_current = channel_sum(grad_flat.reshape(features.shape))
    conv_grads = [None] * LAYERS
    for layer_index in reversed(range(LAYERS)):
        linear = linear_list[layer_index]
        scaled_back = grad_current * inside * affine[layer_index, 0]
        grad_linear = jnp.where(linear > 0, scaled_back, 0.0).astype(jnp.bfloat16)
        gathered = gathered_list[layer_index]
        conv_grads[layer_index], grad_current = conv_backward(
            gathered, grad_linear, kernels[layer_index], layer_index > 0
        )
    unit_grads = jnp.stack(conv_grads).reshape(-1, C // 2, kernels.shape[3])
    summed_all = lax.psum(unit_grads, "dp")
    slot_base = lax.axis_index("dp") * slot_count
    picking = ((slot_base + jnp.arange(slot_count))[:, None] == unit_slots[None, :]).astype(
        jnp.float32
    )
    slot_grads = jnp.einsum("su,urc->src", picking, summed_all, precision=lax.Precision.HIGHEST)
    head_total, join_total, scale_total, loss_total = lax.psum(
        (head_grad, join_grad, scale_grad, loss_local), "dp"
    )
    conv_out = adamw(conv_master, slot_grads, conv_first, conv_second, 0.01, step_count)
    head_out = adamw(head_master, head_total, head_first, head_second, 0.03, step_count)
    join_out = adamw(join_master, join_total, join_first, join_second, 0.4, step_count)
    scale_out = adamw(scale_master, scale_total, scale_first, scale_second, 0.8, step_count)
    return (loss_total.reshape(1),) + conv_out + head_out + join_out + scale_out


def solution(mesh):
    placed = (
        P("dp", None, None, "chan"),
        P(None, None, "chan"),
        P("dp", None),
        P("dp", None, None, None),
        P("dp", None, None, None),
        P(),
        P("dp", None, "chan"),
        P("dp", None, "chan"),
        P("dp", None, "chan"),
        P(None, "chan", None),
        P(None, "chan", None),
        P(None, "chan", None),
        P(None, "chan", None),
        P(None, "chan", None),
        P(None, "chan", None),
        P(None, "chan"),
        P(None, "chan"),
        P(None, "chan"),
        P(),
    )
    return jax.shard_map(
        per_device,
        mesh=mesh,
        in_specs=placed,
        out_specs=(
            P(),
            P("dp", None, "chan"),
            P("dp", None, "chan"),
            P("dp", None, "chan"),
            P(None, "chan", None),
            P(None, "chan", None),
            P(None, "chan", None),
            P(None, "chan", None),
            P(None, "chan", None),
            P(None, "chan", None),
            P(None, "chan"),
            P(None, "chan"),
            P(None, "chan"),
        ),
        check_vma=False,
    )
```

profile of v0, /device:TPU:0, one launch (start us, length us, event | category | flops | bytes accessed | tf_op | source)
XLA Modules:
  0.0 576.5 jit_solution(2468389914004056909)
XLA Ops:
  7.3 2.0 convert_element_type.77
  10.5 1.1 fusion.130
  11.5 23.7 %psum.63 = f32[7]{0:T(128)S(1)} all-reduce(f32[7]{0:T(128)S(1)} %get-tuple-element.75), channel_id=1, replica_groups=mesh['dp'=8,'chan'=4] {'dp'}, use_global_device_ids=true, to_apply=%region_1.2 | all-reduce | flops 7 | bytes 56 | tf_op jit(solution)/shard_map/psum | solution.py:114
  36.5 7.2 %all_gather.15 = bf16[2,16,16,512]{3,2,1,0:T(8,128)(2,1)S(1)} all-gather(bf16[2,16,16,128]{3,2,1,0:T(8,128)(2,1)S(1)} %multiply_convert_fusion.6), channel_id=1, replica_groups=mesh['dp'=8,'chan'=4] {'chan'}, dimensions={3}, use_global_device_ids=true | all-gather | bytes 655360 | tf_op jit(solution)/shard_map/all_gather | solution.py:44
  43.8 36.1 %all-gather.2.cloned.1.call-done = bf16[56,256,128]{2,1,0:T(8,128)(2,1)} async-done(((bf16[7,256,128]{2,1,0:T(8,128)(2,1)}), bf16[56,256,128]{2,1,0:T(8,128)(2,1)}) %all-gather.2.cloned.1.call-update) | async-done | bytes 3670032 | tf_op jit(solution)/shard_map/all_gather | solution.py:108
  79.9 4.9 gather_fusion
  84.8 2.4 broadcast_select_fusion
  91.1 7.2 %all_gather.17 = bf16[2,16,16,512]{3,2,1,0:T(8,128)(2,1)S(1)} all-gather(bf16[2,16,16,128]{3,2,1,0:T(8,128)(2,1)S(1)} %get-tuple-element.134), channel_id=1, replica_groups=mesh['dp'=8,'chan'=4] {'chan'}, dimensions={3}, use_global_device_ids=true | all-gather | bytes 655360 | tf_op jit(solution)/shard_map/all_gather | solution.py:44
  101.9 7.3 %all_gather.18 = bf16[2,16,16,512]{3,2,1,0:T(8,128)(2,1)S(1)} all-gather(bf16[2,16,16,128]{3,2,1,0:T(8,128)(2,1)S(1)} %get-tuple-element.136), channel_id=1, replica_groups=mesh['dp'=8,'chan'=4] {'chan'}, dimensions={3}, use_global_device_ids=true | all-gather | bytes 655360 | tf_op jit(solution)/shard_map/all_gather | solution.py:44
  112.8 7.3 %all_gather.19 = bf16[2,16,16,512]{3,2,1,0:T(8,128)(2,1)S(1)} all-gather(bf16[2,16,16,128]{3,2,1,0:T(8,128)(2,1)S(1)} %get-tuple-element.138), channel_id=1, replica_groups=mesh['dp'=8,'chan'=4] {'chan'}, dimensions={3}, use_global_device_ids=true | all-gather | bytes 655360 | tf_op jit(solution)/shard_map/all_gather | solution.py:44
  120.6 10.7 %psum.64 = f32[512,7]{0,1:T(8,128)S(1)} all-reduce(f32[512,7]{0,1:T(8,128)S(1)} %get-tuple-element.140), channel_id=1, replica_groups=mesh['dp'=8,'chan'=4] {'chan'}, use_global_device_ids=true, to_apply=%region_3.4 | all-reduce | flops 3584 | bytes 28672 | tf_op jit(solution)/shard_map/psum | solution.py:128
  132.5 30.9 %all-reduce.10.cloned.1.call-done = f32[512,7,21]{0,2,1:T(8,128)} async-done(((f32[512,7,21]{0,2,1:T(8,128)}), f32[512,7,21]{0,2,1:T(8,128)}) %all-reduce.10.cloned.1.call-update) | async-done | bytes 301072 | tf_op jit(solution)/shard_map/psum | solution.py:135
  164.4 1.7 fusion.59
  166.2 2.8 multiply_reduce_fusion
  169.0 10.3 %psum.67 = f32[512,7]{0,1:T(8,128)S(1)} all-reduce(f32[512,7]{0,1:T(8,128)S(1)} %get-tuple-element.53), channel_id=1, replica_groups=mesh['dp'=8,'chan'=4] {'chan'}, use_global_device_ids=true, to_apply=%region_11.12 | all-reduce | flops 3584 | bytes 28672 | tf_op jit(solution)/shard_map/psum | solution.py:153
  179.3 1.4 multiply_convert_fusion
  180.7 2.7 fusion.60
  183.5 2.3 pad_slice_fusion.16
  185.9 2.3 pad_slice_fusion
  188.3 2.3 pad_slice_fusion.8
  190.6 1.3 fusion.134
  191.9 16.6 %reduce-scatter.4.cloned.1.call-done = f32[2,16,16,128]{3,2,1,0:T(8,128)} async-done(((f32[2,16,16,512]{3,2,1,0:T(8,128)}), f32[2,16,16,128]{3,2,1,0:T(8,128)}) %reduce-scatter.4.cloned.1.call-update) | async-done | bytes 262160 | tf_op jit(solution)/shard_map/reduce_scatter | solution.py:48
  208.5 1.1 select_convert_fusion.2
  209.6 1.2 fusion.66
  210.9 1.2 convolution_add_fusion.15
  214.9 1.3 convolution_add_fusion.8
  216.2 2.1 fusion.8
  222.5 1.1 fusion.3
  223.5 1.0 fusion.2
  224.6 1.1 fusion.1
  226.7 14.3 %reduce-scatter.6.cloned.1.call-done = f32[2,16,16,128]{3,2,1,0:T(8,128)} async-done(((f32[2,16,16,512]{3,2,1,0:T(8,128)}), f32[2,16,16,128]{3,2,1,0:T(8,128)}) %reduce-scatter.6.cloned.1.call-update) | async-done | bytes 262160 | tf_op jit(solution)/shard_map/reduce_scatter | solution.py:48
  241.0 1.1 select_convert_fusion.1
  245.5 1.3 convolution_add_fusion
  250.2 1.0 fusion.14
  251.3 1.0 fusion.13
  252.4 1.1 fusion.12
  255.6 1.0 fusion.9
  256.6 15.2 %reduce-scatter.8.cloned.1.call-done = f32[2,16,16,128]{3,2,1,0:T(8,128)} async-done(((f32[2,16,16,512]{3,2,1,0:T(8,128)}), f32[2,16,16,128]{3,2,1,0:T(8,128)}) %reduce-scatter.8.cloned.1.call-update) | async-done | bytes 262160 | tf_op jit(solution)/shard_map/reduce_scatter | solution.py:48
  271.8 1.1 select_convert_fusion
  278.3 2.9 pad_maximum_fusion
  281.1 7.1 %copy.215 = f32[54,256,128]{2,0,1:T(8,128)} copy(f32[54,256,128]{2,1,0:T(8,128)S(1)} %bitcast.450) | data formatting | bytes 14155776 | tf_op jit(solution)/shard_map/reshape | solution.py:169
  290.6 41.9 %all-reduce.5 = (f32[1]{0:T(128)}, f32[7,64,21]{1,2,0:T(8,128)S(1)}, f32[7,64]{1,0:T(8,128)S(1)}) all-reduce(f32[1]{0:T(128)} %bitcast.90, f32[7,64,21]{1,2,0:T(8,128)S(1)} %fusion.69, f32[7,64]{1,0:T(8,128)S(1)} %copy-done.86), channel_id=1, replica_groups=mesh['dp'=8,'chan'=4] {'dp'}, use_global_device_ids=true, to_apply=%region_9.10 | all-reduce | flops 9857 | bytes 78856 | tf_op jit(solution)/shard_map/psum | solution.py:176
  333.8 221.9 %all-reduce.12.cloned.1.call-done = (f32[54,256,128]{2,0,1:T(8,128)}, f32[7,64,512]{2,1,0:T(8,128)}) async-done(((f32[54,256,128]{2,0,1:T(8,128)}, f32[7,64,512]{2,1,0:T(8,128)}), (f32[54,256,128]{2,0,1:T(8,128)}, f32[7,64,512]{2,1,0:T(8,128)})) %all-reduce.12.cloned.1.call-update) | async-done | bytes 7995408 | tf_op jit(solution)/shard_map/psum | solution.py:170
  555.7 7.8 %copy_subtract_fusion = (f32[7,256,128]{2,0,1:T(8,128)S(1)}, f32[7,256,128]{2,0,1:T(8,128)S(1)}, f32[7,256,128]{2,0,1:T(8,128)S(1)}) fusion(f32[7,256,128]{2,1,0:T(8,128)S(1)} %copy-done, f32[]{:T(128)} %bitcast.217, f32[]{:T(128)} %bitcast.216, f32[7,256,128]{2,1,0:T(8,128)} %param.27, f32[7,256,128]{2,1,0:T(8,128)} %param.26, ...), kind=kOutput, calls=%fused_computation.126 | convolution fusion | flops 152076672 | bytes 12583164 | tf_op jit(solution)/shard_map/su,urc->src/dot_general | solution.py:175
  563.5 1.1 copy.219
  564.6 1.1 copy.220
  565.6 1.1 copy.221
  567.2 2.0 multiply_subtract_fusion
  (288 shorter events, 41.2 us)
Async XLA Ops:
  7.2 29.1 %copy-start.92 = (s32[54]{0:T(128)S(1)}, s32[54]{0:T(128)}, u32[]{:S(2)}) copy-start(s32[54]{0:T(128)} %param.24) | copy-start | bytes 652
  7.2 29.2 %copy-start.71 = (bf16[2,16,16,128]{3,2,1,0:T(8,128)(2,1)S(1)}, bf16[2,16,16,128]{3,2,1,0:T(8,128)(2,1)}, u32[]{:S(2)}) copy-start(bf16[2,16,16,128]{3,2,1,0:T(8,128)(2,1)} %param.19) | copy-start | bytes 393220
  7.2 36.5 %copy-start.89 = (f32[3,2,128]{2,1,0:T(2,128)S(1)}, f32[3,2,128]{2,1,0:T(2,128)}, u32[]{:S(2)}) copy-start(f32[3,2,128]{2,1,0:T(2,128)} %param.20) | copy-start | bytes 9220
  7.2 72.7 %all-gather.2.cloned.1.call-start = ((), (), s32[]{:S(2)}) async-start(), calls=%async_computation.3 | async-start | bytes 4128768 | tf_op jit(solution)/shard_map/all_gather | solution.py:108
  9.3 154.1 %all-reduce.10.cloned.1.call-start = ((), (), s32[]{:S(2)}) async-start(), calls=%async_computation.4 | async-start | bytes 688128 | tf_op jit(solution)/shard_map/psum | solution.py:135
  11.5 73.2 %copy-start.41 = (f32[2,16,16,7]{2,1,0,3:T(8,128)}, f32[2,16,16,7]{2,1,0,3:T(8,128)S(1)}, u32[]{:S(2)}) copy-start(f32[2,16,16,7]{2,1,0,3:T(8,128)S(1)} %get-tuple-element.76) | copy-start | bytes 43012
  36.2 130.0 %copy-start.75 = (s32[512,7]{0,1:T(8,128)}, s32[512,7]{0,1:T(8,128)S(1)}, u32[]{:S(2)}) copy-start(s32[512,7]{0,1:T(8,128)S(1)} %eq.28) | copy-start | bytes 43012
  43.7 88.7 %copy-start.90 = (f32[7]{0:T(128)}, f32[7]{0:T(128)S(1)}, u32[]{:S(2)}) copy-start(f32[7]{0:T(128)S(1)} %broadcast_maximum_fusion) | copy-start | bytes 88
  43.8 46.3 %copy-start.81 = (f32[128]{0:T(128)}, f32[128]{0:T(128)S(1)}, u32[]{:S(2)}) copy-start(f32[128]{0:T(128)S(1)} %get-tuple-element.132) | copy-start | bytes 1540
  43.8 57.1 %copy-start.83 = (f32[128]{0:T(128)}, f32[128]{0:T(128)S(1)}, u32[]{:S(2)}) copy-start(f32[128]{0:T(128)S(1)} %get-tuple-element.130) | copy-start | bytes 1540
  43.8 68.0 %copy-start.85 = (f32[128]{0:T(128)}, f32[128]{0:T(128)S(1)}, u32[]{:S(2)}) copy-start(f32[128]{0:T(128)S(1)} %get-tuple-element.128) | copy-start | bytes 1540
  87.4 12.2 %copy-start.12 = (bf16[2,256,128]{2,1,0:T(8,128)(2,1)}, bf16[2,256,128]{2,1,0:T(8,128)(2,1)S(1)}, u32[]{:S(2)}) copy-start(bf16[2,256,128]{2,1,0:T(8,128)(2,1)S(1)} %get-tuple-element.90) | copy-start | bytes 393220
  87.4 12.5 %copy-start.10 = (bf16[2,256,128]{2,1,0:T(8,128)(2,1)}, bf16[2,256,128]{2,1,0:T(8,128)(2,1)S(1)}, u32[]{:S(2)}) copy-start(bf16[2,256,128]{2,1,0:T(8,128)(2,1)S(1)} %get-tuple-element.89) | copy-start | bytes 393220
  87.4 12.8 %copy-start.8 = (bf16[2,256,128]{2,1,0:T(8,128)(2,1)}, bf16[2,256,128]{2,1,0:T(8,128)(2,1)S(1)}, u32[]{:S(2)}) copy-start(bf16[2,256,128]{2,1,0:T(8,128)(2,1)S(1)} %get-tuple-element.88) | copy-start | bytes 393220
  87.4 13.1 %copy-start.6 = (bf16[2,256,128]{2,1,0:T(8,128)(2,1)}, bf16[2,256,128]{2,1,0:T(8,128)(2,1)S(1)}, u32[]{:S(2)}) copy-start(bf16[2,256,128]{2,1,0:T(8,128)(2,1)S(1)} %get-tuple-element.87) | copy-start | bytes 393220
  87.4 13.4 %copy-start.4 = (bf16[2,256,128]{2,1,0:T(8,128)(2,1)}, bf16[2,256,128]{2,1,0:T(8,128)(2,1)S(1)}, u32[]{:S(2)}) copy-start(bf16[2,256,128]{2,1,0:T(8,128)(2,1)S(1)} %get-tuple-element.86) | copy-start | bytes 393220
  87.4 21.8 %copy-start.37 = (bf16[2,256,128]{2,1,0:T(8,128)(2,1)}, bf16[2,256,128]{2,1,0:T(8,128)(2,1)S(1)}, u32[]{:S(2)}) copy-start(bf16[2,256,128]{2,1,0:T(8,128)(2,1)S(1)} %get-tuple-element.85) | copy-start | bytes 393220
  87.4 22.1 %copy-start.36 = (bf16[2,256,128]{2,1,0:T(8,128)(2,1)}, bf16[2,256,128]{2,1,0:T(8,128)(2,1)S(1)}, u32[]{:S(2)}) copy-start(bf16[2,256,128]{2,1,0:T(8,128)(2,1)S(1)} %get-tuple-element.84) | copy-start | bytes 393220
  87.4 22.4 %copy-start.34 = (bf16[2,256,128]{2,1,0:T(8,128)(2,1)}, bf16[2,256,128]{2,1,0:T(8,128)(2,1)S(1)}, u32[]{:S(2)}) copy-start(bf16[2,256,128]{2,1,0:T(8,128)(2,1)S(1)} %get-tuple-element.83) | copy-start | bytes 393220
  87.5 22.7 %copy-start.32 = (bf16[2,256,128]{2,1,0:T(8,128)(2,1)}, bf16[2,256,128]{2,1,0:T(8,128)(2,1)S(1)}, u32[]{:S(2)}) copy-start(bf16[2,256,128]{2,1,0:T(8,128)(2,1)S(1)} %get-tuple-element.82) | copy-start | bytes 393220
  87.5 23.0 %copy-start.30 = (bf16[2,256,128]{2,1,0:T(8,128)(2,1)}, bf16[2,256,128]{2,1,0:T(8,128)(2,1)S(1)}, u32[]{:S(2)}) copy-start(bf16[2,256,128]{2,1,0:T(8,128)(2,1)S(1)} %get-tuple-element.81) | copy-start | bytes 393220
  87.5 23.3 %copy-start.28 = (bf16[2,256,128]{2,1,0:T(8,128)(2,1)}, bf16[2,256,128]{2,1,0:T(8,128)(2,1)S(1)}, u32[]{:S(2)}) copy-start(bf16[2,256,128]{2,1,0:T(8,128)(2,1)S(1)} %get-tuple-element.80) | copy-start | bytes 393220
  87.5 23.6 %copy-start.26 = (bf16[2,256,128]{2,1,0:T(8,128)(2,1)}, bf16[2,256,128]{2,1,0:T(8,128)(2,1)S(1)}, u32[]{:S(2)}) copy-start(bf16[2,256,128]{2,1,0:T(8,128)(2,1)S(1)} %get-tuple-element.79) | copy-start | bytes 393220
  87.5 23.9 %copy-start.24 = (bf16[2,256,128]{2,1,0:T(8,128)(2,1)}, bf16[2,256,128]{2,1,0:T(8,128)(2,1)S(1)}, u32[]{:S(2)}) copy-start(bf16[2,256,128]{2,1,0:T(8,128)(2,1)S(1)} %get-tuple-element.78) | copy-start | bytes 393220
  87.5 24.3 %copy-start.22 = (bf16[2,256,128]{2,1,0:T(8,128)(2,1)}, bf16[2,256,128]{2,1,0:T(8,128)(2,1)S(1)}, u32[]{:S(2)}) copy-start(bf16[2,256,128]{2,1,0:T(8,128)(2,1)S(1)} %get-tuple-element.77) | copy-start | bytes 393220
  111.7 19.5 %copy-start.69 = (f32[7,64,21]{1,2,0:T(8,128)S(1)}, f32[7,64,21]{1,2,0:T(8,128)}, u32[]{:S(2)}) copy-start(f32[7,64,21]{1,2,0:T(8,128)} %param.31) | copy-start | bytes 112900
  111.8 19.5 %copy-start.77 = (f32[7,64]{1,0:T(8,128)S(1)}, f32[7,64]{1,0:T(8,128)}, u32[]{:S(2)}) copy-start(f32[7,64]{1,0:T(8,128)} %param.34) | copy-start | bytes 5380
  132.3 76.2 %reduce-scatter.4.cloned.1.call-start = ((), (), s32[]{:S(2)}) async-start(), calls=%async_computation.5 | async-start | bytes 1310720 | tf_op jit(solution)/shard_map/reduce_scatter | solution.py:48
  132.5 46.9 %copy-start.79 = (f32[512,7]{0,1:T(8,128)}, f32[512,7]{0,1:T(8,128)S(1)}, u32[]{:S(2)}) copy-start(f32[512,7]{0,1:T(8,128)S(1)} %broadcast_divide_fusion) | copy-start | bytes 43012
  183.4 57.6 %reduce-scatter.6.cloned.1.call-start = ((), (), s32[]{:S(2)}) async-start(), calls=%async_computation.6 | async-start | bytes 1310720 | tf_op jit(solution)/shard_map/reduce_scatter | solution.py:48
  191.9 20.2 %copy-start.35 = (bf16[2,256,128]{2,1,0:T(8,128)(2,1)S(1)}, bf16[2,256,128]{2,1,0:T(8,128)(2,1)}, u32[]{:S(2)}) copy-start(bf16[2,256,128]{2,1,0:T(8,128)(2,1)} %copy-done.34) | copy-start | bytes 393220
  216.1 55.6 %reduce-scatter.8.cloned.1.call-start = ((), (), s32[]{:S(2)}) async-start(), calls=%async_computation.7 | async-start | bytes 1310720 | tf_op jit(solution)/shard_map/reduce_scatter | solution.py:48
  225.7 15.4 %copy-start.84 = (f32[128]{0:T(128)S(1)}, f32[128]{0:T(128)}, u32[]{:S(2)}) copy-start(f32[128]{0:T(128)} %copy-done.83) | copy-start | bytes 1540
  225.7 16.5 %copy-start.21 = (bf16[2,256,128]{2,1,0:T(8,128)(2,1)S(1)}, bf16[2,256,128]{2,1,0:T(8,128)(2,1)}, u32[]{:S(2)}) copy-start(bf16[2,256,128]{2,1,0:T(8,128)(2,1)} %copy-done.20) | copy-start | bytes 393220
  225.7 16.8 %copy-start.19 = (bf16[2,256,128]{2,1,0:T(8,128)(2,1)S(1)}, bf16[2,256,128]{2,1,0:T(8,128)(2,1)}, u32[]{:S(2)}) copy-start(bf16[2,256,128]{2,1,0:T(8,128)(2,1)} %copy-done.18) | copy-start | bytes 393220
  226.7 16.1 %copy-start.17 = (bf16[2,256,128]{2,1,0:T(8,128)(2,1)S(1)}, bf16[2,256,128]{2,1,0:T(8,128)(2,1)}, u32[]{:S(2)}) copy-start(bf16[2,256,128]{2,1,0:T(8,128)(2,1)} %copy-done.16) | copy-start | bytes 393220
  246.9 308.8 %all-reduce.12.cloned.1.call-start = ((), (), s32[]{:S(2)}) async-start(), calls=%async_computation.8 | async-start | bytes 16515072 | tf_op jit(solution)/shard_map/psum | solution.py:170
  255.6 16.2 %copy-start.38 = (f32[2,16,16,128]{3,2,1,0:T(8,128)S(1)}, f32[2,16,16,128]{3,2,1,0:T(8,128)}, u32[]{:S(2)}) copy-start(f32[2,16,16,128]{3,2,1,0:T(8,128)} %get-tuple-element.135) | copy-start | bytes 786436
  255.6 16.2 %copy-start.82 = (f32[128]{0:T(128)S(1)}, f32[128]{0:T(128)}, u32[]{:S(2)}) copy-start(f32[128]{0:T(128)} %copy-done.81) | copy-start | bytes 1540
  255.6 17.3 %copy-start.53 = (bf16[2,16,16,512]{3,2,1,0:T(8,128)(2,1)S(1)}, bf16[2,16,16,512]{3,2,1,0:T(8,128)(2,1)}, u32[]{:S(2)}) copy-start(bf16[2,16,16,512]{3,2,1,0:T(8,128)(2,1)} %get-tuple-element.111) | copy-start | bytes 1572868
  256.6 16.6 %copy-start.52 = (bf16[2,16,16,512]{3,2,1,0:T(8,128)(2,1)S(1)}, bf16[2,16,16,512]{3,2,1,0:T(8,128)(2,1)}, u32[]{:S(2)}) copy-start(bf16[2,16,16,512]{3,2,1,0:T(8,128)(2,1)} %get-tuple-element.105) | copy-start | bytes 1572868
  288.3 44.1 %copy-start.87 = (f32[7,64]{1,0:T(8,128)S(1)}, f32[7,64]{1,0:T(8,128)}, u32[]{:S(2)}) copy-start(f32[7,64]{1,0:T(8,128)} %param.36) | copy-start | bytes 5380
  288.3 44.1 %copy-start.88 = (f32[7,64]{1,0:T(8,128)S(1)}, f32[7,64]{1,0:T(8,128)}, u32[]{:S(2)}) copy-start(f32[7,64]{1,0:T(8,128)} %param.35) | copy-start | bytes 5380
  288.4 44.7 %copy-start.70 = (f32[7,64,21]{1,2,0:T(8,128)S(1)}, f32[7,64,21]{1,2,0:T(8,128)}, u32[]{:S(2)}) copy-start(f32[7,64,21]{1,2,0:T(8,128)} %param.31) | copy-start | bytes 112900
  288.4 44.7 %copy-start.72 = (f32[7,64,21]{1,2,0:T(8,128)S(1)}, f32[7,64,21]{1,2,0:T(8,128)}, u32[]{:S(2)}) copy-start(f32[7,64,21]{1,2,0:T(8,128)} %param.33) | copy-start | bytes 112900
  288.4 44.7 %copy-start.73 = (f32[7,64,21]{1,2,0:T(8,128)S(1)}, f32[7,64,21]{1,2,0:T(8,128)}, u32[]{:S(2)}) copy-start(f32[7,64,21]{1,2,0:T(8,128)} %param.32) | copy-start | bytes 112900
  288.4 267.3 %copy-start = (f32[7,256,128]{2,1,0:T(8,128)S(1)}, f32[7,256,128]{2,1,0:T(8,128)}, u32[]{:S(2)}) copy-start(f32[7,256,128]{2,1,0:T(8,128)} %param.25) | copy-start | bytes 2752516
  288.4 267.3 %copy-start.93 = (s32[54]{0:T(128)S(1)}, s32[54]{0:T(128)}, u32[]{:S(2)}) copy-start(s32[54]{0:T(128)} %param.24) | copy-start | bytes 652
  (52 other events, 118.7 us)
Sparse Core Ops, SparseCore 0:
  10.8 69.0 all-gather.1
  132.5 30.8 all-reduce.9
  183.6 24.9 reduce-scatter.3
  216.3 24.7 reduce-scatter.5
  247.0 24.7 reduce-scatter.7
  288.4 267.2 all-reduce.11
where the time goes:
time: 586 us; the launch traced here: 577 us
  waiting for transfers between devices  335 us (57%)
  blocking collectives  116 us (20%)
  matrix products  58.8 us (10%)
  local copies, waits for them, and re-layouts  29.6 us (5%)
  other arithmetic  20.3 us (3%)
  between operations  16.8 us (3%)
    psum x1, waiting for transfers between devices, per_device(): summed_all = lax.psum(unit_grads, 'dp')  222 us
    reduce_scatter x3, waiting for transfers between devices, channel_sum(): lax.psum_scatter(partial_term, 'chan', scatter_dimension=3, tiled=True)  46.1 us
    psum x1, blocking collectives, per_device(): lax.psum((head_grad, join_grad, scale_grad, loss_local), 'dp')  41.9 us
    all_gather x1, waiting for transfers between devices, per_device(): lax.all_gather(conv_master.astype(jnp.bfloat16), 'dp', axis=0, tiled=True)  36.1 us
    psum x1, waiting for transfers between devices, per_device(): logits = lax.psum(partial_logits, 'chan')  30.9 us
    all_gather x4, blocking collectives, gather_channels(): return lax.all_gather(local_part, 'chan', axis=3, tiled=True)  29 us
    psum x1, blocking collectives, per_device(): lax.psum(jnp.sum(label_keep, axis=(0, 1, 2)), 'dp')  23.7 us
    dot_general x27, matrix products, conv_backward(): jnp.einsum('ihwc,ihwd->cd', window, grad_linear, preferred_element_type=j...  22.9 us
  transfers between devices with their start and end apart: 6, of which 6 were waited for; matrix products, arithmetic and copies ran while one was open for 6% of the time, Pallas kernels for 0%

commit v1 on v0

v1 whole, which is shorter than its diff:
```python
import functools

import jax
import jax.numpy as jnp
from jax import lax
from jax.experimental import pallas as pl
from jax.experimental.pallas import tpu as pltpu
from jax.sharding import PartitionSpec as P

C = 512
K = 21
TASKS = 7
LAYERS = 3
H = 16
W = 16
PX = 512
IMG = 256
HC = 64
CHUNK = 272
SMALL = 16

beta_one = 0.9
beta_two = 0.999
eps_adam = 1e-08
decay_rate = 0.01
eps_norm = 1e-06

F32 = jnp.float32
BF16 = jnp.bfloat16
MESH = pl.DeviceIdType.MESH
NN = (((1,), (0,)), ((), ()))
NT = (((1,), (1,)), ((), ()))
TN = (((0,), (0,)), ((), ()))


def dot(a, b, dims, precision=None):
    return lax.dot_general(a, b, dims, precision=precision, preferred_element_type=F32)


def encode(values):
    top = jnp.max(jnp.abs(values), axis=0, keepdims=True)
    power = jnp.ceil(jnp.log2(jnp.maximum(top, 1e-30))) - 14.0
    codes = jnp.round(values * jnp.exp2(-power)).astype(jnp.int32).astype(jnp.int16)
    powers = jnp.broadcast_to(power, (16, 128)).astype(jnp.int32).astype(jnp.int16)
    return codes, powers


def decode(codes, powers):
    return codes.astype(F32) * jnp.exp2(powers.astype(F32)[0:1])


def kernel(
    n,
    slots_per,
    slots_ref,
    sizes_ref,
    inputs_ref,
    affine_ref,
    code_ref,
    conv_ref,
    head_ref,
    join_ref,
    grad_out,
    head_out,
    small_out,
    loss_out,
    wall,
    xs,
    xt,
    hall,
    jall,
    aall,
    cnt,
    losses,
    inv_ref,
    mask,
    coef,
    zacc,
    fbuf,
    gh,
    ghall,
    gfeat,
    gsend,
    grecv,
    jt,
    jsend,
    jrecv,
    gs,
    bpart,
    bcore,
    bx,
    bxs,
    dw,
    hg,
    small,
    ysend,
    yrecv,
    lsend,
    lright,
    lleft,
    bsend2,
    brecv2,
    hag,
    zsum,
    w_recv,
    w_zr,
    w_zl,
    w_y,
    x_send,
    x_recv,
    h_send,
    h_recv,
    j_send,
    j_recv,
    a_send,
    a_recv,
    c_send,
    c_recv,
    l_send,
    l_recv,
    f_send,
    f_recv,
    g_send,
    g_recv,
    q_send,
    q_recv,
    s_send,
    s_recv,
    bc_send,
    bc_recv,
    bx_send,
    bx_recv,
    y_send,
    y_recv,
    z_send,
    zr_recv,
    zl_recv,
    b_send,
    b_recv,
    t_recv,
    t_zr,
    t_zl,
    t_y,
):
    nz = n // 2
    last_b = slots_per // 7
    first_a = slots_per - last_b
    cargo = slots_per + last_b + 1
    piece = hg.shape[0] // n

    me = lax.axis_index("dp")
    ch = lax.axis_index("chan")
    z, y = me // 2, me % 2
    core = ch % 2
    partner = ch + 1 - 2 * core
    across = (ch + 2) % 4
    far = (partner + 2) % 4

    def at(dp=None, chan=None):
        return {"dp": me if dp is None else dp, "chan": ch if chan is None else chan}

    right, left, other = at(dp=me + 2), at(dp=me - 2), at(dp=z * 2 + 1 - y)
    has_right, has_left = z < nz - 1, z > 0

    def put(src, dst, send, recv, dev):
        return pltpu.make_async_remote_copy(
            src_ref=src, dst_ref=dst, send_sem=send, recv_sem=recv, device_id=dev, device_id_type=MESH
        )

    def came(ref, recv):
        put(ref, ref, recv, recv, other).wait_recv()

    def left_it(ref, send):
        put(ref, ref, send, send, other).wait_send()

    def loop(count, body):
        lax.fori_loop(0, count, lambda i, c: (body(i), c)[1], 0)

    barrier = pltpu.get_barrier_semaphore()

    def greet(i):
        pl.semaphore_signal(barrier, inc=1, device_id=at(dp=(me + i + 1) % n), device_id_type=MESH)

    loop(n - 1, greet)
    for peer in (partner, across, far):
        pl.semaphore_signal(barrier, inc=1, device_id=at(chan=peer), device_id_type=MESH)

    def cast_block(k):
        wall[me * slots_per + k] = conv_ref[k].astype(BF16)

    loop(slots_per, cast_block)
    pixel = lax.broadcasted_iota(jnp.int32, (IMG, 128), 0)
    row_id, col_id = pixel // W, pixel % W

    def mask_image(i):
        inside = (row_id < sizes_ref[i, 0]) & (col_id < sizes_ref[i, 1])
        rows = pl.ds(pl.multiple_of(i * IMG, IMG), IMG)
        mask[rows, :] = jnp.where(inside, 1.0, 0.0)
        xs[0, ch, rows, :] = (inputs_ref[rows, :].astype(F32) * mask[rows, :]).astype(BF16)

    loop(2, mask_image)

    def cast_head(t):
        hall[t, ch] = head_ref[t].astype(BF16)
        jall[t, ch] = join_ref[t]

    loop(TASKS, cast_head)
    aall[ch] = affine_ref[...]

    lane = lax.broadcasted_iota(jnp.int32, (8, 128), 1)

    def kept(q):
        spot = (q % 2) * 128 + lane
        hit = (spot // W < sizes_ref[q // 2, 0]) & (spot % W < sizes_ref[q // 2, 1])
        return jnp.where(hit & (code_ref[q] >= 0), 1.0, 0.0)

    total_kept = kept(0) + kept(1) + kept(2) + kept(3)
    cnt[me] = jnp.broadcast_to(jnp.sum(total_kept, axis=1, keepdims=True), (8, 128))

    pl.semaphore_wait(barrier, n - 1 + 3)

    def to_right(s):
        return put(wall.at[s], wall.at[s], w_zr.at[s], w_recv.at[s], right)

    def to_left(s):
        return put(wall.at[s], wall.at[s], w_zl.at[s], w_recv.at[s], left)

    def to_other(s):
        return put(wall.at[s], wall.at[s], w_y.at[s], w_recv.at[s], other)

    def both_ways(s):
        @pl.when(has_right)
        def _():
            to_right(s).start()

        @pl.when(has_left)
        def _():
            to_left(s).start()

    def x_copy(l, i, owner, peer, k):
        rows = pl.ds(pl.multiple_of(i * IMG, IMG), IMG)
        ref = xs.at[l, owner, rows, :]
        return put(ref, ref, x_send.at[l, i, k], x_recv.at[l, i, k], at(chan=peer))

    def x_start(l, i):
        x_copy(l, i, ch, across, 0).start()
        x_copy(l, i, ch, partner, 1).start()

    def x_relay(l, i):
        x_copy(l, i, across, across, 0).wait_recv()
        x_copy(l, i, across, partner, 2).start()

    def x_arrive(l, i):
        x_copy(l, i, partner, partner, 1).wait_recv()
        x_copy(l, i, far, partner, 2).wait_recv()

    def x_drain(l, i):
        for k in range(3):
            x_copy(l, i, ch, partner, k).wait_send()

    def h_copy(t, owner, peer, k):
        ref = hall.at[t, owner]
        return put(ref, ref, h_send.at[t, k], h_recv.at[t, k], at(chan=peer))

    def j_copy(owner, peer, k):
        ref = jall.at[:, owner]
        return put(ref, ref, j_send.at[k], j_recv.at[k], at(chan=peer))

    def a_copy(owner, peer, k):
        ref = aall.at[owner]
        return put(ref, ref, a_send.at[k], a_recv.at[k], at(chan=peer))

    def c_copy(i):
        dev = (me + i + 1) % n
        return put(cnt.at[me], cnt.at[me], c_send.at[i], c_recv.at[me], at(dp=dev))

    base = me * slots_per

    def own_b(k):
        to_other(base + first_a + k).start()

    loop(last_b, own_b)

    def own_a(k):
        both_ways(base + k)
        to_other(base + k).start()

    loop(first_a, own_a)
    for i in range(2):
        x_start(0, i)

    def own_head(t):
        h_copy(t, ch, across, 0).start()
        h_copy(t, ch, partner, 1).start()

    loop(TASKS, own_head)
    loop(last_b, lambda k: both_ways(base + first_a + k))
    for copy in (j_copy, a_copy):
        copy(ch, across, 0).start()
        copy(ch, partner, 1).start()
    loop(n - 1, lambda i: c_copy(i).start())

    neighbour = (z * 2 + 1 - y) * slots_per

    def pass_b(k):
        s = neighbour + first_a + k
        came(wall.at[s], w_recv.at[s])
        both_ways(s)

    loop(last_b, pass_b)
    for i in range(2):
        x_relay(0, i)

    def relay_head(t):
        h_copy(t, across, across, 0).wait_recv()
        h_copy(t, across, partner, 2).start()

    def line_in(d, c):
        def source(zz):
            row = jnp.where(c < slots_per, y, 1 - y)
            return (zz * 2 + row) * slots_per + jnp.where(c < slots_per, c, c - last_b)

        @pl.when(z - d >= 0)
        def _():
            s = source(z - d)
            came(wall.at[s], w_recv.at[s])

            @pl.when(has_right)
            def _():
                to_right(s).start()

            @pl.when(c < first_a)
            def _():
                to_other(s).start()

        @pl.when(z + d < nz)
        def _():
            s = source(z + d)
            came(wall.at[s], w_recv.at[s])

            @pl.when(has_left)
            def _():
                to_left(s).start()

            @pl.when(c < first_a)
            def _():
                to_other(s).start()

    def first_step(c):
        pl.when(c < slots_per + last_b)(lambda: line_in(1, c))
        pl.when(c < TASKS)(lambda: relay_head(c))

    loop(max(slots_per + last_b, TASKS), first_step)
    for copy in (j_copy, a_copy):
        copy(across, across, 0).wait_recv()
        copy(across, partner, 2).start()

    def invert(s):
        def look(u, found):
            return jnp.where(slots_ref[u] == s, u, found)

        inv_ref[s] = lax.fori_loop(0, slots_ref.shape[0], look, -1)

    loop(n * slots_per, invert)

    def transpose_layer(l):
        for c in range(4):
            xt[l, c // 2, (c % 2) * 128 : (c % 2) * 128 + 128, :] = xs[l, c].T

    for i in range(2):
        x_arrive(0, i)
    transpose_layer(0)

    loop(nz - 2, lambda d: loop(slots_per + last_b, lambda c: line_in(d + 2, c)))

    def last_in(zz):
        def block(k):
            s = (zz * 2 + 1 - y) * slots_per + k
            came(wall.at[s], w_recv.at[s])

        loop(first_a, block)

    loop(nz, last_in)

    def conv_forward(l, i):
        rows = pl.ds(pl.multiple_of(i * IMG, IMG), IMG)
        left_side = jnp.concatenate([xs[l, c, rows, :] for c in range(4)], axis=1)
        zacc[...] = jnp.zeros_like(zacc)
        for first in range(0, 9, 2):
            taps = [t for t in (first, first + 1) if t < 9]
            sides = [
                jnp.concatenate([wall[slots_ref[(l * 9 + t) * 2 + h]] for h in range(2)], axis=0)
                for t in taps
            ]
            side = jnp.concatenate(sides, axis=1) if len(sides) > 1 else sides[0]
            out = dot(left_side, side, NN)
            for k, t in enumerate(taps):
                a, e = divmod(t, 3)
                part = out[:, k * 128 : (k + 1) * 128]
                if a == 0:
                    zacc[e, W:IMG, :] += part[: IMG - W]
                elif a == 1:
                    zacc[e] += part
                else:
                    zacc[e, : IMG - W, :] += part[W:]
        linear = zacc[1]
        linear += jnp.where(col_id >= 1, pltpu.roll(zacc[0], 1, 0), 0.0)
        linear += jnp.where(col_id < W - 1, pltpu.roll(zacc[2], IMG - 1, 0), 0.0)
        inside = mask[rows, :]
        gain, shift = affine_ref[2 * l : 2 * l + 1, :], affine_ref[2 * l + 1 : 2 * l + 2, :]
        passed = jnp.where(linear > 0, inside, 0.0)
        coef[l, rows, :] = passed * gain if l < LAYERS - 1 else passed
        out = (jnp.maximum(linear, 0.0) * gain + shift) * inside
        xs[l + 1, ch, rows, :] = out.astype(BF16)

    def quarter(q):
        return pl.ds(pl.multiple_of(q * 128, 128), 128)

    for l in range(LAYERS):

        def forward_image(i, l=l):
            if l > 0:
                x_relay(l, i)
                x_arrive(l, i)
            conv_forward(l, i)
            if l < LAYERS - 1:
                x_start(l + 1, i)

        loop(2, forward_image)
        if 0 < l:
            transpose_layer(l)

    def f_copy(peer, k):
        return put(xs.at[LAYERS, ch, quarter(peer), :], fbuf.at[ch], f_send.at[k], f_recv.at[ch], at(chan=peer))

    peers = (across, far, partner)
    for k, peer in enumerate(peers):
        f_copy(peer, k).start()
    for i in range(2):
        x_start(LAYERS, i)
    fbuf[ch] = xs[LAYERS, ch, quarter(ch), :]

    loop(n - 1, lambda i: came(cnt.at[(me + i + 1) % n], c_recv.at[(me + i + 1) % n]))
    counts = lax.fori_loop(0, n, lambda i, acc: acc + cnt[i], jnp.zeros((8, 128), F32))
    counts = jnp.maximum(counts, 1.0)

    def head_in(t):
        h_copy(t, partner, partner, 1).wait_recv()
        h_copy(t, far, partner, 2).wait_recv()

    loop(TASKS, head_in)
    for copy in (j_copy, a_copy):
        copy(partner, partner, 1).wait_recv()
        copy(far, partner, 2).wait_recv()
    for peer in peers:
        came(fbuf.at[peer], f_recv.at[peer])

    weight = kept(ch) / counts
    losses[0] = weight
    losses[1] = jnp.zeros((8, 128), F32)
    features = jnp.concatenate([fbuf[c] for c in range(4)], axis=1)
    gfeat[...] = jnp.zeros_like(gfeat)
    klass = lax.broadcasted_iota(jnp.int32, (32, 128), 0)

    def head_task(t):
        low = hall[t].reshape(4 * HC, C)
        both = jall[t].reshape(4 * HC, 128)
        join = both.astype(BF16)
        scale = both[:, 32:33]
        hidden = dot(low, features, NT)
        inverse = lax.rsqrt(jnp.sum(hidden * hidden, axis=0, keepdims=True) + eps_norm)
        normed = hidden * inverse
        scaled = (scale * normed).astype(BF16)
        logits = dot(join, scaled, TN)[0:32]
        real = klass < K
        largest = jnp.max(jnp.where(real, logits, -jnp.inf), axis=0, keepdims=True)
        shifted = jnp.where(real, jnp.exp(jnp.where(real, logits - largest, 0.0)), 0.0)
        totals = jnp.sum(shifted, axis=0, keepdims=True)
        onehot = klass == code_ref[ch, pl.ds(t, 1), :]
        picked = jnp.sum(jnp.where(onehot, logits, 0.0), axis=0, keepdims=True)
        share = losses[0, pl.ds(t, 1), :]
        losses[1, pl.ds(t, 1), :] = share * (largest + jnp.log(totals) - picked)
        slope = (share * (shifted / totals - jnp.where(onehot, 1.0, 0.0))).astype(BF16)
        grad_scaled = dot(join, jnp.concatenate([slope, jnp.zeros((96, 128), BF16)], axis=0), NN)
        jt[t, 0:24, :] = dot(slope, scaled, NT)[0:24]
        jt[t, 24:32, :] = dot(jnp.ones((8, 128), F32), grad_scaled * normed, NT, lax.Precision.HIGHEST)
        grad_normed = grad_scaled * scale
        along = jnp.sum(normed * grad_normed, axis=0, keepdims=True)
        grad_hidden = ((grad_normed - normed * along) * inverse).astype(BF16)
        gh[t] = grad_hidden
        gfeat[...] += dot(grad_hidden, low, TN)

    loop(TASKS, head_task)
    loss_tile = jnp.broadcast_to(jnp.sum(losses[1], axis=1, keepdims=True), (8, 128))
    jt[TASKS, 0:8, 0:128] = loss_tile
    jt[TASKS, 0:8, 128:256] = loss_tile

    my_mask = mask[quarter(ch), :]
    for c in range(4):
        gsend[c] = (gfeat[:, c * 128 : (c + 1) * 128] * my_mask * aall[c, 4:5, :]).astype(BF16)

    def g_copy(peer, k):
        return put(gsend.at[peer], grecv.at[ch], g_send.at[k], g_recv.at[ch], at(chan=peer))

    def q_copy(peer, k):
        rows = pl.ds(pl.multiple_of(peer * HC, HC), HC)
        return put(gh.at[:, rows, :], ghall.at[ch], q_send.at[k], q_recv.at[ch], at(chan=peer))

    def s_copy(peer, k):
        return put(jsend.at[peer], jrecv.at[ch], s_send.at[k], s_recv.at[ch], at(chan=peer))

    for k, peer in enumerate(peers):
        g_copy(peer, k).start()
    for i in range(2):
        x_relay(LAYERS, i)
    grecv[ch] = gsend[ch]
    low_lane = lax.broadcasted_iota(jnp.int32, (32, 128), 1) < HC
    for c in range(4):
        side = slice((c // 2) * 128, (c // 2) * 128 + 128)
        for m in range(4):
            one, two = jt[2 * m, :, side], jt[2 * m + 1, :, side]
            if m == 3:
                two = jnp.where(lax.broadcasted_iota(jnp.int32, (32, 128), 0) < 8, two, 0.0)
            if c % 2 == 0:
                two = pltpu.roll(two, HC, 1)
            else:
                one = pltpu.roll(one, HC, 1)
            jsend[c, m] = jnp.where(low_lane, one, two)
    for k, peer in enumerate(peers):
        s_copy(peer, k).start()
        q_copy(peer, k).start()
    ghall[ch] = gh[:, pl.ds(pl.multiple_of(ch * HC, HC), HC), :]
    jrecv[ch] = jsend[ch]

    def spread(l, i, grad):
        columns = (
            jnp.where(col_id < W - 1, pltpu.roll(grad, IMG - 1, 0), 0.0),
            grad,
            jnp.where(col_id >= 1, pltpu.roll(grad, 1, 0), 0.0),
        )
        top = pl.multiple_of(i * IMG, IMG)
        blank = jnp.zeros((W, 128), BF16)
        for e in range(3):
            low = columns[e].astype(BF16)
            gs[l * 9 + e, pl.ds(top, IMG - W), :] = low[W:]
            gs[l * 9 + e, pl.ds(top + IMG - W, W), :] = blank
            gs[l * 9 + 3 + e, pl.ds(top, IMG), :] = low
            gs[l * 9 + 6 + e, pl.ds(top + W, IMG - W), :] = low[: IMG - W]
            gs[l * 9 + 6 + e, pl.ds(top, W), :] = blank

    def conv_backward(l, i):
        rows = pl.ds(pl.multiple_of(i * IMG, IMG), IMG)
        lefts = []
        for first in range(0, 9, 2):
            taps = [t for t in (first, first + 1) if t < 9]
            sides = [gs[l * 9 + t, rows, :] for t in taps]
            lefts.append(jnp.concatenate(sides, axis=1) if len(sides) > 1 else sides[0])
        for h in range(2):
            total = None
            for first in range(0, 9, 2):
                taps = [t for t in (first, first + 1) if t < 9]
                sides = [wall[slots_ref[(l * 9 + t) * 2 + h]] for t in taps]
                side = jnp.concatenate(sides, axis=1) if len(sides) > 1 else sides[0]
                term = dot(lefts[first // 2], side, NT)
                total = term if total is None else total + term
            bpart[l - 1, i, h, 0] = total[:, :128]
            bpart[l - 1, i, h, 1] = total[:, 128:]

    def bc_copy(l, i):
        return put(
            bpart.at[l - 1, i, :, 1 - core],
            bcore.at[l - 1, i],
            bc_send.at[l - 1, i],
            bc_recv.at[l - 1, i],
            at(chan=partner),
        )

    def bx_copy(l, i):
        return put(bxs.at[l - 1, i], bx.at[l - 1, i], bx_send.at[l - 1, i], bx_recv.at[l - 1, i], at(chan=across))

    def weight_grads(l):
        def half(h):
            lhs = xt[l, h]

            def pair(p):
                t = 2 * p
                rhs = jnp.concatenate([gs[l * 9 + t], gs[l * 9 + t + 1]], axis=1)
                out = dot(lhs, rhs, NN)
                dw[(l * 9 + t) * 2 + h] = out[:, :128]
                dw[(l * 9 + t + 1) * 2 + h] = out[:, 128:]

            loop(4, pair)
            dw[(l * 9 + 8) * 2 + h] = dot(lhs, gs[l * 9 + 8], NN)

        loop(2, half)

    for peer in peers:
        came(grecv.at[peer], g_recv.at[peer])

    def top_grad(i):
        rows = pl.ds(pl.multiple_of(i * IMG, IMG), IMG)
        grad = jnp.concatenate([grecv[2 * i], grecv[2 * i + 1]], axis=0).astype(F32)
        spread(LAYERS - 1, i, grad * coef[LAYERS - 1, rows, :])

    loop(2, top_grad)
    x_side = ch // 2
    for l in (2, 1):

        def partial_image(i, l=l):
            conv_backward(l, i)
            bc_copy(l, i).start()

        loop(2, partial_image)

        def chip_sum(i, l=l):
            bc_copy(l, i).wait_recv()
            bxs[l - 1, i] = bpart[l - 1, i, 1 - x_side, core] + bcore[l - 1, i, 1 - x_side]
            bx_copy(l, i).start()

        loop(2, chip_sum)
        weight_grads(l)

        def finish_image(i, l=l):
            bx_copy(l, i).wait_recv()
            grad = bpart[l - 1, i, x_side, core] + bcore[l - 1, i, x_side] + bx[l - 1, i]
            rows = pl.ds(pl.multiple_of(i * IMG, IMG), IMG)
            spread(l - 1, i, grad * coef[l - 1, rows, :])

        loop(2, finish_image)
    weight_grads(0)

    for i in range(2):
        x_arrive(LAYERS, i)
    for peer in peers:
        came(ghall.at[peer], q_recv.at[peer])
        came(jrecv.at[peer], s_recv.at[peer])
    lhs = [
        jnp.concatenate([ghall[2 * m].reshape(TASKS * HC, 128), ghall[2 * m + 1].reshape(TASKS * HC, 128)], axis=1)
        for m in range(2)
    ]
    for c in range(0, 4, 2):
        total = None
        for m in range(2):
            rows = slice(m * IMG, (m + 1) * IMG)
            rhs = jnp.concatenate([xs[LAYERS, c, rows, :], xs[LAYERS, c + 1, rows, :]], axis=1)
            term = dot(lhs[m], rhs, NN)
            total = term if total is None else total + term
        hg[c * 448 : (c + 1) * 448, :] = total[:, :128]
        hg[(c + 1) * 448 : (c + 2) * 448, :] = total[:, 128:]
    if hg.shape[0] > 1792:
        hg[1792:, :] = jnp.zeros((hg.shape[0] - 1792, 128), F32)
    small[...] = jnp.zeros_like(small)
    for m in range(4):
        small[m * 32 : (m + 1) * 32, :] = jrecv[0, m] + jrecv[1, m] + jrecv[2, m] + jrecv[3, m]
    losses[2 + me] = small[96:104, :]

    def l_copy(i):
        dev = (me + i + 1) % n
        return put(losses.at[2 + me], losses.at[2 + me], l_send.at[i], l_recv.at[me], at(dp=dev))

    def part(dest, k):
        u = inv_ref[dest * slots_per + k]
        return dw[jnp.maximum(u, 0)] * jnp.where(u >= 0, 1.0, 0.0)

    def head_part(dest):
        rows = hg[pl.ds(pl.multiple_of(dest * piece, 16), piece), :]
        return rows, small[pl.ds(pl.multiple_of(dest * SMALL, SMALL), SMALL), :]

    def write(ref, values):
        codes, powers = encode(values)
        ref[0:256, :] = codes
        ref[256:272, :] = powers

    def read(ref):
        return decode(ref[0:256, :], ref[256:272, :])

    def write_head(ref, values):
        codes, powers = encode(values[0])
        ref[0:piece, :] = codes
        ref[piece : piece + 16, :] = powers
        codes, powers = encode(values[1])
        ref[piece + 16 : piece + 32, :] = codes
        ref[piece + 32 : piece + 48, :] = powers

    def read_head(ref):
        one = decode(ref[0:piece, :], ref[piece : piece + 16, :])
        return one, decode(ref[piece + 16 : piece + 32, :], ref[piece + 32 : piece + 48, :])

    def y_copy(zz, k):
        return put(ysend.at[zz, k], yrecv.at[zz, k], y_send.at[zz, k], y_recv.at[zz, k], other)

    def z_right(zz, k):
        return put(lsend.at[zz, k], lleft.at[zz, k], z_send.at[zz, k], zl_recv.at[zz, k], right)

    def z_left(zz, k):
        return put(lsend.at[zz, k], lright.at[zz, k], z_send.at[zz, k], zr_recv.at[zz, k], left)

    def cross(zz):
        dest = zz * 2 + 1 - y

        def block(k):
            write(ysend.at[zz, k], part(dest, k))
            y_copy(zz, k).start()

        loop(first_a, block)
        write_head(ysend.at[zz, first_a], head_part(dest))
        y_copy(zz, first_a).start()

    def pass_on(zz, k):
        @pl.when(zz > z)
        def _():
            z_right(zz, k).start()

        @pl.when(zz < z)
        def _():
            z_left(zz, k).start()

    def line_conv(zz, k):
        is_a, is_own = k < first_a, k < slots_per
        dest = zz * 2 + jnp.where(is_own, y, 1 - y)
        slot = jnp.where(is_own, k, k - last_b)
        zsum[...] = part(dest, slot)

        @pl.when(is_a)
        def _():
            came(yrecv.at[zz, k], y_recv.at[zz, k])
            zsum[...] += read(yrecv.at[zz, k])

        @pl.when((zz >= z) & has_left)
        def _():
            came(lleft.at[zz, k], zl_recv.at[zz, k])
            zsum[...] += read(lleft.at[zz, k])

        @pl.when((zz <= z) & has_right)
        def _():
            came(lright.at[zz, k], zr_recv.at[zz, k])
            zsum[...] += read(lright.at[zz, k])

    def line_head(zz):
        k = cargo - 1
        dest = zz * 2 + y
        rows, few = head_part(dest)
        zsum[0:piece, :] = rows
        zsum[piece : piece + SMALL, :] = few
        came(yrecv.at[zz, first_a], y_recv.at[zz, first_a])

        def add(ref):
            one, two = read_head(ref)
            zsum[0:piece, :] += one
            zsum[piece : piece + SMALL, :] += two

        add(yrecv.at[zz, first_a])

        @pl.when((zz >= z) & has_left)
        def _():
            came(lleft.at[zz, k], zl_recv.at[zz, k])
            add(lleft.at[zz, k])

        @pl.when((zz <= z) & has_right)
        def _():
            came(lright.at[zz, k], zr_recv.at[zz, k])
            add(lright.at[zz, k])

    def head_values():
        return zsum[0:piece, :], zsum[piece : piece + SMALL, :]

    def out_step(d):
        for zz, ok in ((z - d, z - d >= 0), (z + d, z + d < nz)):

            @pl.when(ok)
            def _(zz=zz):
                cross(zz)

        for zz, ok in ((z - d, z - d >= 0), (z + d, z + d < nz)):

            @pl.when(ok)
            def _(zz=zz):
                def block(k):
                    line_conv(zz, k)
                    write(lsend.at[zz, k], zsum[...])
                    pass_on(zz, k)

                loop(cargo - 1, block)
                line_head(zz)
                write_head(lsend.at[zz, cargo - 1], head_values())
                pass_on(zz, cargo - 1)

    loop(nz - 1, lambda i: out_step(nz - 1 - i))
    loop(n - 1, lambda i: l_copy(i).start())
    cross(z)

    def b_copy(k):
        return put(bsend2.at[k], brecv2.at[k], b_send.at[k], b_recv.at[k], other)

    def give_b(k):
        line_conv(z, slots_per + k)
        write(bsend2.at[k], zsum[...])
        b_copy(k).start()

    loop(last_b, give_b)

    line_head(z)
    write_head(hag.at[me], head_values())

    def tag(j):
        return hag.at[j]

    def t_right(j):
        return put(tag(j), tag(j), t_zr.at[j], t_recv.at[j], right)

    def t_left(j):
        return put(tag(j), tag(j), t_zl.at[j], t_recv.at[j], left)

    def t_other(j):
        return put(tag(j), tag(j), t_y.at[j], t_recv.at[j], other)

    @pl.when(has_right)
    def _():
        t_right(me).start()

    @pl.when(has_left)
    def _():
        t_left(me).start()

    t_other(me).start()

    def own_slot(k):
        line_conv(z, k)
        grad_out[k] = zsum[...]

    loop(first_a, own_slot)

    def tail(d):
        @pl.when(z - d - 1 >= 0)
        def _():
            j = (z - d - 1) * 2 + y
            came(tag(j), t_recv.at[j])

            @pl.when(has_right)
            def _():
                t_right(j).start()

            t_other(j).start()

        @pl.when(z + d + 1 < nz)
        def _():
            j = (z + d + 1) * 2 + y
            came(tag(j), t_recv.at[j])

            @pl.when(has_left)
            def _():
                t_left(j).start()

            t_other(j).start()

    loop(nz - 1, tail)

    def own_last(k):
        line_conv(z, first_a + k)
        came(brecv2.at[k], b_recv.at[k])
        grad_out[first_a + k] = zsum[...] + read(brecv2.at[k])

    loop(last_b, own_last)

    loop(n - 1, lambda i: came(losses.at[2 + (me + i + 1) % n], l_recv.at[(me + i + 1) % n]))
    loss_out[...] = lax.fori_loop(0, n, lambda i, acc: acc + losses[2 + i], jnp.zeros((8, 128), F32))

    def other_row(zz):
        j = zz * 2 + 1 - y
        came(tag(j), t_recv.at[j])

    loop(nz, other_row)
    per = 448 // piece

    def unpack(j):
        one, two = read_head(hag.at[j])

        @pl.when(j < 4 * per)
        def _():
            rows = pl.ds(pl.multiple_of((j % per) * piece, 16), piece)
            head_out[rows, pl.ds(pl.multiple_of((j // per) * 128, 128), 128)] = one

        @pl.when(j < 8)
        def _():
            small_out[pl.ds(pl.multiple_of(j * SMALL, SMALL), SMALL), :] = two

    loop(n, unpack)

    def drain_w(s):
        k = s % slots_per
        zz, row = s // (2 * slots_per), (s // slots_per) % 2
        on_line = (row == y) | (k >= first_a)

        @pl.when(on_line & has_right & (zz <= z))
        def _():
            left_it(wall.at[s], w_zr.at[s])

        @pl.when(on_line & has_left & (zz >= z))
        def _():
            left_it(wall.at[s], w_zl.at[s])

        @pl.when((row == y) & ((k < first_a) | (zz == z)))
        def _():
            left_it(wall.at[s], w_y.at[s])

    loop(n * slots_per, drain_w)

    def drain_t(zz):
        j = zz * 2 + y

        @pl.when(has_right & (zz <= z))
        def _():
            left_it(tag(j), t_zr.at[j])

        @pl.when(has_left & (zz >= z))
        def _():
            left_it(tag(j), t_zl.at[j])

        left_it(tag(j), t_y.at[j])

        def y_block(k):
            y_copy(zz, k).wait_send()

        loop(first_a + 1, y_block)

        @pl.when(zz != z)
        def _():
            loop(cargo, lambda k: left_it(lsend.at[zz, k], z_send.at[zz, k]))

    loop(nz, drain_t)
    loop(last_b, lambda k: b_copy(k).wait_send())
    for l in range(LAYERS + 1):
        for i in range(2):
            x_drain(l, i)
    for k in range(3):
        loop(TASKS, lambda t, k=k: h_copy(t, ch, partner, k).wait_send())
        j_copy(ch, partner, k).wait_send()
        a_copy(ch, partner, k).wait_send()
    for k, peer in enumerate(peers):
        f_copy(peer, k).wait_send()
        g_copy(peer, k).wait_send()
        q_copy(peer, k).wait_send()
        s_copy(peer, k).wait_send()
    for l in (1, 2):
        for i in range(2):
            bc_copy(l, i).wait_send()
            bx_copy(l, i).wait_send()
    loop(n - 1, lambda i: c_copy(i).wait_send())
    loop(n - 1, lambda i: l_copy(i).wait_send())


def adamw(weight, gradient, moment_one, moment_two, step_rate, step_count):
    step_float = step_count[0].astype(F32)
    moment_one = beta_one * moment_one + (1.0 - beta_one) * gradient
    moment_two = beta_two * moment_two + (1.0 - beta_two) * gradient * gradient
    first_hat = moment_one / (1.0 - beta_one**step_float)
    second_hat = moment_two / (1.0 - beta_two**step_float)
    weight = weight - step_rate * (
        first_hat / (jnp.sqrt(second_hat) + eps_adam) + decay_rate * weight
    )
    return (weight, moment_one, moment_two)


def per_device(
    n,
    inputs,
    affine,
    image_sizes,
    labels,
    label_mask,
    unit_slots,
    conv_master,
    conv_first,
    conv_second,
    head_master,
    head_first,
    head_second,
    join_master,
    join_first,
    join_second,
    scale_master,
    scale_first,
    scale_second,
    step_count,
):
    slots_per = conv_master.shape[0]
    nz = n // 2
    last_b = slots_per // 7
    first_a = slots_per - last_b
    cargo = slots_per + last_b + 1
    piece = -(-1792 // (n * 16)) * 16
    code = jnp.where(label_mask > 0, labels, -1).reshape(4, 128, TASKS).transpose(0, 2, 1)
    code = jnp.pad(code, ((0, 0), (0, 8 - TASKS), (0, 0)), constant_values=-1)
    join_pad = jnp.concatenate(
        [
            join_master,
            jnp.zeros((TASKS, HC, 32 - K), F32),
            scale_master[:, :, None],
            jnp.zeros((TASKS, HC, 128 - 33), F32),
        ],
        axis=2,
    )
    affine_pad = jnp.pad(affine.reshape(2 * LAYERS, 128), ((0, 2), (0, 0)))
    vm, sm, dma = pltpu.VMEM, pltpu.SMEM, pltpu.SemaphoreType.DMA
    shape = jax.ShapeDtypeStruct
    scratch = [
        vm((n * slots_per, 256, 128), BF16),
        vm((LAYERS + 1, 4, PX, 128), BF16),
        vm((LAYERS, 2, 256, PX), BF16),
        vm((TASKS, 4, HC, C), BF16),
        vm((TASKS, 4, HC, 128), F32),
        vm((4, 8, 128), F32),
        vm((n, 8, 128), F32),
        vm((n + 2, 8, 128), F32),
        sm((n * slots_per,), jnp.int32),
        vm((PX, 128), F32),
        vm((LAYERS, PX, 128), F32),
        vm((3, IMG, 128), F32),
        vm((4, 128, 128), BF16),
        vm((TASKS, 256, 128), BF16),
        vm((4, TASKS, HC, 128), BF16),
        vm((128, C), F32),
        vm((4, 128, 128), BF16),
        vm((4, 128, 128), BF16),
        vm((8, 32, 256), F32),
        vm((4, 4, 32, 128), F32),
        vm((4, 4, 32, 128), F32),
        vm((27, PX, 128), BF16),
        vm((2, 2, 2, 2, IMG, 128), F32),
        vm((2, 2, 2, IMG, 128), F32),
        vm((2, 2, IMG, 128), F32),
        vm((2, 2, IMG, 128), F32),
        vm((54, 256, 128), F32),
        vm((n * piece, 128), F32),
        vm((n * SMALL, 128), F32),
        vm((nz, first_a + 1, CHUNK, 128), jnp.int16),
        vm((nz, first_a + 1, CHUNK, 128), jnp.int16),
        vm((nz, cargo, CHUNK, 128), jnp.int16),
        vm((nz, cargo, CHUNK, 128), jnp.int16),
        vm((nz, cargo, CHUNK, 128), jnp.int16),
        vm((max(last_b, 1), CHUNK, 128), jnp.int16),
        vm((max(last_b, 1), CHUNK, 128), jnp.int16),
        vm((n, CHUNK, 128), jnp.int16),
        vm((256, 128), F32),
        *[dma((n * slots_per,)) for _ in range(4)],
        *[dma((LAYERS + 1, 2, 3)) for _ in range(2)],
        *[dma((TASKS, 3)) for _ in range(2)],
        *[dma((3,)) for _ in range(4)],
        *[dma((n,)) for _ in range(4)],
        dma((3,)), dma((4,)),
        dma((3,)), dma((4,)),
        dma((3,)), dma((4,)),
        dma((3,)), dma((4,)),
        *[dma((2, 2)) for _ in range(4)],
        *[dma((nz, first_a + 1)) for _ in range(2)],
        *[dma((nz, cargo)) for _ in range(3)],
        *[dma((max(last_b, 1),)) for _ in range(2)],
        *[dma((n,)) for _ in range(4)],
    ]
    in_smem, in_vmem = pl.BlockSpec(memory_space=pltpu.SMEM), pl.BlockSpec(memory_space=pltpu.VMEM)
    slot_grads, head_total, small_total, loss_total = pl.pallas_call(
        functools.partial(kernel, n, slots_per),
        out_shape=(
            shape((slots_per, 256, 128), F32),
            shape((448, C), F32),
            shape((128, 128), F32),
            shape((8, 128), F32),
        ),
        in_specs=[in_smem] * 2 + [in_vmem] * 6,
        out_specs=(in_vmem,) * 4,
        scratch_shapes=scratch,
        compiler_params=pltpu.CompilerParams(
            collective_id=0, has_side_effects=True, vmem_limit_bytes=60 * 2**20
        ),
    )(
        unit_slots,
        image_sizes,
        inputs.reshape(PX, 128),
        affine_pad,
        code,
        conv_master,
        head_master,
        join_pad,
    )
    pairs = small_total.reshape(4, 32, 2, HC).transpose(0, 2, 1, 3).reshape(8, 32, HC)[:TASKS]
    join_total = pairs[:, :K].transpose(0, 2, 1)
    scale_total = pairs[:, 24]
    head_total = head_total.reshape(TASKS, HC, C)
    conv_out = adamw(conv_master, slot_grads, conv_first, conv_second, 0.01, step_count)
    head_out = adamw(head_master, head_total, head_first, head_second, 0.03, step_count)
    join_out = adamw(join_master, join_total, join_first, join_second, 0.4, step_count)
    scale_out = adamw(scale_master, scale_total, scale_first, scale_second, 0.8, step_count)
    loss = jnp.sum(loss_total[:TASKS, 64])
    return (loss.reshape(1),) + conv_out + head_out + join_out + scale_out


def solution(mesh):
    placed = (
        P("dp", None, None, "chan"),
        P(None, None, "chan"),
        P("dp", None),
        P("dp", None, None, None),
        P("dp", None, None, None),
        P(),
        P("dp", None, "chan"),
        P("dp", None, "chan"),
        P("dp", None, "chan"),
        P(None, "chan", None),
        P(None, "chan", None),
        P(None, "chan", None),
        P(None, "chan", None),
        P(None, "chan", None),
        P(None, "chan", None),
        P(None, "chan"),
        P(None, "chan"),
        P(None, "chan"),
        P(),
    )
    return jax.shard_map(
        functools.partial(per_device, mesh.shape["dp"]),
        mesh=mesh,
        in_specs=placed,
        out_specs=(P(),) + placed[6:18],
        check_vma=False,
    )
```

time: 586 us -> 213 us (0.36); the launches traced: 577 us -> 213 us
  waiting for transfers between devices: 335 us -> 0 us
  Pallas kernels: 0 us -> 196 us
  blocking collectives: 116 us -> 0 us
  matrix products: 58.8 us -> 0 us
  local copies, waits for them, and re-layouts: 29.6 us -> 6.34 us
  between operations: 16.8 us -> 1.57 us
  other arithmetic: 20.3 us -> 9.16 us
    psum x2 -> x0, waiting for transfers between devices: 253 us -> none  [the longest x1 222 us: per_device(): summed_all = lax.psum(unit_grads, 'dp')]
    pallas_call x0 -> x1, Pallas kernels: none -> 196 us  [per_device(): pl.pallas_call(functools.partial(kernel, n, slots_per), out_shape=(shape(...]
    psum x4 -> x0, blocking collectives: 86.6 us -> none  [the longest x1 41.9 us: per_device(): lax.psum((head_grad, join_grad, scale_grad, loss_local), 'dp')]
    dot_general x79 -> x0, matrix products: 58.8 us -> none  [the longest x27 22.9 us: conv_backward(): jnp.einsum('ihwc,ihwd->cd', window, grad_linear, preferred_element_type=j...]
    reduce_scatter x3 -> x0, waiting for transfers between devices: 46.1 us -> none  [channel_sum(): lax.psum_scatter(partial_term, 'chan', scatter_dimension=3, tiled=True)]
    all_gather x1 -> x0, waiting for transfers between devices: 36.1 us -> none  [per_device(): lax.all_gather(conv_master.astype(jnp.bfloat16), 'dp', axis=0, tiled=True)]
    all_gather x4 -> x0, blocking collectives: 29 us -> none  [gather_channels(): return lax.all_gather(local_part, 'chan', axis=3, tiled=True)]
    slice x6 -> x0, local copies, waits for them, and re-layouts: 8.21 us -> none  [the longest x3 6.96 us: conv_forward(): window = padded[:, row_shift:row_shift + H, col_shift:col_shift + W, :]]
  transfers between devices with their start and end apart: 6 -> 0, of which waited for: 6 -> 0; matrix products, arithmetic and copies ran while one was open for 6% -> 0% of each run, Pallas kernels for 0% -> 0%
where the time goes in v1:
time: 213 us
  Pallas kernels  196 us (92%)
  other arithmetic  9.16 us (4%)
  local copies, waits for them, and re-layouts  6.34 us (3%)
    pallas_call x1, Pallas kernels, per_device(): pl.pallas_call(functools.partial(kernel, n, slots_per), out_shape=(shape(...  196 us
    sub x4, other arithmetic, adamw(): weight - step_rate * (first_hat / (jnp.sqrt(second_hat) + eps_adam) + dec...  6.02 us

profile of v1, /device:TPU:0, one launch (start us, length us, event | category | flops | bytes accessed | tf_op | source)
XLA Modules:
  0.0 212.8 jit_solution(17758453957396966428)
XLA Ops:
  0.6 0.7 reshape.57
  1.3 0.6 pad.8.affine_ref
  1.9 1.0 compare_select_fusion
  2.9 0.1 reshape.58
  3.0 0.0 copy-start.11
  3.1 0.6 pad.9.code_ref
  3.7 0.1 copy-done.11
  3.7 0.0 copy-start.7
  3.7 0.1 copy.44
  3.9 0.7 copy-done.7
  4.6 0.1 copy.43
  4.8 0.1 pad.13.clone
  4.9 0.1 pad.11.clone
  4.9 0.0 copy-start.3
  4.9 0.8 maximum_maximum_fusion.join_ref
  5.8 0.0 copy-start
  5.8 0.0 copy-start.2
  5.8 195.8 %shard_map.282 = (f32[7,256,128]{2,1,0:T(8,128)}, f32[448,512]{1,0:T(8,128)}, f32[128,128]{1,0:T(8,128)}, f32[8,128]{1,0:T(8,128)}) custom-call(s32[54]{0:T(128)} %slots_ref.1, s32[2,2]{1,0:T(2,128)} %sizes_ref.1, bf16[512,128]{1,0:T(8,128)(2,1)} %bitcast.35, f32[8,128]{1,0:T(8,128)} %pad.8.affine_ref, s32[4,8,128]{2,1,0:T(8,128)} %pad.9.code_ref, ...), custom_call_target="tpu_custom_call" | custom-call | tf_op jit(solution)/shard_map/pallas_call | solution.py:1061
  201.5 1.3 slice_reduce_fusion
  203.6 0.0 copy-done.3
  203.6 0.0 copy-done
  203.6 0.0 copy-done.2
  203.6 0.0 copy-start.1
  203.6 0.0 copy-start.4
  203.7 0.0 copy-start.5
  203.7 0.0 copy-start.6
  203.7 3.3 %multiply_subtract_fusion.1 = (f32[7,256,128]{2,1,0:T(8,128)}, f32[7,256,128]{2,1,0:T(8,128)}, f32[7,256,128]{2,1,0:T(8,128)}) fusion(f32[7,256,128]{2,1,0:T(8,128)S(1)} %copy-done, f32[]{:T(128)} %bitcast.5, f32[]{:T(128)} %bitcast.4, f32[7,256,128]{2,1,0:T(8,128)} %get-tuple-element.18, f32[7,256,128]{2,1,0:T(8,128)S(1)} %copy-done.2, ...), kind=kLoop, calls=%fused_computation.6 | loop fusion | flops 3440640 | bytes 6422536 | tf_op jit(solution)/shard_map/sub | solution.py:958
  207.0 0.0 copy-done.1
  207.0 0.0 copy-done.4
  207.0 0.0 copy-done.5
  207.0 0.0 copy-done.6
  207.0 0.0 copy-start.10
  207.0 2.0 multiply_subtract_fusion
  209.0 0.0 copy-done.10
  209.0 0.1 reshape.61
  209.2 0.0 copy-start.8
  209.2 0.0 copy-start.9
  209.2 0.8 copy-done.8
  210.1 0.0 copy-done.9
  210.1 0.1 multiply_subtract_fusion.2
  210.2 0.7 copy.50
  210.8 0.7 copy.51
  211.5 0.0 copy-start.12
  211.5 0.0 copy-start.13
  211.5 0.7 copy.52
  212.2 0.0 copy-done.12
  212.2 0.0 copy-done.13
  212.2 0.6 multiply_subtract_fusion.3
  (5 shorter events, 0.1 us)
Async XLA Ops:
  3.0 0.7 copy-start.11
  3.7 0.9 copy-start.7
  4.9 198.7 %copy-start.3 = (f32[7,256,128]{2,1,0:T(8,128)S(1)}, f32[7,256,128]{2,1,0:T(8,128)}, u32[]{:S(2)}) copy-start(f32[7,256,128]{2,1,0:T(8,128)} %param.26) | copy-start | bytes 2752516
  5.8 197.9 %copy-start = (f32[7,256,128]{2,1,0:T(8,128)S(1)}, f32[7,256,128]{2,1,0:T(8,128)}, u32[]{:S(2)}) copy-start(f32[7,256,128]{2,1,0:T(8,128)} %conv_ref.1) | copy-start | bytes 2752516
  5.8 197.9 %copy-start.2 = (f32[7,256,128]{2,1,0:T(8,128)S(1)}, f32[7,256,128]{2,1,0:T(8,128)}, u32[]{:S(2)}) copy-start(f32[7,256,128]{2,1,0:T(8,128)} %param.27) | copy-start | bytes 2752516
  203.6 3.3 %copy-start.1 = (f32[7,64,512]{2,1,0:T(8,128)S(1)}, f32[7,64,512]{2,1,0:T(8,128)}, u32[]{:S(2)}) copy-start(f32[7,64,512]{2,1,0:T(8,128)} %head_ref.1) | copy-start | bytes 2752516
  203.6 3.3 %copy-start.4 = (f32[7,64,512]{2,1,0:T(8,128)S(1)}, f32[7,64,512]{2,1,0:T(8,128)}, u32[]{:S(2)}) copy-start(f32[7,64,512]{2,1,0:T(8,128)} %param.30) | copy-start | bytes 2752516
  203.7 3.3 %copy-start.5 = (f32[7,64,512]{2,1,0:T(8,128)S(1)}, f32[7,64,512]{2,1,0:T(8,128)}, u32[]{:S(2)}) copy-start(f32[7,64,512]{2,1,0:T(8,128)} %param.29) | copy-start | bytes 2752516
  203.7 3.3 %copy-start.6 = (f32[448,512]{1,0:T(8,128)S(1)}, f32[448,512]{1,0:T(8,128)}, u32[]{:S(2)}) copy-start(f32[448,512]{1,0:T(8,128)} %get-tuple-element.19) | copy-start | bytes 2752516
  207.0 2.0 copy-start.10
  209.2 0.9 copy-start.8
  209.2 0.9 copy-start.9
  211.5 0.7 copy-start.12
  211.5 0.7 copy-start.13

commit v2 on v1

--- a/solution.py
+++ b/solution.py
@@ -53,6 +53,7 @@
     n,
     slots_per,
     slots_ref,
+    inv_ref,
     sizes_ref,
     inputs_ref,
     affine_ref,
@@ -72,7 +73,6 @@
     aall,
     cnt,
     losses,
-    inv_ref,
     mask,
     coef,
     zacc,
@@ -355,14 +355,6 @@
         copy(across, across, 0).wait_recv()
         copy(across, partner, 2).start()
 
-    def invert(s):
-        def look(u, found):
-            return jnp.where(slots_ref[u] == s, u, found)
-
-        inv_ref[s] = lax.fori_loop(0, slots_ref.shape[0], look, -1)
-
-    loop(n * slots_per, invert)
-
     def transpose_layer(l):
         for c in range(4):
             xt[l, c // 2, (c % 2) * 128 : (c % 2) * 128 + 128, :] = xs[l, c].T
@@ -991,6 +983,9 @@
     piece = -(-1792 // (n * 16)) * 16
     code = jnp.where(label_mask > 0, labels, -1).reshape(4, 128, TASKS).transpose(0, 2, 1)
     code = jnp.pad(code, ((0, 0), (0, 8 - TASKS), (0, 0)), constant_values=-1)
+    units = jnp.arange(unit_slots.shape[0], dtype=jnp.int32)
+    holds = unit_slots[None, :] == jnp.arange(n * slots_per, dtype=jnp.int32)[:, None]
+    slot_units = jnp.max(jnp.where(holds, units[None, :], -1), axis=1)
     join_pad = jnp.concatenate(
         [
             join_master,
@@ -1001,7 +996,7 @@
         axis=2,
     )
     affine_pad = jnp.pad(affine.reshape(2 * LAYERS, 128), ((0, 2), (0, 0)))
-    vm, sm, dma = pltpu.VMEM, pltpu.SMEM, pltpu.SemaphoreType.DMA
+    vm, dma = pltpu.VMEM, pltpu.SemaphoreType.DMA
     shape = jax.ShapeDtypeStruct
     scratch = [
         vm((n * slots_per, 256, 128), BF16),
@@ -1012,7 +1007,6 @@
         vm((4, 8, 128), F32),
         vm((n, 8, 128), F32),
         vm((n + 2, 8, 128), F32),
-        sm((n * slots_per,), jnp.int32),
         vm((PX, 128), F32),
         vm((LAYERS, PX, 128), F32),
         vm((3, IMG, 128), F32),
@@ -1066,7 +1060,7 @@
             shape((128, 128), F32),
             shape((8, 128), F32),
         ),
-        in_specs=[in_smem] * 2 + [in_vmem] * 6,
+        in_specs=[in_smem] * 3 + [in_vmem] * 6,
         out_specs=(in_vmem,) * 4,
         scratch_shapes=scratch,
         compiler_params=pltpu.CompilerParams(
@@ -1074,6 +1068,7 @@
         ),
     )(
         unit_slots,
+        slot_units,
         image_sizes,
         inputs.reshape(PX, 128),
         affine_pad,

time: 213 us -> 190 us (0.89)
  Pallas kernels: 196 us -> 172 us
    pallas_call x1, Pallas kernels: 196 us -> 172 us  [per_device(): pl.pallas_call(functools.partial(kernel, n, slots_per), out_shape=(shape(...]
where the time goes in v2:
time: 190 us
  Pallas kernels  172 us (91%)
  other arithmetic  10.5 us (6%)
  local copies, waits for them, and re-layouts  5.66 us (3%)
    pallas_call x1, Pallas kernels, per_device(): pl.pallas_call(functools.partial(kernel, n, slots_per), out_shape=(shape(...  172 us
    sub x4, other arithmetic, adamw(): weight - step_rate * (first_hat / (jnp.sqrt(second_hat) + eps_adam) + dec...  6.02 us
    unnamed x34, local copies, waits for them, and re-layouts  3.86 us

profile of v2, /device:TPU:0, one launch (start us, length us, event | category | flops | bytes accessed | tf_op | source)
XLA Modules:
  0.0 189.7 jit_solution(8949217021996134452)
XLA Ops:
  0.6 0.0 copy-start.14
  0.7 1.3 select_reduce_fusion.inv_ref
  1.9 0.0 copy-done.14
  2.0 0.6 pad.8.affine_ref
  2.6 1.0 compare_select_fusion
  3.5 0.1 reshape.59
  3.7 0.0 copy-start.11
  3.7 0.6 pad.9.code_ref
  4.3 0.1 copy-done.11
  4.4 0.0 copy-start.7
  4.4 0.1 copy.56
  4.5 0.7 copy-done.7
  5.2 0.1 copy.55
  5.4 0.1 pad.13.clone
  5.5 0.1 pad.11.clone
  5.5 0.0 copy-start.3
  5.5 0.8 maximum_maximum_fusion.join_ref
  6.4 0.0 copy-start
  6.4 0.0 copy-start.2
  6.4 172.0 %shard_map.282 = (f32[7,256,128]{2,1,0:T(8,128)}, f32[448,512]{1,0:T(8,128)}, f32[128,128]{1,0:T(8,128)}, f32[8,128]{1,0:T(8,128)}) custom-call(s32[54]{0:T(128)} %slots_ref.1, s32[56]{0:T(128)} %select_reduce_fusion.inv_ref, s32[2,2]{1,0:T(2,128)} %sizes_ref.1, bf16[512,128]{1,0:T(8,128)(2,1)} %bitcast.35, f32[8,128]{1,0:T(8,128)} %pad.8.affine_ref, ...), custom_call_target="tpu_custom_call" | custom-call | tf_op jit(solution)/shard_map/pallas_call | solution.py:1055
  178.4 1.3 slice_reduce_fusion
  180.5 0.0 copy-done.3
  180.5 0.0 copy-done
  180.5 0.0 copy-done.2
  180.5 0.0 copy-start.1
  180.5 0.0 copy-start.4
  180.6 0.0 copy-start.5
  180.6 0.0 copy-start.6
  180.6 3.3 %multiply_subtract_fusion.1 = (f32[7,256,128]{2,1,0:T(8,128)}, f32[7,256,128]{2,1,0:T(8,128)}, f32[7,256,128]{2,1,0:T(8,128)}) fusion(f32[7,256,128]{2,1,0:T(8,128)S(1)} %copy-done, f32[]{:T(128)} %bitcast.5, f32[]{:T(128)} %bitcast.4, f32[7,256,128]{2,1,0:T(8,128)} %get-tuple-element.18, f32[7,256,128]{2,1,0:T(8,128)S(1)} %copy-done.2, ...), kind=kLoop, calls=%fused_computation.6 | loop fusion | flops 3440640 | bytes 6422536 | tf_op jit(solution)/shard_map/sub | solution.py:950
  183.8 0.0 copy-done.1
  183.9 0.0 copy-done.4
  183.9 0.0 copy-done.5
  183.9 0.0 copy-done.6
  183.9 0.0 copy-start.10
  183.9 2.0 %multiply_subtract_fusion = (f32[7,64,512]{2,1,0:T(8,128)}, f32[7,64,512]{2,1,0:T(8,128)}, f32[7,64,512]{2,1,0:T(8,128)}) fusion(f32[7,64,512]{2,1,0:T(8,128)S(1)} %copy-done.1, f32[]{:T(128)} %bitcast.5, f32[]{:T(128)} %bitcast.4, f32[7,64,512]{2,1,0:T(8,128)S(1)} %bitcast.31, f32[7,64,512]{2,1,0:T(8,128)S(1)} %copy-done.4, f32[7,64,512]{2,1,0:T(8,128)S(1)} %copy-done.5), kind=kLoop, calls=%fused_computation.4 | loop fusion | flops 3440640 | bytes 6422536 | tf_op jit(solution)/shard_map/sub | solution.py:950
  185.9 0.0 copy-done.10
  185.9 0.1 reshape.62
  186.1 0.0 copy-start.8
  186.1 0.0 copy-start.9
  186.1 0.8 copy-done.8
  186.9 0.0 copy-done.9
  187.0 0.1 multiply_subtract_fusion.2
  187.1 0.7 copy.62
  187.7 0.7 copy.63
  188.4 0.7 copy.64
  189.0 0.0 copy-done.12
  189.1 0.0 copy-done.13
  189.1 0.6 multiply_subtract_fusion.3
  (8 shorter events, 0.1 us)
Async XLA Ops:
  0.6 1.3 copy-start.14
  3.7 0.7 copy-start.11
  4.4 0.9 copy-start.7
  5.5 175.0 %copy-start.3 = (f32[7,256,128]{2,1,0:T(8,128)S(1)}, f32[7,256,128]{2,1,0:T(8,128)}, u32[]{:S(2)}) copy-start(f32[7,256,128]{2,1,0:T(8,128)} %param.26) | copy-start | bytes 2752516
  6.4 174.1 %copy-start = (f32[7,256,128]{2,1,0:T(8,128)S(1)}, f32[7,256,128]{2,1,0:T(8,128)}, u32[]{:S(2)}) copy-start(f32[7,256,128]{2,1,0:T(8,128)} %conv_ref.1) | copy-start | bytes 2752516
  6.4 174.1 %copy-start.2 = (f32[7,256,128]{2,1,0:T(8,128)S(1)}, f32[7,256,128]{2,1,0:T(8,128)}, u32[]{:S(2)}) copy-start(f32[7,256,128]{2,1,0:T(8,128)} %param.27) | copy-start | bytes 2752516
  180.5 3.3 %copy-start.1 = (f32[7,64,512]{2,1,0:T(8,128)S(1)}, f32[7,64,512]{2,1,0:T(8,128)}, u32[]{:S(2)}) copy-start(f32[7,64,512]{2,1,0:T(8,128)} %head_ref.1) | copy-start | bytes 2752516
  180.5 3.3 %copy-start.4 = (f32[7,64,512]{2,1,0:T(8,128)S(1)}, f32[7,64,512]{2,1,0:T(8,128)}, u32[]{:S(2)}) copy-start(f32[7,64,512]{2,1,0:T(8,128)} %param.30) | copy-start | bytes 2752516
  180.6 3.3 %copy-start.5 = (f32[7,64,512]{2,1,0:T(8,128)S(1)}, f32[7,64,512]{2,1,0:T(8,128)}, u32[]{:S(2)}) copy-start(f32[7,64,512]{2,1,0:T(8,128)} %param.29) | copy-start | bytes 2752516
  180.6 3.3 %copy-start.6 = (f32[448,512]{1,0:T(8,128)S(1)}, f32[448,512]{1,0:T(8,128)}, u32[]{:S(2)}) copy-start(f32[448,512]{1,0:T(8,128)} %get-tuple-element.19) | copy-start | bytes 2752516
  183.9 2.0 %copy-start.10 = (f32[128,128]{1,0:T(8,128)S(1)}, f32[128,128]{1,0:T(8,128)}, u32[]{:S(2)}) copy-start(f32[128,128]{1,0:T(8,128)} %get-tuple-element.20) | copy-start | bytes 196612
  186.1 0.9 copy-start.8
  186.1 0.9 copy-start.9
  188.4 0.7 copy-start.12
  188.4 0.7 copy-start.13

commit v3 on v2

--- a/solution.py
+++ b/solution.py
@@ -93,6 +93,8 @@
     dw,
     hg,
     small,
+    psend,
+    precv,
     ysend,
     yrecv,
     lsend,
@@ -124,6 +126,8 @@
     g_recv,
     q_send,
     q_recv,
+    p_send,
+    p_recv,
     s_send,
     s_recv,
     bc_send,
@@ -145,7 +149,7 @@
     nz = n // 2
     last_b = slots_per // 7
     first_a = slots_per - last_b
-    cargo = slots_per + last_b + 1
+    cargo = slots_per + last_b
     piece = hg.shape[0] // n
 
     me = lax.axis_index("dp")
@@ -454,6 +458,10 @@
     gfeat[...] = jnp.zeros_like(gfeat)
     klass = lax.broadcasted_iota(jnp.int32, (32, 128), 0)
 
+    def q_copy(t, peer, k):
+        rows = pl.ds(pl.multiple_of(peer * HC, HC), HC)
+        return put(gh.at[t, rows, :], ghall.at[ch, t], q_send.at[t, k], q_recv.at[t, ch], at(chan=peer))
+
     def head_task(t):
         low = hall[t].reshape(4 * HC, C)
         both = jall[t].reshape(4 * HC, 128)
@@ -480,6 +488,8 @@
         along = jnp.sum(normed * grad_normed, axis=0, keepdims=True)
         grad_hidden = ((grad_normed - normed * along) * inverse).astype(BF16)
         gh[t] = grad_hidden
+        for k, peer in enumerate(peers):
+            q_copy(t, peer, k).start()
         gfeat[...] += dot(grad_hidden, low, TN)
 
     loop(TASKS, head_task)
@@ -493,10 +503,6 @@
 
     def g_copy(peer, k):
         return put(gsend.at[peer], grecv.at[ch], g_send.at[k], g_recv.at[ch], at(chan=peer))
-
-    def q_copy(peer, k):
-        rows = pl.ds(pl.multiple_of(peer * HC, HC), HC)
-        return put(gh.at[:, rows, :], ghall.at[ch], q_send.at[k], q_recv.at[ch], at(chan=peer))
 
     def s_copy(peer, k):
         return put(jsend.at[peer], jrecv.at[ch], s_send.at[k], s_recv.at[ch], at(chan=peer))
@@ -520,7 +526,6 @@
             jsend[c, m] = jnp.where(low_lane, one, two)
     for k, peer in enumerate(peers):
         s_copy(peer, k).start()
-        q_copy(peer, k).start()
     ghall[ch] = gh[:, pl.ds(pl.multiple_of(ch * HC, HC), HC), :]
     jrecv[ch] = jsend[ch]
 
@@ -586,73 +591,9 @@
 
         loop(2, half)
 
-    for peer in peers:
-        came(grecv.at[peer], g_recv.at[peer])
-
-    def top_grad(i):
-        rows = pl.ds(pl.multiple_of(i * IMG, IMG), IMG)
-        grad = jnp.concatenate([grecv[2 * i], grecv[2 * i + 1]], axis=0).astype(F32)
-        spread(LAYERS - 1, i, grad * coef[LAYERS - 1, rows, :])
-
-    loop(2, top_grad)
-    x_side = ch // 2
-    for l in (2, 1):
-
-        def partial_image(i, l=l):
-            conv_backward(l, i)
-            bc_copy(l, i).start()
-
-        loop(2, partial_image)
-
-        def chip_sum(i, l=l):
-            bc_copy(l, i).wait_recv()
-            bxs[l - 1, i] = bpart[l - 1, i, 1 - x_side, core] + bcore[l - 1, i, 1 - x_side]
-            bx_copy(l, i).start()
-
-        loop(2, chip_sum)
-        weight_grads(l)
-
-        def finish_image(i, l=l):
-            bx_copy(l, i).wait_recv()
-            grad = bpart[l - 1, i, x_side, core] + bcore[l - 1, i, x_side] + bx[l - 1, i]
-            rows = pl.ds(pl.multiple_of(i * IMG, IMG), IMG)
-            spread(l - 1, i, grad * coef[l - 1, rows, :])
-
-        loop(2, finish_image)
-    weight_grads(0)
-
-    for i in range(2):
-        x_arrive(LAYERS, i)
-    for peer in peers:
-        came(ghall.at[peer], q_recv.at[peer])
-        came(jrecv.at[peer], s_recv.at[peer])
-    lhs = [
-        jnp.concatenate([ghall[2 * m].reshape(TASKS * HC, 128), ghall[2 * m + 1].reshape(TASKS * HC, 128)], axis=1)
-        for m in range(2)
-    ]
-    for c in range(0, 4, 2):
-        total = None
-        for m in range(2):
-            rows = slice(m * IMG, (m + 1) * IMG)
-            rhs = jnp.concatenate([xs[LAYERS, c, rows, :], xs[LAYERS, c + 1, rows, :]], axis=1)
-            term = dot(lhs[m], rhs, NN)
-            total = term if total is None else total + term
-        hg[c * 448 : (c + 1) * 448, :] = total[:, :128]
-        hg[(c + 1) * 448 : (c + 2) * 448, :] = total[:, 128:]
-    if hg.shape[0] > 1792:
-        hg[1792:, :] = jnp.zeros((hg.shape[0] - 1792, 128), F32)
-    small[...] = jnp.zeros_like(small)
-    for m in range(4):
-        small[m * 32 : (m + 1) * 32, :] = jrecv[0, m] + jrecv[1, m] + jrecv[2, m] + jrecv[3, m]
-    losses[2 + me] = small[96:104, :]
-
     def l_copy(i):
         dev = (me + i + 1) % n
         return put(losses.at[2 + me], losses.at[2 + me], l_send.at[i], l_recv.at[me], at(dp=dev))
-
-    def part(dest, k):
-        u = inv_ref[dest * slots_per + k]
-        return dw[jnp.maximum(u, 0)] * jnp.where(u >= 0, 1.0, 0.0)
 
     def head_part(dest):
         rows = hg[pl.ds(pl.multiple_of(dest * piece, 16), piece), :]
@@ -678,6 +619,86 @@
         one = decode(ref[0:piece, :], ref[piece : piece + 16, :])
         return one, decode(ref[piece + 16 : piece + 32, :], ref[piece + 32 : piece + 48, :])
 
+    def p_copy(i):
+        dest = (me + i + 1) % n
+        return put(psend.at[dest], precv.at[me], p_send.at[i], p_recv.at[me], at(dp=dest))
+
+    def head_grads():
+        for i in range(2):
+            x_arrive(LAYERS, i)
+        for peer in peers:
+            loop(TASKS, lambda t, peer=peer: came(ghall.at[peer, t], q_recv.at[t, peer]))
+            came(jrecv.at[peer], s_recv.at[peer])
+        lhs = [
+            jnp.concatenate([ghall[2 * m].reshape(TASKS * HC, 128), ghall[2 * m + 1].reshape(TASKS * HC, 128)], axis=1)
+            for m in range(2)
+        ]
+        for c in range(0, 4, 2):
+            total = None
+            for m in range(2):
+                rows = slice(m * IMG, (m + 1) * IMG)
+                rhs = jnp.concatenate([xs[LAYERS, c, rows, :], xs[LAYERS, c + 1, rows, :]], axis=1)
+                term = dot(lhs[m], rhs, NN)
+                total = term if total is None else total + term
+            hg[c * 448 : (c + 1) * 448, :] = total[:, :128]
+            hg[(c + 1) * 448 : (c + 2) * 448, :] = total[:, 128:]
+        if hg.shape[0] > 1792:
+            hg[1792:, :] = jnp.zeros((hg.shape[0] - 1792, 128), F32)
+        small[...] = jnp.zeros_like(small)
+        for m in range(4):
+            small[m * 32 : (m + 1) * 32, :] = jrecv[0, m] + jrecv[1, m] + jrecv[2, m] + jrecv[3, m]
+        losses[2 + me] = small[96:104, :]
+
+
+        def give(i):
+            dest = (me + i + 1) % n
+            write_head(psend.at[dest], head_part(dest))
+            p_copy(i).start()
+
+        loop(n - 1, give)
+        loop(n - 1, lambda i: l_copy(i).start())
+
+    for peer in peers:
+        came(grecv.at[peer], g_recv.at[peer])
+
+    def top_grad(i):
+        rows = pl.ds(pl.multiple_of(i * IMG, IMG), IMG)
+        grad = jnp.concatenate([grecv[2 * i], grecv[2 * i + 1]], axis=0).astype(F32)
+        spread(LAYERS - 1, i, grad * coef[LAYERS - 1, rows, :])
+
+    loop(2, top_grad)
+    x_side = ch // 2
+    for l in (2, 1):
+
+        def partial_image(i, l=l):
+            conv_backward(l, i)
+            bc_copy(l, i).start()
+
+        loop(2, partial_image)
+
+        def chip_sum(i, l=l):
+            bc_copy(l, i).wait_recv()
+            bxs[l - 1, i] = (bpart[l - 1, i, 1 - x_side, core] + bcore[l - 1, i, 1 - x_side]).astype(BF16)
+            bx_copy(l, i).start()
+
+        loop(2, chip_sum)
+        if l == LAYERS - 1:
+            head_grads()
+        weight_grads(l)
+
+        def finish_image(i, l=l):
+            bx_copy(l, i).wait_recv()
+            grad = bpart[l - 1, i, x_side, core] + bcore[l - 1, i, x_side] + bx[l - 1, i].astype(F32)
+            rows = pl.ds(pl.multiple_of(i * IMG, IMG), IMG)
+            spread(l - 1, i, grad * coef[l - 1, rows, :])
+
+        loop(2, finish_image)
+    weight_grads(0)
+
+    def part(dest, k):
+        u = inv_ref[dest * slots_per + k]
+        return dw[jnp.maximum(u, 0)] * jnp.where(u >= 0, 1.0, 0.0)
+
     def y_copy(zz, k):
         return put(ysend.at[zz, k], yrecv.at[zz, k], y_send.at[zz, k], y_recv.at[zz, k], other)
 
@@ -686,6 +707,13 @@
 
     def z_left(zz, k):
         return put(lsend.at[zz, k], lright.at[zz, k], z_send.at[zz, k], zr_recv.at[zz, k], left)
+
+    def both_sides(d, body):
+        for zz, ok in ((z - d, z - d >= 0), (z + d, z + d < nz)):
+
+            @pl.when(ok)
+            def _(zz=zz):
+                body(zz)
 
     def cross(zz):
         dest = zz * 2 + 1 - y
@@ -695,8 +723,6 @@
             y_copy(zz, k).start()
 
         loop(first_a, block)
-        write_head(ysend.at[zz, first_a], head_part(dest))
-        y_copy(zz, first_a).start()
 
     def pass_on(zz, k):
         @pl.when(zz > z)
@@ -728,58 +754,85 @@
             came(lright.at[zz, k], zr_recv.at[zz, k])
             zsum[...] += read(lright.at[zz, k])
 
-    def line_head(zz):
-        k = cargo - 1
-        dest = zz * 2 + y
-        rows, few = head_part(dest)
-        zsum[0:piece, :] = rows
-        zsum[piece : piece + SMALL, :] = few
-        came(yrecv.at[zz, first_a], y_recv.at[zz, first_a])
-
-        def add(ref):
-            one, two = read_head(ref)
-            zsum[0:piece, :] += one
-            zsum[piece : piece + SMALL, :] += two
-
-        add(yrecv.at[zz, first_a])
-
-        @pl.when((zz >= z) & has_left)
-        def _():
-            came(lleft.at[zz, k], zl_recv.at[zz, k])
-            add(lleft.at[zz, k])
-
-        @pl.when((zz <= z) & has_right)
-        def _():
-            came(lright.at[zz, k], zr_recv.at[zz, k])
-            add(lright.at[zz, k])
-
-    def head_values():
-        return zsum[0:piece, :], zsum[piece : piece + SMALL, :]
-
-    def out_step(d):
-        for zz, ok in ((z - d, z - d >= 0), (z + d, z + d < nz)):
-
-            @pl.when(ok)
-            def _(zz=zz):
-                cross(zz)
-
-        for zz, ok in ((z - d, z - d >= 0), (z + d, z + d < nz)):
-
-            @pl.when(ok)
-            def _(zz=zz):
-                def block(k):
-                    line_conv(zz, k)
-                    write(lsend.at[zz, k], zsum[...])
-                    pass_on(zz, k)
-
-                loop(cargo - 1, block)
-                line_head(zz)
-                write_head(lsend.at[zz, cargo - 1], head_values())
-                pass_on(zz, cargo - 1)
-
-    loop(nz - 1, lambda i: out_step(nz - 1 - i))
-    loop(n - 1, lambda i: l_copy(i).start())
+    loop(nz - 1, lambda i: both_sides(nz - 1 - i, cross))
     cross(z)
+
+    def tag(j):
+        return hag.at[j]
+
+    def t_right(j):
+        return put(tag(j), tag(j), t_zr.at[j], t_recv.at[j], right)
+
+    def t_left(j):
+        return put(tag(j), tag(j), t_zl.at[j], t_recv.at[j], left)
+
+    def t_other(j):
+        return put(tag(j), tag(j), t_y.at[j], t_recv.at[j], other)
+
+    rows, few = head_part(me)
+    zsum[0:piece, :] = rows
+    zsum[piece : piece + SMALL, :] = few
+
+    def add_piece(i):
+        source = (me + i + 1) % n
+        came(precv.at[source], p_recv.at[source])
+        one, two = read_head(precv.at[source])
+        zsum[0:piece, :] += one
+        zsum[piece : piece + SMALL, :] += two
+
+    loop(n - 1, add_piece)
+    write_head(hag.at[me], (zsum[0:piece, :], zsum[piece : piece + SMALL, :]))
+
+    @pl.when(has_right)
+    def _():
+        t_right(me).start()
+
+    @pl.when(has_left)
+    def _():
+        t_left(me).start()
+
+    t_other(me).start()
+
+    def tail(d):
+        @pl.when(z - d >= 0)
+        def _():
+            j = (z - d) * 2 + y
+            came(tag(j), t_recv.at[j])
+
+            @pl.when(has_right)
+            def _():
+                t_right(j).start()
+
+            t_other(j).start()
+
+        @pl.when(z + d < nz)
+        def _():
+            j = (z + d) * 2 + y
+            came(tag(j), t_recv.at[j])
+
+            @pl.when(has_left)
+            def _():
+                t_left(j).start()
+
+            t_other(j).start()
+
+    def out_step(i):
+        d = nz - 1 - i
+
+        def item(c):
+            k = (c + first_a) % cargo
+
+            def send(zz):
+                line_conv(zz, k)
+                write(lsend.at[zz, k], zsum[...])
+                pass_on(zz, k)
+
+            both_sides(d, send)
+
+        loop(cargo, item)
+        tail(i + 1)
+
+    loop(nz - 1, out_step)
 
     def b_copy(k):
         return put(bsend2.at[k], brecv2.at[k], b_send.at[k], b_recv.at[k], other)
@@ -791,61 +844,35 @@
 
     loop(last_b, give_b)
 
-    line_head(z)
-    write_head(hag.at[me], head_values())
-
-    def tag(j):
-        return hag.at[j]
-
-    def t_right(j):
-        return put(tag(j), tag(j), t_zr.at[j], t_recv.at[j], right)
-
-    def t_left(j):
-        return put(tag(j), tag(j), t_zl.at[j], t_recv.at[j], left)
-
-    def t_other(j):
-        return put(tag(j), tag(j), t_y.at[j], t_recv.at[j], other)
-
-    @pl.when(has_right)
-    def _():
-        t_right(me).start()
-
-    @pl.when(has_left)
-    def _():
-        t_left(me).start()
-
-    t_other(me).start()
-
     def own_slot(k):
         line_conv(z, k)
         grad_out[k] = zsum[...]
 
     loop(first_a, own_slot)
 
-    def tail(d):
-        @pl.when(z - d - 1 >= 0)
-        def _():
-            j = (z - d - 1) * 2 + y
-            came(tag(j), t_recv.at[j])
-
-            @pl.when(has_right)
-            def _():
-                t_right(j).start()
-
-            t_other(j).start()
-
-        @pl.when(z + d + 1 < nz)
-        def _():
-            j = (z + d + 1) * 2 + y
-            came(tag(j), t_recv.at[j])
-
-            @pl.when(has_left)
-            def _():
-                t_left(j).start()
-
-            t_other(j).start()
-
-    loop(nz - 1, tail)
+    loop(n - 1, lambda i: came(losses.at[2 + (me + i + 1) % n], l_recv.at[(me + i + 1) % n]))
+    loss_out[...] = lax.fori_loop(0, n, lambda i, acc: acc + losses[2 + i], jnp.zeros((8, 128), F32))
+
+    def other_row(zz):
+        j = zz * 2 + 1 - y
+        came(tag(j), t_recv.at[j])
+
+    loop(nz, other_row)
+    per = 448 // piece
+
+    def unpack(j):
+        one, two = read_head(hag.at[j])
+
+        @pl.when(j < 4 * per)
+        def _():
+            rows = pl.ds(pl.multiple_of((j % per) * piece, 16), piece)
+            head_out[rows, pl.ds(pl.multiple_of((j // per) * 128, 128), 128)] = one
+
+        @pl.when(j < 8)
+        def _():
+            small_out[pl.ds(pl.multiple_of(j * SMALL, SMALL), SMALL), :] = two
+
+    loop(n, unpack)
 
     def own_last(k):
         line_conv(z, first_a + k)
@@ -854,30 +881,6 @@
 
     loop(last_b, own_last)
 
-    loop(n - 1, lambda i: came(losses.at[2 + (me + i + 1) % n], l_recv.at[(me + i + 1) % n]))
-    loss_out[...] = lax.fori_loop(0, n, lambda i, acc: acc + losses[2 + i], jnp.zeros((8, 128), F32))
-
-    def other_row(zz):
-        j = zz * 2 + 1 - y
-        came(tag(j), t_recv.at[j])
-
-    loop(nz, other_row)
-    per = 448 // piece
-
-    def unpack(j):
-        one, two = read_head(hag.at[j])
-
-        @pl.when(j < 4 * per)
-        def _():
-            rows = pl.ds(pl.multiple_of((j % per) * piece, 16), piece)
-            head_out[rows, pl.ds(pl.multiple_of((j // per) * 128, 128), 128)] = one
-
-        @pl.when(j < 8)
-        def _():
-            small_out[pl.ds(pl.multiple_of(j * SMALL, SMALL), SMALL), :] = two
-
-    loop(n, unpack)
-
     def drain_w(s):
         k = s % slots_per
         zz, row = s // (2 * slots_per), (s // slots_per) % 2
@@ -913,7 +916,7 @@
         def y_block(k):
             y_copy(zz, k).wait_send()
 
-        loop(first_a + 1, y_block)
+        loop(first_a, y_block)
 
         @pl.when(zz != z)
         def _():
@@ -931,7 +934,7 @@
     for k, peer in enumerate(peers):
         f_copy(peer, k).wait_send()
         g_copy(peer, k).wait_send()
-        q_copy(peer, k).wait_send()
+        loop(TASKS, lambda t, k=k, peer=peer: q_copy(t, peer, k).wait_send())
         s_copy(peer, k).wait_send()
     for l in (1, 2):
         for i in range(2):
@@ -939,6 +942,7 @@
             bx_copy(l, i).wait_send()
     loop(n - 1, lambda i: c_copy(i).wait_send())
     loop(n - 1, lambda i: l_copy(i).wait_send())
+    loop(n - 1, lambda i: p_copy(i).wait_send())
 
 
 def adamw(weight, gradient, moment_one, moment_two, step_rate, step_count):
@@ -979,7 +983,7 @@
     nz = n // 2
     last_b = slots_per // 7
     first_a = slots_per - last_b
-    cargo = slots_per + last_b + 1
+    cargo = slots_per + last_b
     piece = -(-1792 // (n * 16)) * 16
     code = jnp.where(label_mask > 0, labels, -1).reshape(4, 128, TASKS).transpose(0, 2, 1)
     code = jnp.pad(code, ((0, 0), (0, 8 - TASKS), (0, 0)), constant_values=-1)
@@ -1022,19 +1026,21 @@
         vm((27, PX, 128), BF16),
         vm((2, 2, 2, 2, IMG, 128), F32),
         vm((2, 2, 2, IMG, 128), F32),
-        vm((2, 2, IMG, 128), F32),
-        vm((2, 2, IMG, 128), F32),
+        vm((2, 2, IMG, 128), BF16),
+        vm((2, 2, IMG, 128), BF16),
         vm((54, 256, 128), F32),
         vm((n * piece, 128), F32),
         vm((n * SMALL, 128), F32),
-        vm((nz, first_a + 1, CHUNK, 128), jnp.int16),
-        vm((nz, first_a + 1, CHUNK, 128), jnp.int16),
+        vm((n, piece + 48, 128), jnp.int16),
+        vm((n, piece + 48, 128), jnp.int16),
+        vm((nz, first_a, CHUNK, 128), jnp.int16),
+        vm((nz, first_a, CHUNK, 128), jnp.int16),
         vm((nz, cargo, CHUNK, 128), jnp.int16),
         vm((nz, cargo, CHUNK, 128), jnp.int16),
         vm((nz, cargo, CHUNK, 128), jnp.int16),
         vm((max(last_b, 1), CHUNK, 128), jnp.int16),
         vm((max(last_b, 1), CHUNK, 128), jnp.int16),
-        vm((n, CHUNK, 128), jnp.int16),
+        vm((n, piece + 48, 128), jnp.int16),
         vm((256, 128), F32),
         *[dma((n * slots_per,)) for _ in range(4)],
         *[dma((LAYERS + 1, 2, 3)) for _ in range(2)],
@@ -1043,10 +1049,11 @@
         *[dma((n,)) for _ in range(4)],
         dma((3,)), dma((4,)),
         dma((3,)), dma((4,)),
-        dma((3,)), dma((4,)),
+        *[dma((TASKS, k)) for k in (3, 4)],
+        *[dma((n,)) for _ in range(2)],
         dma((3,)), dma((4,)),
         *[dma((2, 2)) for _ in range(4)],
-        *[dma((nz, first_a + 1)) for _ in range(2)],
+        *[dma((nz, first_a)) for _ in range(2)],
         *[dma((nz, cargo)) for _ in range(3)],
         *[dma((max(last_b, 1),)) for _ in range(2)],
         *[dma((n,)) for _ in range(4)],

time: 190 us -> 160 us (0.84)
  Pallas kernels: 172 us -> 142 us
    pallas_call x1, Pallas kernels: 172 us -> 142 us  [per_device(): pl.pallas_call(functools.partial(kernel, n, slots_per), out_shape=(shape(...]
where the time goes in v3:
time: 160 us
  Pallas kernels  142 us (89%)
  other arithmetic  10.5 us (7%)
  local copies, waits for them, and re-layouts  5.66 us (4%)
    pallas_call x1, Pallas kernels, per_device(): pl.pallas_call(functools.partial(kernel, n, slots_per), out_shape=(shape(...  142 us
    sub x4, other arithmetic, adamw(): weight - step_rate * (first_hat / (jnp.sqrt(second_hat) + eps_adam) + dec...  6.02 us
    unnamed x34, local copies, waits for them, and re-layouts  3.86 us

profile of v3, /device:TPU:0, one launch (start us, length us, event | category | flops | bytes accessed | tf_op | source)
XLA Modules:
  0.0 159.7 jit_solution(4398427461515192545)
XLA Ops:
  0.6 0.0 copy-start.14
  0.7 1.3 select_reduce_fusion.inv_ref
  1.9 0.0 copy-done.14
  2.0 0.6 pad.8.affine_ref
  2.6 1.0 compare_select_fusion
  3.5 0.1 reshape.59
  3.7 0.0 copy-start.11
  3.7 0.6 pad.9.code_ref
  4.3 0.1 copy-done.11
  4.4 0.0 copy-start.7
  4.4 0.1 copy.56
  4.5 0.7 copy-done.7
  5.2 0.1 copy.55
  5.4 0.1 pad.13.clone
  5.5 0.1 pad.11.clone
  5.5 0.0 copy-start.3
  5.5 0.8 maximum_maximum_fusion.join_ref
  6.4 0.0 copy-start
  6.4 0.0 copy-start.2
  6.4 142.0 %shard_map.282 = (f32[7,256,128]{2,1,0:T(8,128)}, f32[448,512]{1,0:T(8,128)}, f32[128,128]{1,0:T(8,128)}, f32[8,128]{1,0:T(8,128)}) custom-call(s32[54]{0:T(128)} %slots_ref.1, s32[56]{0:T(128)} %select_reduce_fusion.inv_ref, s32[2,2]{1,0:T(2,128)} %sizes_ref.1, bf16[512,128]{1,0:T(8,128)(2,1)} %bitcast.35, f32[8,128]{1,0:T(8,128)} %pad.8.affine_ref, ...), custom_call_target="tpu_custom_call" | custom-call | tf_op jit(solution)/shard_map/pallas_call | solution.py:1062
  148.4 1.3 slice_reduce_fusion
  150.5 0.0 copy-done.3
  150.5 0.0 copy-done
  150.5 0.0 copy-done.2
  150.5 0.0 copy-start.1
  150.5 0.0 copy-start.4
  150.6 0.0 copy-start.5
  150.6 0.0 copy-start.6
  150.6 3.3 %multiply_subtract_fusion.1 = (f32[7,256,128]{2,1,0:T(8,128)}, f32[7,256,128]{2,1,0:T(8,128)}, f32[7,256,128]{2,1,0:T(8,128)}) fusion(f32[7,256,128]{2,1,0:T(8,128)S(1)} %copy-done, f32[]{:T(128)} %bitcast.5, f32[]{:T(128)} %bitcast.4, f32[7,256,128]{2,1,0:T(8,128)} %get-tuple-element.18, f32[7,256,128]{2,1,0:T(8,128)S(1)} %copy-done.2, ...), kind=kLoop, calls=%fused_computation.6 | loop fusion | flops 3440640 | bytes 6422536 | tf_op jit(solution)/shard_map/sub | solution.py:954
  153.9 0.0 copy-done.1
  153.9 0.0 copy-done.4
  153.9 0.0 copy-done.5
  153.9 0.0 copy-done.6
  153.9 0.0 copy-start.10
  153.9 2.0 %multiply_subtract_fusion = (f32[7,64,512]{2,1,0:T(8,128)}, f32[7,64,512]{2,1,0:T(8,128)}, f32[7,64,512]{2,1,0:T(8,128)}) fusion(f32[7,64,512]{2,1,0:T(8,128)S(1)} %copy-done.1, f32[]{:T(128)} %bitcast.5, f32[]{:T(128)} %bitcast.4, f32[7,64,512]{2,1,0:T(8,128)S(1)} %bitcast.31, f32[7,64,512]{2,1,0:T(8,128)S(1)} %copy-done.4, f32[7,64,512]{2,1,0:T(8,128)S(1)} %copy-done.5), kind=kLoop, calls=%fused_computation.4 | loop fusion | flops 3440640 | bytes 6422536 | tf_op jit(solution)/shard_map/sub | solution.py:954
  155.9 0.0 copy-done.10
  155.9 0.1 reshape.62
  156.1 0.0 copy-start.8
  156.1 0.0 copy-start.9
  156.1 0.8 copy-done.8
  156.9 0.0 copy-done.9
  157.0 0.1 multiply_subtract_fusion.2
  157.1 0.7 copy.62
  157.7 0.7 copy.63
  158.4 0.7 copy.64
  159.0 0.0 copy-done.12
  159.1 0.0 copy-done.13
  159.1 0.6 multiply_subtract_fusion.3
  (8 shorter events, 0.1 us)
Async XLA Ops:
  0.6 1.3 copy-start.14
  3.7 0.7 copy-start.11
  4.4 0.9 copy-start.7
  5.5 145.0 %copy-start.3 = (f32[7,256,128]{2,1,0:T(8,128)S(1)}, f32[7,256,128]{2,1,0:T(8,128)}, u32[]{:S(2)}) copy-start(f32[7,256,128]{2,1,0:T(8,128)} %param.26) | copy-start | bytes 2752516
  6.4 144.1 %copy-start = (f32[7,256,128]{2,1,0:T(8,128)S(1)}, f32[7,256,128]{2,1,0:T(8,128)}, u32[]{:S(2)}) copy-start(f32[7,256,128]{2,1,0:T(8,128)} %conv_ref.1) | copy-start | bytes 2752516
  6.4 144.1 %copy-start.2 = (f32[7,256,128]{2,1,0:T(8,128)S(1)}, f32[7,256,128]{2,1,0:T(8,128)}, u32[]{:S(2)}) copy-start(f32[7,256,128]{2,1,0:T(8,128)} %param.27) | copy-start | bytes 2752516
  150.5 3.3 %copy-start.1 = (f32[7,64,512]{2,1,0:T(8,128)S(1)}, f32[7,64,512]{2,1,0:T(8,128)}, u32[]{:S(2)}) copy-start(f32[7,64,512]{2,1,0:T(8,128)} %head_ref.1) | copy-start | bytes 2752516
  150.5 3.3 %copy-start.4 = (f32[7,64,512]{2,1,0:T(8,128)S(1)}, f32[7,64,512]{2,1,0:T(8,128)}, u32[]{:S(2)}) copy-start(f32[7,64,512]{2,1,0:T(8,128)} %param.30) | copy-start | bytes 2752516
  150.6 3.3 %copy-start.5 = (f32[7,64,512]{2,1,0:T(8,128)S(1)}, f32[7,64,512]{2,1,0:T(8,128)}, u32[]{:S(2)}) copy-start(f32[7,64,512]{2,1,0:T(8,128)} %param.29) | copy-start | bytes 2752516
  150.6 3.3 %copy-start.6 = (f32[448,512]{1,0:T(8,128)S(1)}, f32[448,512]{1,0:T(8,128)}, u32[]{:S(2)}) copy-start(f32[448,512]{1,0:T(8,128)} %get-tuple-element.19) | copy-start | bytes 2752516
  153.9 2.0 %copy-start.10 = (f32[128,128]{1,0:T(8,128)S(1)}, f32[128,128]{1,0:T(8,128)}, u32[]{:S(2)}) copy-start(f32[128,128]{1,0:T(8,128)} %get-tuple-element.20) | copy-start | bytes 196612
  156.1 0.9 copy-start.8
  156.1 0.9 copy-start.9
  158.4 0.7 copy-start.12
  158.4 0.7 copy-start.13

commit v4 on v3

--- a/solution.py
+++ b/solution.py
@@ -17,6 +17,8 @@
 IMG = 256
 HC = 64
 CHUNK = 272
+VMEM_MIB = 60
+STEPS = 2
 SMALL = 16
 
 beta_one = 0.9
@@ -53,18 +55,25 @@
     n,
     slots_per,
     slots_ref,
-    inv_ref,
     sizes_ref,
     inputs_ref,
     affine_ref,
-    code_ref,
+    labels_ref,
+    kept_ref,
+    join_ref,
+    scale_ref,
     conv_ref,
     head_ref,
-    join_ref,
     grad_out,
     head_out,
     small_out,
     loss_out,
+    conv_in,
+    head_in_ref,
+    inv_row,
+    inv_ref,
+    code_ref,
+    flip,
     wall,
     xs,
     xt,
@@ -104,6 +113,7 @@
     brecv2,
     hag,
     zsum,
+    in_sem,
     w_recv,
     w_zr,
     w_zl,
@@ -149,7 +159,9 @@
     nz = n // 2
     last_b = slots_per // 7
     first_a = slots_per - last_b
-    cargo = slots_per + last_b
+    last_r = 2 * slots_per // 7
+    first_r = slots_per - last_r
+    cargo = slots_per + last_r
     piece = hg.shape[0] // n
 
     me = lax.axis_index("dp")
@@ -180,6 +192,13 @@
     def loop(count, body):
         lax.fori_loop(0, count, lambda i, c: (body(i), c)[1], 0)
 
+    def conv_copy(k):
+        return pltpu.make_async_copy(conv_ref.at[k], conv_in.at[k], in_sem.at[k])
+
+    head_copy = pltpu.make_async_copy(head_ref, head_in_ref, in_sem.at[slots_per])
+    inv_copy = pltpu.make_async_copy(inv_row, inv_ref, in_sem.at[slots_per + 1])
+    loop(slots_per, lambda k: conv_copy(k).start())
+    head_copy.start()
     barrier = pltpu.get_barrier_semaphore()
 
     def greet(i):
@@ -190,9 +209,80 @@
         pl.semaphore_signal(barrier, inc=1, device_id=at(chan=peer), device_id_type=MESH)
 
     def cast_block(k):
-        wall[me * slots_per + k] = conv_ref[k].astype(BF16)
+        conv_copy(k).wait()
+        wall[me * slots_per + k] = conv_in[k].astype(BF16)
 
     loop(slots_per, cast_block)
+    pl.semaphore_wait(barrier, n - 1 + 3)
+
+    def to_right(s):
+        return put(wall.at[s], wall.at[s], w_zr.at[s], w_recv.at[s], right)
+
+    def to_left(s):
+        return put(wall.at[s], wall.at[s], w_zl.at[s], w_recv.at[s], left)
+
+    def to_other(s):
+        return put(wall.at[s], wall.at[s], w_y.at[s], w_recv.at[s], other)
+
+    def both_ways(s):
+        @pl.when(has_right)
+        def _():
+            to_right(s).start()
+
+        @pl.when(has_left)
+        def _():
+            to_left(s).start()
+
+    def x_copy(l, i, owner, peer, k):
+        rows = pl.ds(pl.multiple_of(i * IMG, IMG), IMG)
+        ref = xs.at[l, owner, rows, :]
+        return put(ref, ref, x_send.at[l, i, k], x_recv.at[l, i, k], at(chan=peer))
+
+    def x_start(l, i):
+        x_copy(l, i, ch, across, 0).start()
+        x_copy(l, i, ch, partner, 1).start()
+
+    def x_relay(l, i):
+        x_copy(l, i, across, across, 0).wait_recv()
+        x_copy(l, i, across, partner, 2).start()
+
+    def x_arrive(l, i):
+        x_copy(l, i, partner, partner, 1).wait_recv()
+        x_copy(l, i, far, partner, 2).wait_recv()
+
+    def x_drain(l, i):
+        for k in range(3):
+            x_copy(l, i, ch, partner, k).wait_send()
+
+    def h_copy(t, owner, peer, k):
+        ref = hall.at[t, owner]
+        return put(ref, ref, h_send.at[t, k], h_recv.at[t, k], at(chan=peer))
+
+    def j_copy(owner, peer, k):
+        ref = jall.at[:, owner]
+        return put(ref, ref, j_send.at[k], j_recv.at[k], at(chan=peer))
+
+    def a_copy(owner, peer, k):
+        ref = aall.at[owner]
+        return put(ref, ref, a_send.at[k], a_recv.at[k], at(chan=peer))
+
+    def c_copy(i):
+        dev = (me + i + 1) % n
+        return put(cnt.at[me], cnt.at[me], c_send.at[i], c_recv.at[me], at(dp=dev))
+
+    base = me * slots_per
+
+    def own_b(k):
+        to_other(base + first_a + k).start()
+
+    loop(last_b, own_b)
+
+    def own_a(k):
+        both_ways(base + k)
+        to_other(base + k).start()
+
+    loop(first_a, own_a)
+    loop(last_b, lambda k: both_ways(base + first_a + k))
     pixel = lax.broadcasted_iota(jnp.int32, (IMG, 128), 0)
     row_id, col_id = pixel // W, pixel % W
 
@@ -201,15 +291,35 @@
         rows = pl.ds(pl.multiple_of(i * IMG, IMG), IMG)
         mask[rows, :] = jnp.where(inside, 1.0, 0.0)
         xs[0, ch, rows, :] = (inputs_ref[rows, :].astype(F32) * mask[rows, :]).astype(BF16)
+        x_start(0, i)
 
     loop(2, mask_image)
+    head_copy.wait()
 
     def cast_head(t):
-        hall[t, ch] = head_ref[t].astype(BF16)
-        jall[t, ch] = join_ref[t]
+        hall[t, ch] = head_in_ref[t].astype(BF16)
+        h_copy(t, ch, across, 0).start()
+        h_copy(t, ch, partner, 1).start()
 
     loop(TASKS, cast_head)
-    aall[ch] = affine_ref[...]
+    flip[...] = jnp.zeros_like(flip)
+    for t in range(TASKS):
+        flip[0:K, 0:HC] = join_ref[t]
+        flip[32:33, 0:HC] = scale_ref[t : t + 1, :]
+        jall[t, ch] = flip[...].T[0:HC]
+    aall[ch] = jnp.broadcast_to(affine_ref[LAYERS - 1, 0:1, :], (8, 128))
+
+    code = jnp.where(kept_ref[...] > 0, labels_ref[...], -1).astype(F32).astype(BF16).reshape(2 * TASKS * H, W)
+    lane_row = lax.broadcasted_iota(jnp.int32, (W, 128), 1) % W == lax.broadcasted_iota(jnp.int32, (W, 128), 0)
+    wide = dot(code, jnp.where(lane_row, 1.0, 0.0).astype(BF16), NN).reshape(4 * TASKS, 8, 128)
+    own_row = lax.broadcasted_iota(jnp.int32, (1, 8, 128), 1) == lax.broadcasted_iota(jnp.int32, (1, 8, 128), 2) // W
+    rows_of = jnp.sum(jnp.where(own_row, wide, 0.0), axis=1).astype(jnp.int32)
+    code_ref[...] = jnp.full(code_ref.shape, -1, jnp.int32)
+    for b in range(2):
+        for t in range(TASKS):
+            for half in range(2):
+                place = (b * TASKS + t) * 2 + half
+                code_ref[2 * b + half, t : t + 1, :] = rows_of[place : place + 1, :]
 
     lane = lax.broadcasted_iota(jnp.int32, (8, 128), 1)
 
@@ -221,84 +331,12 @@
     total_kept = kept(0) + kept(1) + kept(2) + kept(3)
     cnt[me] = jnp.broadcast_to(jnp.sum(total_kept, axis=1, keepdims=True), (8, 128))
 
-    pl.semaphore_wait(barrier, n - 1 + 3)
-
-    def to_right(s):
-        return put(wall.at[s], wall.at[s], w_zr.at[s], w_recv.at[s], right)
-
-    def to_left(s):
-        return put(wall.at[s], wall.at[s], w_zl.at[s], w_recv.at[s], left)
-
-    def to_other(s):
-        return put(wall.at[s], wall.at[s], w_y.at[s], w_recv.at[s], other)
-
-    def both_ways(s):
-        @pl.when(has_right)
-        def _():
-            to_right(s).start()
-
-        @pl.when(has_left)
-        def _():
-            to_left(s).start()
-
-    def x_copy(l, i, owner, peer, k):
-        rows = pl.ds(pl.multiple_of(i * IMG, IMG), IMG)
-        ref = xs.at[l, owner, rows, :]
-        return put(ref, ref, x_send.at[l, i, k], x_recv.at[l, i, k], at(chan=peer))
-
-    def x_start(l, i):
-        x_copy(l, i, ch, across, 0).start()
-        x_copy(l, i, ch, partner, 1).start()
-
-    def x_relay(l, i):
-        x_copy(l, i, across, across, 0).wait_recv()
-        x_copy(l, i, across, partner, 2).start()
-
-    def x_arrive(l, i):
-        x_copy(l, i, partner, partner, 1).wait_recv()
-        x_copy(l, i, far, partner, 2).wait_recv()
-
-    def x_drain(l, i):
-        for k in range(3):
-            x_copy(l, i, ch, partner, k).wait_send()
-
-    def h_copy(t, owner, peer, k):
-        ref = hall.at[t, owner]
-        return put(ref, ref, h_send.at[t, k], h_recv.at[t, k], at(chan=peer))
-
-    def j_copy(owner, peer, k):
-        ref = jall.at[:, owner]
-        return put(ref, ref, j_send.at[k], j_recv.at[k], at(chan=peer))
-
-    def a_copy(owner, peer, k):
-        ref = aall.at[owner]
-        return put(ref, ref, a_send.at[k], a_recv.at[k], at(chan=peer))
-
-    def c_copy(i):
-        dev = (me + i + 1) % n
-        return put(cnt.at[me], cnt.at[me], c_send.at[i], c_recv.at[me], at(dp=dev))
-
-    base = me * slots_per
-
-    def own_b(k):
-        to_other(base + first_a + k).start()
-
-    loop(last_b, own_b)
-
-    def own_a(k):
-        both_ways(base + k)
-        to_other(base + k).start()
-
-    loop(first_a, own_a)
-    for i in range(2):
-        x_start(0, i)
-
-    def own_head(t):
-        h_copy(t, ch, across, 0).start()
-        h_copy(t, ch, partner, 1).start()
-
-    loop(TASKS, own_head)
-    loop(last_b, lambda k: both_ways(base + first_a + k))
+    found = jnp.full((8, 128), -1, jnp.int32)
+    for u in range(slots_ref.shape[0]):
+        found = jnp.where(lane == slots_ref[u], u, found)
+    inv_row[...] = found
+    inv_copy.start()
+
     for copy in (j_copy, a_copy):
         copy(ch, across, 0).start()
         copy(ch, partner, 1).start()
@@ -358,6 +396,8 @@
     for copy in (j_copy, a_copy):
         copy(across, across, 0).wait_recv()
         copy(across, partner, 2).start()
+
+    inv_copy.wait()
 
     def transpose_layer(l):
         for c in range(4):
@@ -403,7 +443,7 @@
         linear += jnp.where(col_id >= 1, pltpu.roll(zacc[0], 1, 0), 0.0)
         linear += jnp.where(col_id < W - 1, pltpu.roll(zacc[2], IMG - 1, 0), 0.0)
         inside = mask[rows, :]
-        gain, shift = affine_ref[2 * l : 2 * l + 1, :], affine_ref[2 * l + 1 : 2 * l + 2, :]
+        gain, shift = affine_ref[l, 0:1, :], affine_ref[l, 1:2, :]
         passed = jnp.where(linear > 0, inside, 0.0)
         coef[l, rows, :] = passed * gain if l < LAYERS - 1 else passed
         out = (jnp.maximum(linear, 0.0) * gain + shift) * inside
@@ -492,14 +532,15 @@
             q_copy(t, peer, k).start()
         gfeat[...] += dot(grad_hidden, low, TN)
 
-    loop(TASKS, head_task)
+    for t in range(TASKS):
+        head_task(t)
     loss_tile = jnp.broadcast_to(jnp.sum(losses[1], axis=1, keepdims=True), (8, 128))
     jt[TASKS, 0:8, 0:128] = loss_tile
     jt[TASKS, 0:8, 128:256] = loss_tile
 
     my_mask = mask[quarter(ch), :]
     for c in range(4):
-        gsend[c] = (gfeat[:, c * 128 : (c + 1) * 128] * my_mask * aall[c, 4:5, :]).astype(BF16)
+        gsend[c] = (gfeat[:, c * 128 : (c + 1) * 128] * my_mask * aall[c, 0:1, :]).astype(BF16)
 
     def g_copy(peer, k):
         return put(gsend.at[peer], grecv.at[ch], g_send.at[k], g_recv.at[ch], at(chan=peer))
@@ -545,30 +586,27 @@
             gs[l * 9 + 6 + e, pl.ds(top + W, IMG - W), :] = low[: IMG - W]
             gs[l * 9 + 6 + e, pl.ds(top, W), :] = blank
 
-    def conv_backward(l, i):
+    def conv_backward(l, i, h):
         rows = pl.ds(pl.multiple_of(i * IMG, IMG), IMG)
-        lefts = []
+        total = None
         for first in range(0, 9, 2):
             taps = [t for t in (first, first + 1) if t < 9]
-            sides = [gs[l * 9 + t, rows, :] for t in taps]
-            lefts.append(jnp.concatenate(sides, axis=1) if len(sides) > 1 else sides[0])
-        for h in range(2):
-            total = None
-            for first in range(0, 9, 2):
-                taps = [t for t in (first, first + 1) if t < 9]
-                sides = [wall[slots_ref[(l * 9 + t) * 2 + h]] for t in taps]
-                side = jnp.concatenate(sides, axis=1) if len(sides) > 1 else sides[0]
-                term = dot(lefts[first // 2], side, NT)
-                total = term if total is None else total + term
-            bpart[l - 1, i, h, 0] = total[:, :128]
-            bpart[l - 1, i, h, 1] = total[:, 128:]
-
-    def bc_copy(l, i):
+            grads = [gs[l * 9 + t, rows, :] for t in taps]
+            sides = [wall[slots_ref[(l * 9 + t) * 2 + h]] for t in taps]
+            if len(taps) > 1:
+                term = dot(jnp.concatenate(grads, axis=1), jnp.concatenate(sides, axis=1), NT)
+            else:
+                term = dot(grads[0], sides[0], NT)
+            total = term if total is None else total + term
+        bpart[l - 1, i, h, 0] = total[:, :128]
+        bpart[l - 1, i, h, 1] = total[:, 128:]
+
+    def bc_copy(l, i, h):
         return put(
-            bpart.at[l - 1, i, :, 1 - core],
-            bcore.at[l - 1, i],
-            bc_send.at[l - 1, i],
-            bc_recv.at[l - 1, i],
+            bpart.at[l - 1, i, h, 1 - core],
+            bcore.at[l - 1, i, h],
+            bc_send.at[l - 1, i, h],
+            bc_recv.at[l - 1, i, h],
             at(chan=partner),
         )
 
@@ -576,20 +614,20 @@
         return put(bxs.at[l - 1, i], bx.at[l - 1, i], bx_send.at[l - 1, i], bx_recv.at[l - 1, i], at(chan=across))
 
     def weight_grads(l):
-        def half(h):
-            lhs = xt[l, h]
-
-            def pair(p):
-                t = 2 * p
-                rhs = jnp.concatenate([gs[l * 9 + t], gs[l * 9 + t + 1]], axis=1)
-                out = dot(lhs, rhs, NN)
-                dw[(l * 9 + t) * 2 + h] = out[:, :128]
-                dw[(l * 9 + t + 1) * 2 + h] = out[:, 128:]
-
-            loop(4, pair)
-            dw[(l * 9 + 8) * 2 + h] = dot(lhs, gs[l * 9 + 8], NN)
-
-        loop(2, half)
+        lhs = xt[l].reshape(C, PX)
+
+        def pair(p):
+            t = 2 * p
+            rhs = jnp.concatenate([gs[l * 9 + t], gs[l * 9 + t + 1]], axis=1)
+            out = dot(lhs, rhs, NN)
+            for h in range(2):
+                dw[(l * 9 + t) * 2 + h] = out[h * 256 : (h + 1) * 256, :128]
+                dw[(l * 9 + t + 1) * 2 + h] = out[h * 256 : (h + 1) * 256, 128:]
+
+        loop(4, pair)
+        out = dot(lhs, gs[l * 9 + 8], NN)
+        for h in range(2):
+            dw[(l * 9 + 8) * 2 + h] = out[h * 256 : (h + 1) * 256]
 
     def l_copy(i):
         dev = (me + i + 1) % n
@@ -670,24 +708,27 @@
     x_side = ch // 2
     for l in (2, 1):
 
-        def partial_image(i, l=l):
-            conv_backward(l, i)
-            bc_copy(l, i).start()
-
-        loop(2, partial_image)
+        def partial_image(i, h, l=l):
+            conv_backward(l, i, h)
+            bc_copy(l, i, h).start()
 
         def chip_sum(i, l=l):
-            bc_copy(l, i).wait_recv()
+            bc_copy(l, i, 1 - x_side).wait_recv()
             bxs[l - 1, i] = (bpart[l - 1, i, 1 - x_side, core] + bcore[l - 1, i, 1 - x_side]).astype(BF16)
             bx_copy(l, i).start()
 
+        loop(2, lambda i: partial_image(i, 1 - x_side))
         loop(2, chip_sum)
+        loop(2, lambda i: partial_image(i, x_side))
         if l == LAYERS - 1:
             head_grads()
-        weight_grads(l)
+        else:
+            weight_grads(LAYERS - 1)
+            weight_grads(l)
 
         def finish_image(i, l=l):
             bx_copy(l, i).wait_recv()
+            bc_copy(l, i, x_side).wait_recv()
             grad = bpart[l - 1, i, x_side, core] + bcore[l - 1, i, x_side] + bx[l - 1, i].astype(F32)
             rows = pl.ds(pl.multiple_of(i * IMG, IMG), IMG)
             spread(l - 1, i, grad * coef[l - 1, rows, :])
@@ -696,7 +737,7 @@
     weight_grads(0)
 
     def part(dest, k):
-        u = inv_ref[dest * slots_per + k]
+        u = inv_ref[0, dest * slots_per + k]
         return dw[jnp.maximum(u, 0)] * jnp.where(u >= 0, 1.0, 0.0)
 
     def y_copy(zz, k):
@@ -722,7 +763,7 @@
             write(ysend.at[zz, k], part(dest, k))
             y_copy(zz, k).start()
 
-        loop(first_a, block)
+        loop(first_r, block)
 
     def pass_on(zz, k):
         @pl.when(zz > z)
@@ -734,9 +775,9 @@
             z_left(zz, k).start()
 
     def line_conv(zz, k):
-        is_a, is_own = k < first_a, k < slots_per
+        is_a, is_own = k < first_r, k < slots_per
         dest = zz * 2 + jnp.where(is_own, y, 1 - y)
-        slot = jnp.where(is_own, k, k - last_b)
+        slot = jnp.where(is_own, k, k - last_r)
         zsum[...] = part(dest, slot)
 
         @pl.when(is_a)
@@ -820,7 +861,7 @@
         d = nz - 1 - i
 
         def item(c):
-            k = (c + first_a) % cargo
+            k = (c + first_r) % cargo
 
             def send(zz):
                 line_conv(zz, k)
@@ -842,16 +883,17 @@
         write(bsend2.at[k], zsum[...])
         b_copy(k).start()
 
-    loop(last_b, give_b)
+    loop(last_r, give_b)
 
     def own_slot(k):
         line_conv(z, k)
         grad_out[k] = zsum[...]
 
-    loop(first_a, own_slot)
+    loop(first_r, own_slot)
 
     loop(n - 1, lambda i: came(losses.at[2 + (me + i + 1) % n], l_recv.at[(me + i + 1) % n]))
-    loss_out[...] = lax.fori_loop(0, n, lambda i, acc: acc + losses[2 + i], jnp.zeros((8, 128), F32))
+    loss_tile = lax.fori_loop(0, n, lambda i, acc: acc + losses[2 + i], jnp.zeros((8, 128), F32))
+    loss_out[0] = jnp.sum(loss_tile[:TASKS, HC : HC + 1])
 
     def other_row(zz):
         j = zz * 2 + 1 - y
@@ -870,16 +912,20 @@
 
         @pl.when(j < 8)
         def _():
-            small_out[pl.ds(pl.multiple_of(j * SMALL, SMALL), SMALL), :] = two
+            small[pl.ds(pl.multiple_of(j * SMALL, SMALL), SMALL), :] = two
 
     loop(n, unpack)
+    for m in range(4):
+        pair = small[m * 32 : (m + 1) * 32, :]
+        small_out[2 * m] = pair
+        small_out[2 * m + 1] = pltpu.roll(pair, HC, 1)
 
     def own_last(k):
-        line_conv(z, first_a + k)
+        line_conv(z, first_r + k)
         came(brecv2.at[k], b_recv.at[k])
-        grad_out[first_a + k] = zsum[...] + read(brecv2.at[k])
-
-    loop(last_b, own_last)
+        grad_out[first_r + k] = zsum[...] + read(brecv2.at[k])
+
+    loop(last_r, own_last)
 
     def drain_w(s):
         k = s % slots_per
@@ -916,14 +962,14 @@
         def y_block(k):
             y_copy(zz, k).wait_send()
 
-        loop(first_a, y_block)
+        loop(first_r, y_block)
 
         @pl.when(zz != z)
         def _():
             loop(cargo, lambda k: left_it(lsend.at[zz, k], z_send.at[zz, k]))
 
     loop(nz, drain_t)
-    loop(last_b, lambda k: b_copy(k).wait_send())
+    loop(last_r, lambda k: b_copy(k).wait_send())
     for l in range(LAYERS + 1):
         for i in range(2):
             x_drain(l, i)
@@ -938,23 +984,74 @@
         s_copy(peer, k).wait_send()
     for l in (1, 2):
         for i in range(2):
-            bc_copy(l, i).wait_send()
+            for h in range(2):
+                bc_copy(l, i, h).wait_send()
             bx_copy(l, i).wait_send()
     loop(n - 1, lambda i: c_copy(i).wait_send())
     loop(n - 1, lambda i: l_copy(i).wait_send())
     loop(n - 1, lambda i: p_copy(i).wait_send())
 
 
-def adamw(weight, gradient, moment_one, moment_two, step_rate, step_count):
-    step_float = step_count[0].astype(F32)
+def adamw(weight, gradient, moment_one, moment_two, step_rate, one_over, two_over):
     moment_one = beta_one * moment_one + (1.0 - beta_one) * gradient
     moment_two = beta_two * moment_two + (1.0 - beta_two) * gradient * gradient
-    first_hat = moment_one / (1.0 - beta_one**step_float)
-    second_hat = moment_two / (1.0 - beta_two**step_float)
+    first_hat = moment_one * one_over
+    second_hat = moment_two * two_over
     weight = weight - step_rate * (
         first_hat / (jnp.sqrt(second_hat) + eps_adam) + decay_rate * weight
     )
     return (weight, moment_one, moment_two)
+
+
+def update(
+    over_ref,
+    conv_g,
+    conv_w,
+    conv_m,
+    conv_v,
+    head_g,
+    head_w,
+    head_m,
+    head_v,
+    small_g,
+    join_w,
+    join_m,
+    join_v,
+    scale_w,
+    scale_m,
+    scale_v,
+    conv_out,
+    conv_out_m,
+    conv_out_v,
+    head_out,
+    head_out_m,
+    head_out_v,
+    join_out,
+    join_out_m,
+    join_out_v,
+    scale_out,
+    scale_out_m,
+    scale_out_v,
+):
+    one_over, two_over = over_ref[0], over_ref[1]
+
+    def put_all(outs, values):
+        for out, value in zip(outs, values):
+            out[...] = value
+
+    conv = adamw(conv_w[...], conv_g[...], conv_m[...], conv_v[...], 0.01, one_over, two_over)
+    put_all((conv_out, conv_out_m, conv_out_v), conv)
+    head = adamw(head_w[...], head_g[...], head_m[...], head_v[...], 0.03, one_over, two_over)
+    put_all((head_out, head_out_m, head_out_v), head)
+
+    @pl.when(pl.program_id(0) == 0)
+    def _():
+        join_g = small_g[:TASKS, :K, :HC]
+        join = adamw(join_w[...], join_g, join_m[...], join_v[...], 0.4, one_over, two_over)
+        put_all((join_out, join_out_m, join_out_v), join)
+        scale_g = jnp.concatenate([small_g[t, 24:25, :HC] for t in range(TASKS)], axis=0)
+        scale = adamw(scale_w[...], scale_g, scale_m[...], scale_v[...], 0.8, one_over, two_over)
+        put_all((scale_out, scale_out_m, scale_out_v), scale)
 
 
 def per_device(
@@ -981,28 +1078,19 @@
 ):
     slots_per = conv_master.shape[0]
     nz = n // 2
-    last_b = slots_per // 7
-    first_a = slots_per - last_b
-    cargo = slots_per + last_b
+    last_r = 2 * slots_per // 7
+    first_r = slots_per - last_r
+    cargo = slots_per + last_r
     piece = -(-1792 // (n * 16)) * 16
-    code = jnp.where(label_mask > 0, labels, -1).reshape(4, 128, TASKS).transpose(0, 2, 1)
-    code = jnp.pad(code, ((0, 0), (0, 8 - TASKS), (0, 0)), constant_values=-1)
-    units = jnp.arange(unit_slots.shape[0], dtype=jnp.int32)
-    holds = unit_slots[None, :] == jnp.arange(n * slots_per, dtype=jnp.int32)[:, None]
-    slot_units = jnp.max(jnp.where(holds, units[None, :], -1), axis=1)
-    join_pad = jnp.concatenate(
-        [
-            join_master,
-            jnp.zeros((TASKS, HC, 32 - K), F32),
-            scale_master[:, :, None],
-            jnp.zeros((TASKS, HC, 128 - 33), F32),
-        ],
-        axis=2,
-    )
-    affine_pad = jnp.pad(affine.reshape(2 * LAYERS, 128), ((0, 2), (0, 0)))
     vm, dma = pltpu.VMEM, pltpu.SemaphoreType.DMA
     shape = jax.ShapeDtypeStruct
     scratch = [
+        vm((slots_per, 256, 128), F32),
+        vm((TASKS, HC, C), F32),
+        vm((8, 128), jnp.int32),
+        pltpu.SMEM((8, 128), jnp.int32),
+        vm((4, 8, 128), jnp.int32),
+        vm((128, 128), F32),
         vm((n * slots_per, 256, 128), BF16),
         vm((LAYERS + 1, 4, PX, 128), BF16),
         vm((LAYERS, 2, 256, PX), BF16),
@@ -1033,15 +1121,16 @@
         vm((n * SMALL, 128), F32),
         vm((n, piece + 48, 128), jnp.int16),
         vm((n, piece + 48, 128), jnp.int16),
-        vm((nz, first_a, CHUNK, 128), jnp.int16),
-        vm((nz, first_a, CHUNK, 128), jnp.int16),
+        vm((nz, first_r, CHUNK, 128), jnp.int16),
+        vm((nz, first_r, CHUNK, 128), jnp.int16),
         vm((nz, cargo, CHUNK, 128), jnp.int16),
         vm((nz, cargo, CHUNK, 128), jnp.int16),
         vm((nz, cargo, CHUNK, 128), jnp.int16),
-        vm((max(last_b, 1), CHUNK, 128), jnp.int16),
-        vm((max(last_b, 1), CHUNK, 128), jnp.int16),
+        vm((max(last_r, 1), CHUNK, 128), jnp.int16),
+        vm((max(last_r, 1), CHUNK, 128), jnp.int16),
         vm((n, piece + 48, 128), jnp.int16),
         vm((256, 128), F32),
+        dma((slots_per + 2,)),
         *[dma((n * slots_per,)) for _ in range(4)],
         *[dma((LAYERS + 1, 2, 3)) for _ in range(2)],
         *[dma((TASKS, 3)) for _ in range(2)],
@@ -1052,48 +1141,78 @@
         *[dma((TASKS, k)) for k in (3, 4)],
         *[dma((n,)) for _ in range(2)],
         dma((3,)), dma((4,)),
-        *[dma((2, 2)) for _ in range(4)],
-        *[dma((nz, first_a)) for _ in range(2)],
+        *[dma((2, 2, 2)) for _ in range(2)],
+        *[dma((2, 2)) for _ in range(2)],
+        *[dma((nz, first_r)) for _ in range(2)],
         *[dma((nz, cargo)) for _ in range(3)],
-        *[dma((max(last_b, 1),)) for _ in range(2)],
+        *[dma((max(last_r, 1),)) for _ in range(2)],
         *[dma((n,)) for _ in range(4)],
     ]
     in_smem, in_vmem = pl.BlockSpec(memory_space=pltpu.SMEM), pl.BlockSpec(memory_space=pltpu.VMEM)
-    slot_grads, head_total, small_total, loss_total = pl.pallas_call(
+    in_hbm = pl.BlockSpec(memory_space=pltpu.HBM)
+    slot_grads, head_total, small_total, loss = pl.pallas_call(
         functools.partial(kernel, n, slots_per),
         out_shape=(
             shape((slots_per, 256, 128), F32),
             shape((448, C), F32),
-            shape((128, 128), F32),
-            shape((8, 128), F32),
+            shape((8, 32, 128), F32),
+            shape((1,), F32),
         ),
-        in_specs=[in_smem] * 3 + [in_vmem] * 6,
-        out_specs=(in_vmem,) * 4,
+        in_specs=[in_smem] * 2 + [in_vmem] * 6 + [in_hbm] * 2,
+        out_specs=(in_vmem,) * 3 + (in_smem,),
         scratch_shapes=scratch,
         compiler_params=pltpu.CompilerParams(
-            collective_id=0, has_side_effects=True, vmem_limit_bytes=60 * 2**20
+            collective_id=0, has_side_effects=True, vmem_limit_bytes=VMEM_MIB * 2**20
         ),
     )(
         unit_slots,
-        slot_units,
         image_sizes,
         inputs.reshape(PX, 128),
-        affine_pad,
-        code,
+        affine,
+        labels.transpose(0, 3, 1, 2),
+        label_mask.transpose(0, 3, 1, 2),
+        join_master.transpose(0, 2, 1),
+        scale_master,
         conv_master,
         head_master,
-        join_pad,
     )
-    pairs = small_total.reshape(4, 32, 2, HC).transpose(0, 2, 1, 3).reshape(8, 32, HC)[:TASKS]
-    join_total = pairs[:, :K].transpose(0, 2, 1)
-    scale_total = pairs[:, 24]
-    head_total = head_total.reshape(TASKS, HC, C)
-    conv_out = adamw(conv_master, slot_grads, conv_first, conv_second, 0.01, step_count)
-    head_out = adamw(head_master, head_total, head_first, head_second, 0.03, step_count)
-    join_out = adamw(join_master, join_total, join_first, join_second, 0.4, step_count)
-    scale_out = adamw(scale_master, scale_total, scale_first, scale_second, 0.8, step_count)
-    loss = jnp.sum(loss_total[:TASKS, 64])
-    return (loss.reshape(1),) + conv_out + head_out + join_out + scale_out
+    step_float = step_count.astype(F32)
+    over = jnp.concatenate([1.0 / (1.0 - beta_one**step_float), 1.0 / (1.0 - beta_two**step_float)])
+    conv_rows, head_rows = slots_per * 256, TASKS * HC
+    steps = STEPS
+
+    def tile(rows, columns):
+        return pl.BlockSpec((rows // steps, columns), lambda i: (i, 0))
+
+    def whole(*sizes):
+        return pl.BlockSpec(sizes, lambda i: (0,) * len(sizes))
+
+    conv_tile, head_tile = tile(conv_rows, 128), tile(head_rows, C)
+    join_tile, scale_tile = whole(TASKS, K, HC), whole(TASKS, HC)
+    flat_conv = [a.reshape(conv_rows, 128) for a in (slot_grads, conv_master, conv_first, conv_second)]
+    flat_head = [a.reshape(head_rows, C) for a in (head_total, head_master, head_first, head_second)]
+    flat_join = [a.transpose(0, 2, 1) for a in (join_master, join_first, join_second)]
+    out = pl.pallas_call(
+        update,
+        grid=(steps,),
+        out_shape=tuple(
+            [shape((conv_rows, 128), F32)] * 3
+            + [shape((head_rows, C), F32)] * 3
+            + [shape((TASKS, K, HC), F32)] * 3
+            + [shape((TASKS, HC), F32)] * 3
+        ),
+        in_specs=[in_smem]
+        + [conv_tile] * 4
+        + [head_tile] * 4
+        + [whole(8, 32, 128)]
+        + [join_tile] * 3
+        + [scale_tile] * 3,
+        out_specs=tuple([conv_tile] * 3 + [head_tile] * 3 + [join_tile] * 3 + [scale_tile] * 3),
+    )(over, *flat_conv, *flat_head, small_total, *flat_join, scale_master, scale_first, scale_second)
+    conv_out = tuple(a.reshape(slots_per, 256, 128) for a in out[0:3])
+    head_out = tuple(a.reshape(TASKS, HC, C) for a in out[3:6])
+    join_out = tuple(a.transpose(0, 2, 1) for a in out[6:9])
+    return (loss,) + conv_out + head_out + join_out + tuple(out[9:12])
 
 
 def solution(mesh):

time: 160 us -> 147 us (0.919); the launches traced: 160 us -> 145 us
  other arithmetic: 10.5 us -> 0.59 us
  local copies, waits for them, and re-layouts: 5.66 us -> 0 us
  between operations: 1.58 us -> 3.2 us
    pallas_call x1, Pallas kernels: 142 us -> 135 us  [per_device(): pl.pallas_call(functools.partial(kernel, n, slots_per), out_shape=(shape(...]
    sub x4 -> x0, other arithmetic: 6.02 us -> none  [adamw(): weight - step_rate * (first_hat / (jnp.sqrt(second_hat) + eps_adam) + dec...]
    pallas_call x0 -> x1, Pallas kernels: none -> 5.99 us  [per_device(): pl.pallas_call(update, grid=(steps,), out_shape=tuple([shape((conv_rows,...]
    unnamed x34 -> x0, local copies, waits for them, and re-layouts: 3.86 us -> none
where the time goes in v4:
time: 147 us; the launch traced here: 145 us
  Pallas kernels  141 us (96%)
  between operations  3.2 us (2%)
    pallas_call x1, Pallas kernels, per_device(): pl.pallas_call(functools.partial(kernel, n, slots_per), out_shape=(shape(...  135 us
    pallas_call x1, Pallas kernels, per_device(): pl.pallas_call(update, grid=(steps,), out_shape=tuple([shape((conv_rows,...  5.99 us

profile of v4, /device:TPU:0, one launch (start us, length us, event | category | flops | bytes accessed | tf_op | source)
XLA Modules:
  0.0 144.7 jit_solution(113032514008712015)
XLA Ops:
  1.5 0.6 pad_maximum_fusion.over_ref
  2.0 134.9 %shard_map.282 = (f32[7,256,128]{2,1,0:T(8,128)}, f32[448,512]{1,0:T(8,128)}, f32[8,32,128]{2,1,0:T(8,128)}, f32[1]{0:T(128)}) custom-call(s32[54]{0:T(128)} %slots_ref.1, s32[2,2]{1,0:T(2,128)} %sizes_ref.1, bf16[512,128]{1,0:T(8,128)(2,1)} %bitcast.31, f32[3,2,128]{2,1,0:T(2,128)} %affine_ref.1, s32[2,7,16,16]{3,2,1,0:T(8,128)} %bitcast.32, ...), custom_call_target="tpu_custom_call" | custom-call | tf_op jit(solution)/shard_map/pallas_call | solution.py:1153
  136.9 6.0 %shard_map.283 = (f32[1792,128]{1,0:T(8,128)}, f32[1792,128]{1,0:T(8,128)}, f32[1792,128]{1,0:T(8,128)}, f32[448,512]{1,0:T(8,128)}, f32[448,512]{1,0:T(8,128)},...) custom-call(f32[2]{0:T(128)} %pad_maximum_fusion.over_ref, ...), custom_call_target="tpu_custom_call" | custom-call | tf_op jit(solution)/shard_map/pallas_call | solution.py:1195

commit v5 on v4

--- a/solution.py
+++ b/solution.py
@@ -15,6 +15,7 @@
 W = 16
 PX = 512
 IMG = 256
+TALL = IMG + 2 * W
 HC = 64
 CHUNK = 272
 VMEM_MIB = 60
@@ -159,7 +160,7 @@
     nz = n // 2
     last_b = slots_per // 7
     first_a = slots_per - last_b
-    last_r = 2 * slots_per // 7
+    last_r = slots_per // 7
     first_r = slots_per - last_r
     cargo = slots_per + last_r
     piece = hg.shape[0] // n
@@ -201,28 +202,33 @@
     head_copy.start()
     barrier = pltpu.get_barrier_semaphore()
 
-    def greet(i):
-        pl.semaphore_signal(barrier, inc=1, device_id=at(dp=(me + i + 1) % n), device_id_type=MESH)
-
-    loop(n - 1, greet)
     for peer in (partner, across, far):
         pl.semaphore_signal(barrier, inc=1, device_id=at(chan=peer), device_id_type=MESH)
+    pl.semaphore_signal(barrier, inc=1, device_id=other, device_id_type=MESH)
+
+    @pl.when(has_right)
+    def _():
+        pl.semaphore_signal(barrier, inc=1, device_id=right, device_id_type=MESH)
+
+    @pl.when(has_left)
+    def _():
+        pl.semaphore_signal(barrier, inc=1, device_id=left, device_id_type=MESH)
 
     def cast_block(k):
         conv_copy(k).wait()
         wall[me * slots_per + k] = conv_in[k].astype(BF16)
 
     loop(slots_per, cast_block)
-    pl.semaphore_wait(barrier, n - 1 + 3)
+    pl.semaphore_wait(barrier, 4 + jnp.where(has_right, 1, 0) + jnp.where(has_left, 1, 0))
 
     def to_right(s):
-        return put(wall.at[s], wall.at[s], w_zr.at[s], w_recv.at[s], right)
+        return put(wall.at[s], wall.at[s], w_zr.at[0], w_recv.at[s], right)
 
     def to_left(s):
-        return put(wall.at[s], wall.at[s], w_zl.at[s], w_recv.at[s], left)
+        return put(wall.at[s], wall.at[s], w_zl.at[0], w_recv.at[s], left)
 
     def to_other(s):
-        return put(wall.at[s], wall.at[s], w_y.at[s], w_recv.at[s], other)
+        return put(wall.at[s], wall.at[s], w_y.at[0], w_recv.at[s], other)
 
     def both_ways(s):
         @pl.when(has_right)
@@ -236,7 +242,7 @@
     def x_copy(l, i, owner, peer, k):
         rows = pl.ds(pl.multiple_of(i * IMG, IMG), IMG)
         ref = xs.at[l, owner, rows, :]
-        return put(ref, ref, x_send.at[l, i, k], x_recv.at[l, i, k], at(chan=peer))
+        return put(ref, ref, x_send.at[0], x_recv.at[l, i, k], at(chan=peer))
 
     def x_start(l, i):
         x_copy(l, i, ch, across, 0).start()
@@ -250,13 +256,9 @@
         x_copy(l, i, partner, partner, 1).wait_recv()
         x_copy(l, i, far, partner, 2).wait_recv()
 
-    def x_drain(l, i):
-        for k in range(3):
-            x_copy(l, i, ch, partner, k).wait_send()
-
     def h_copy(t, owner, peer, k):
         ref = hall.at[t, owner]
-        return put(ref, ref, h_send.at[t, k], h_recv.at[t, k], at(chan=peer))
+        return put(ref, ref, h_send.at[0], h_recv.at[t, k], at(chan=peer))
 
     def j_copy(owner, peer, k):
         ref = jall.at[:, owner]
@@ -268,7 +270,7 @@
 
     def c_copy(i):
         dev = (me + i + 1) % n
-        return put(cnt.at[me], cnt.at[me], c_send.at[i], c_recv.at[me], at(dp=dev))
+        return put(cnt.at[me], cnt.at[me], c_send.at[0], c_recv.at[me], at(dp=dev))
 
     base = me * slots_per
 
@@ -302,6 +304,9 @@
         h_copy(t, ch, partner, 1).start()
 
     loop(TASKS, cast_head)
+    for i in range(2):
+        gs[:, i * TALL : i * TALL + W, :] = jnp.zeros((9, W, 128), BF16)
+        gs[:, (i + 1) * TALL - W : (i + 1) * TALL, :] = jnp.zeros((9, W, 128), BF16)
     flip[...] = jnp.zeros_like(flip)
     for t in range(TASKS):
         flip[0:K, 0:HC] = join_ref[t]
@@ -340,7 +345,6 @@
     for copy in (j_copy, a_copy):
         copy(ch, across, 0).start()
         copy(ch, partner, 1).start()
-    loop(n - 1, lambda i: c_copy(i).start())
 
     neighbour = (z * 2 + 1 - y) * slots_per
 
@@ -417,6 +421,8 @@
         loop(first_a, block)
 
     loop(nz, last_in)
+
+    loop(n - 1, lambda i: c_copy(i).start())
 
     def conv_forward(l, i):
         rows = pl.ds(pl.multiple_of(i * IMG, IMG), IMG)
@@ -500,7 +506,7 @@
 
     def q_copy(t, peer, k):
         rows = pl.ds(pl.multiple_of(peer * HC, HC), HC)
-        return put(gh.at[t, rows, :], ghall.at[ch, t], q_send.at[t, k], q_recv.at[t, ch], at(chan=peer))
+        return put(gh.at[t, rows, :], ghall.at[ch, t], q_send.at[0], q_recv.at[t, ch], at(chan=peer))
 
     def head_task(t):
         low = hall[t].reshape(4 * HC, C)
@@ -576,22 +582,22 @@
             grad,
             jnp.where(col_id >= 1, pltpu.roll(grad, 1, 0), 0.0),
         )
-        top = pl.multiple_of(i * IMG, IMG)
-        blank = jnp.zeros((W, 128), BF16)
+        top = pl.multiple_of(i * TALL + W, W)
         for e in range(3):
-            low = columns[e].astype(BF16)
-            gs[l * 9 + e, pl.ds(top, IMG - W), :] = low[W:]
-            gs[l * 9 + e, pl.ds(top + IMG - W, W), :] = blank
-            gs[l * 9 + 3 + e, pl.ds(top, IMG), :] = low
-            gs[l * 9 + 6 + e, pl.ds(top + W, IMG - W), :] = low[: IMG - W]
-            gs[l * 9 + 6 + e, pl.ds(top, W), :] = blank
+            gs[l * 3 + e, pl.ds(top, IMG), :] = columns[e].astype(BF16)
+
+    def shifted(l, t, i):
+        a, e = divmod(t, 3) if isinstance(t, int) else (t // 3, t % 3)
+        return gs[l * 3 + e, pl.ds(pl.multiple_of(i * TALL + (2 - a) * W, W), IMG), :]
+
+    def tap_grad(l, t):
+        return jnp.concatenate([shifted(l, t, 0), shifted(l, t, 1)], axis=0)
 
     def conv_backward(l, i, h):
-        rows = pl.ds(pl.multiple_of(i * IMG, IMG), IMG)
         total = None
         for first in range(0, 9, 2):
             taps = [t for t in (first, first + 1) if t < 9]
-            grads = [gs[l * 9 + t, rows, :] for t in taps]
+            grads = [shifted(l, t, i) for t in taps]
             sides = [wall[slots_ref[(l * 9 + t) * 2 + h]] for t in taps]
             if len(taps) > 1:
                 term = dot(jnp.concatenate(grads, axis=1), jnp.concatenate(sides, axis=1), NT)
@@ -618,20 +624,20 @@
 
         def pair(p):
             t = 2 * p
-            rhs = jnp.concatenate([gs[l * 9 + t], gs[l * 9 + t + 1]], axis=1)
+            rhs = jnp.concatenate([tap_grad(l, t), tap_grad(l, t + 1)], axis=1)
             out = dot(lhs, rhs, NN)
             for h in range(2):
                 dw[(l * 9 + t) * 2 + h] = out[h * 256 : (h + 1) * 256, :128]
                 dw[(l * 9 + t + 1) * 2 + h] = out[h * 256 : (h + 1) * 256, 128:]
 
         loop(4, pair)
-        out = dot(lhs, gs[l * 9 + 8], NN)
+        out = dot(lhs, tap_grad(l, 8), NN)
         for h in range(2):
             dw[(l * 9 + 8) * 2 + h] = out[h * 256 : (h + 1) * 256]
 
     def l_copy(i):
         dev = (me + i + 1) % n
-        return put(losses.at[2 + me], losses.at[2 + me], l_send.at[i], l_recv.at[me], at(dp=dev))
+        return put(losses.at[2 + me], losses.at[2 + me], l_send.at[0], l_recv.at[me], at(dp=dev))
 
     def head_part(dest):
         rows = hg[pl.ds(pl.multiple_of(dest * piece, 16), piece), :]
@@ -659,7 +665,7 @@
 
     def p_copy(i):
         dest = (me + i + 1) % n
-        return put(psend.at[dest], precv.at[me], p_send.at[i], p_recv.at[me], at(dp=dest))
+        return put(psend.at[dest], precv.at[me], p_send.at[0], p_recv.at[me], at(dp=dest))
 
     def head_grads():
         for i in range(2):
@@ -741,13 +747,13 @@
         return dw[jnp.maximum(u, 0)] * jnp.where(u >= 0, 1.0, 0.0)
 
     def y_copy(zz, k):
-        return put(ysend.at[zz, k], yrecv.at[zz, k], y_send.at[zz, k], y_recv.at[zz, k], other)
+        return put(ysend.at[zz, k], yrecv.at[zz, k], y_send.at[0], y_recv.at[zz, k], other)
 
     def z_right(zz, k):
-        return put(lsend.at[zz, k], lleft.at[zz, k], z_send.at[zz, k], zl_recv.at[zz, k], right)
+        return put(lsend.at[zz, k], lleft.at[zz, k], z_send.at[0], zl_recv.at[zz, k], right)
 
     def z_left(zz, k):
-        return put(lsend.at[zz, k], lright.at[zz, k], z_send.at[zz, k], zr_recv.at[zz, k], left)
+        return put(lsend.at[zz, k], lright.at[zz, k], z_send.at[0], zr_recv.at[zz, k], left)
 
     def both_sides(d, body):
         for zz, ok in ((z - d, z - d >= 0), (z + d, z + d < nz)):
@@ -795,67 +801,64 @@
             came(lright.at[zz, k], zr_recv.at[zz, k])
             zsum[...] += read(lright.at[zz, k])
 
-    loop(nz - 1, lambda i: both_sides(nz - 1 - i, cross))
-    cross(z)
-
     def tag(j):
         return hag.at[j]
 
     def t_right(j):
-        return put(tag(j), tag(j), t_zr.at[j], t_recv.at[j], right)
+        return put(tag(j), tag(j), t_zr.at[0], t_recv.at[j], right)
 
     def t_left(j):
-        return put(tag(j), tag(j), t_zl.at[j], t_recv.at[j], left)
+        return put(tag(j), tag(j), t_zl.at[0], t_recv.at[j], left)
 
     def t_other(j):
-        return put(tag(j), tag(j), t_y.at[j], t_recv.at[j], other)
-
-    rows, few = head_part(me)
-    zsum[0:piece, :] = rows
-    zsum[piece : piece + SMALL, :] = few
-
-    def add_piece(i):
-        source = (me + i + 1) % n
-        came(precv.at[source], p_recv.at[source])
-        one, two = read_head(precv.at[source])
-        zsum[0:piece, :] += one
-        zsum[piece : piece + SMALL, :] += two
-
-    loop(n - 1, add_piece)
-    write_head(hag.at[me], (zsum[0:piece, :], zsum[piece : piece + SMALL, :]))
-
-    @pl.when(has_right)
-    def _():
-        t_right(me).start()
-
-    @pl.when(has_left)
-    def _():
-        t_left(me).start()
-
-    t_other(me).start()
+        return put(tag(j), tag(j), t_y.at[0], t_recv.at[j], other)
+
+    def both_tags(j):
+        @pl.when(has_right)
+        def _():
+            t_right(j).start()
+
+        @pl.when(has_left)
+        def _():
+            t_left(j).start()
+
+    def sum_head():
+        rows, few = head_part(me)
+        zsum[0:piece, :] = rows
+        zsum[piece : piece + SMALL, :] = few
+
+        def add_piece(i):
+            source = (me + i + 1) % n
+            came(precv.at[source], p_recv.at[source])
+            one, two = read_head(precv.at[source])
+            zsum[0:piece, :] += one
+            zsum[piece : piece + SMALL, :] += two
+
+        loop(n - 1, add_piece)
+        write_head(hag.at[me], (zsum[0:piece, :], zsum[piece : piece + SMALL, :]))
+        t_other(me).start()
+        both_tags(me)
+
+    both_sides(nz - 1, cross)
+    sum_head()
+    loop(nz - 2, lambda i: both_sides(nz - 2 - i, cross))
+    cross(z)
+    neighbour_tag = z * 2 + 1 - y
 
     def tail(d):
-        @pl.when(z - d >= 0)
-        def _():
-            j = (z - d) * 2 + y
-            came(tag(j), t_recv.at[j])
-
-            @pl.when(has_right)
-            def _():
-                t_right(j).start()
-
-            t_other(j).start()
-
-        @pl.when(z + d < nz)
-        def _():
-            j = (z + d) * 2 + y
-            came(tag(j), t_recv.at[j])
-
-            @pl.when(has_left)
-            def _():
-                t_left(j).start()
-
-            t_other(j).start()
+        for row in range(2):
+
+            @pl.when(z - d >= 0)
+            def _(row=row):
+                j = (z - d) * 2 + row
+                came(tag(j), t_recv.at[j])
+                pl.when(has_right)(lambda: t_right(j).start())
+
+            @pl.when(z + d < nz)
+            def _(row=row):
+                j = (z + d) * 2 + row
+                came(tag(j), t_recv.at[j])
+                pl.when(has_left)(lambda: t_left(j).start())
 
     def out_step(i):
         d = nz - 1 - i
@@ -871,7 +874,13 @@
             both_sides(d, send)
 
         loop(cargo, item)
-        tail(i + 1)
+
+        @pl.when(i == 0)
+        def _():
+            came(tag(neighbour_tag), t_recv.at[neighbour_tag])
+            both_tags(neighbour_tag)
+
+        pl.when(i > 0)(lambda: tail(i))
 
     loop(nz - 1, out_step)
 
@@ -889,17 +898,7 @@
         line_conv(z, k)
         grad_out[k] = zsum[...]
 
-    loop(first_r, own_slot)
-
-    loop(n - 1, lambda i: came(losses.at[2 + (me + i + 1) % n], l_recv.at[(me + i + 1) % n]))
-    loss_tile = lax.fori_loop(0, n, lambda i, acc: acc + losses[2 + i], jnp.zeros((8, 128), F32))
-    loss_out[0] = jnp.sum(loss_tile[:TASKS, HC : HC + 1])
-
-    def other_row(zz):
-        j = zz * 2 + 1 - y
-        came(tag(j), t_recv.at[j])
-
-    loop(nz, other_row)
+    tail(nz - 1)
     per = 448 // piece
 
     def unpack(j):
@@ -920,6 +919,12 @@
         small_out[2 * m] = pair
         small_out[2 * m + 1] = pltpu.roll(pair, HC, 1)
 
+    loop(first_r, own_slot)
+
+    loop(n - 1, lambda i: came(losses.at[2 + (me + i + 1) % n], l_recv.at[(me + i + 1) % n]))
+    loss_tile = lax.fori_loop(0, n, lambda i, acc: acc + losses[2 + i], jnp.zeros((8, 128), F32))
+    loss_out[0] = jnp.sum(loss_tile[:TASKS, HC : HC + 1])
+
     def own_last(k):
         line_conv(z, first_r + k)
         came(brecv2.at[k], b_recv.at[k])
@@ -927,69 +932,44 @@
 
     loop(last_r, own_last)
 
-    def drain_w(s):
-        k = s % slots_per
-        zz, row = s // (2 * slots_per), (s // slots_per) % 2
-        on_line = (row == y) | (k >= first_a)
-
-        @pl.when(on_line & has_right & (zz <= z))
-        def _():
-            left_it(wall.at[s], w_zr.at[s])
-
-        @pl.when(on_line & has_left & (zz >= z))
-        def _():
-            left_it(wall.at[s], w_zl.at[s])
-
-        @pl.when((row == y) & ((k < first_a) | (zz == z)))
-        def _():
-            left_it(wall.at[s], w_y.at[s])
-
-    loop(n * slots_per, drain_w)
-
-    def drain_t(zz):
-        j = zz * 2 + y
-
-        @pl.when(has_right & (zz <= z))
-        def _():
-            left_it(tag(j), t_zr.at[j])
-
-        @pl.when(has_left & (zz >= z))
-        def _():
-            left_it(tag(j), t_zl.at[j])
-
-        left_it(tag(j), t_y.at[j])
-
-        def y_block(k):
-            y_copy(zz, k).wait_send()
-
-        loop(first_r, y_block)
-
-        @pl.when(zz != z)
-        def _():
-            loop(cargo, lambda k: left_it(lsend.at[zz, k], z_send.at[zz, k]))
-
-    loop(nz, drain_t)
+    line = slots_per + last_b
+
+    def left_line(zz):
+        @pl.when((z == zz) & has_right)
+        def _():
+            left_it(wall.at[pl.ds(0, (zz + 1) * line)], w_zr.at[0])
+            left_it(hag.at[pl.ds(0, (zz + 1) * 2)], t_zr.at[0])
+
+        @pl.when((z == zz) & has_left)
+        def _():
+            left_it(wall.at[pl.ds(0, (nz - zz) * line)], w_zl.at[0])
+            left_it(hag.at[pl.ds(0, (nz - zz) * 2)], t_zl.at[0])
+
+    for zz in range(nz):
+        left_line(zz)
+    left_it(wall.at[pl.ds(0, nz * first_a + last_b)], w_y.at[0])
+    left_it(hag.at[0], t_y.at[0])
+    left_it(ysend, y_send.at[0])
+    left_it(lsend.at[pl.ds(0, nz - 1)], z_send.at[0])
     loop(last_r, lambda k: b_copy(k).wait_send())
-    for l in range(LAYERS + 1):
-        for i in range(2):
-            x_drain(l, i)
+    left_it(xs.at[pl.ds(0, LAYERS)], x_send.at[0])
+    left_it(hall.at[:, pl.ds(0, 3)], h_send.at[0])
+    left_it(ghall.at[pl.ds(0, 3)], q_send.at[0])
+    left_it(cnt.at[pl.ds(0, n - 1)], c_send.at[0])
+    left_it(losses.at[pl.ds(0, n - 1)], l_send.at[0])
+    left_it(psend.at[pl.ds(0, n - 1)], p_send.at[0])
     for k in range(3):
-        loop(TASKS, lambda t, k=k: h_copy(t, ch, partner, k).wait_send())
         j_copy(ch, partner, k).wait_send()
         a_copy(ch, partner, k).wait_send()
     for k, peer in enumerate(peers):
         f_copy(peer, k).wait_send()
         g_copy(peer, k).wait_send()
-        loop(TASKS, lambda t, k=k, peer=peer: q_copy(t, peer, k).wait_send())
         s_copy(peer, k).wait_send()
     for l in (1, 2):
         for i in range(2):
             for h in range(2):
                 bc_copy(l, i, h).wait_send()
             bx_copy(l, i).wait_send()
-    loop(n - 1, lambda i: c_copy(i).wait_send())
-    loop(n - 1, lambda i: l_copy(i).wait_send())
-    loop(n - 1, lambda i: p_copy(i).wait_send())
 
 
 def adamw(weight, gradient, moment_one, moment_two, step_rate, one_over, two_over):
@@ -1078,7 +1058,7 @@
 ):
     slots_per = conv_master.shape[0]
     nz = n // 2
-    last_r = 2 * slots_per // 7
+    last_r = slots_per // 7
     first_r = slots_per - last_r
     cargo = slots_per + last_r
     piece = -(-1792 // (n * 16)) * 16
@@ -1111,7 +1091,7 @@
         vm((8, 32, 256), F32),
         vm((4, 4, 32, 128), F32),
         vm((4, 4, 32, 128), F32),
-        vm((27, PX, 128), BF16),
+        vm((9, 2 * TALL, 128), BF16),
         vm((2, 2, 2, 2, IMG, 128), F32),
         vm((2, 2, 2, IMG, 128), F32),
         vm((2, 2, IMG, 128), BF16),
@@ -1131,22 +1111,25 @@
         vm((n, piece + 48, 128), jnp.int16),
         vm((256, 128), F32),
         dma((slots_per + 2,)),
-        *[dma((n * slots_per,)) for _ in range(4)],
-        *[dma((LAYERS + 1, 2, 3)) for _ in range(2)],
-        *[dma((TASKS, 3)) for _ in range(2)],
+        dma((n * slots_per,)),
+        *[dma((1,)) for _ in range(3)],
+        dma((1,)), dma((LAYERS + 1, 2, 3)),
+        dma((1,)), dma((TASKS, 3)),
         *[dma((3,)) for _ in range(4)],
-        *[dma((n,)) for _ in range(4)],
+        dma((1,)), dma((n,)),
+        dma((1,)), dma((n,)),
         dma((3,)), dma((4,)),
         dma((3,)), dma((4,)),
-        *[dma((TASKS, k)) for k in (3, 4)],
-        *[dma((n,)) for _ in range(2)],
+        dma((1,)), dma((TASKS, 4)),
+        dma((1,)), dma((n,)),
         dma((3,)), dma((4,)),
         *[dma((2, 2, 2)) for _ in range(2)],
         *[dma((2, 2)) for _ in range(2)],
-        *[dma((nz, first_r)) for _ in range(2)],
-        *[dma((nz, cargo)) for _ in range(3)],
+        dma((1,)), dma((nz, first_r)),
+        dma((1,)), dma((nz, cargo)), dma((nz, cargo)),
         *[dma((max(last_r, 1),)) for _ in range(2)],
-        *[dma((n,)) for _ in range(4)],
+        dma((n,)),
+        *[dma((1,)) for _ in range(3)],
     ]
     in_smem, in_vmem = pl.BlockSpec(memory_space=pltpu.SMEM), pl.BlockSpec(memory_space=pltpu.VMEM)
     in_hbm = pl.BlockSpec(memory_space=pltpu.HBM)

time: 147 us -> 138 us (0.939); the launches traced: 145 us -> 138 us
  Pallas kernels: 141 us -> 134 us
    pallas_call x1, Pallas kernels: 135 us -> 128 us  [per_device(): pl.pallas_call(functools.partial(kernel, n, slots_per), out_shape=(shape(...]
where the time goes in v5:
time: 138 us
  Pallas kernels  134 us (97%)
  between operations  3.2 us (2%)
    pallas_call x1, Pallas kernels, per_device(): pl.pallas_call(functools.partial(kernel, n, slots_per), out_shape=(shape(...  128 us
    pallas_call x1, Pallas kernels, per_device(): pl.pallas_call(update, grid=(steps,), out_shape=tuple([shape((conv_rows,...  5.99 us

profile of v5, /device:TPU:0, one launch (start us, length us, event | category | flops | bytes accessed | tf_op | source)
XLA Modules:
  0.0 137.9 jit_solution(7244942202361309438)
XLA Ops:
  1.5 0.6 pad_maximum_fusion.over_ref
  2.0 128.1 %shard_map.282 = (f32[7,256,128]{2,1,0:T(8,128)}, f32[448,512]{1,0:T(8,128)}, f32[8,32,128]{2,1,0:T(8,128)}, f32[1]{0:T(128)}) custom-call(s32[54]{0:T(128)} %slots_ref.1, s32[2,2]{1,0:T(2,128)} %sizes_ref.1, bf16[512,128]{1,0:T(8,128)(2,1)} %bitcast.31, f32[3,2,128]{2,1,0:T(2,128)} %affine_ref.1, s32[2,7,16,16]{3,2,1,0:T(8,128)} %bitcast.32, ...), custom_call_target="tpu_custom_call" | custom-call | tf_op jit(solution)/shard_map/pallas_call | solution.py:1136
  130.1 6.0 %shard_map.283 = (f32[1792,128]{1,0:T(8,128)}, f32[1792,128]{1,0:T(8,128)}, f32[1792,128]{1,0:T(8,128)}, f32[448,512]{1,0:T(8,128)}, f32[448,512]{1,0:T(8,128)},...) custom-call(f32[2]{0:T(128)} %pad_maximum_fusion.over_ref, ...), custom_call_target="tpu_custom_call" | custom-call | tf_op jit(solution)/shard_map/pallas_call | solution.py:1178

commit v6 on v5

--- a/solution.py
+++ b/solution.py
@@ -1,4 +1,5 @@
 import functools
+import math
 
 import jax
 import jax.numpy as jnp
@@ -149,7 +150,6 @@
     y_recv,
     z_send,
     zr_recv,
-    zl_recv,
     b_send,
     b_recv,
     t_recv,
@@ -258,7 +258,7 @@
 
     def h_copy(t, owner, peer, k):
         ref = hall.at[t, owner]
-        return put(ref, ref, h_send.at[0], h_recv.at[t, k], at(chan=peer))
+        return put(ref, ref, h_send.at[0], h_recv.at[k], at(chan=peer))
 
     def j_copy(owner, peer, k):
         ref = jall.at[:, owner]
@@ -270,7 +270,7 @@
 
     def c_copy(i):
         dev = (me + i + 1) % n
-        return put(cnt.at[me], cnt.at[me], c_send.at[0], c_recv.at[me], at(dp=dev))
+        return put(cnt.at[me], cnt.at[me], c_send.at[0], c_recv.at[0], at(dp=dev))
 
     base = me * slots_per
 
@@ -358,7 +358,6 @@
         x_relay(0, i)
 
     def relay_head(t):
-        h_copy(t, across, across, 0).wait_recv()
         h_copy(t, across, partner, 2).start()
 
     def line_in(d, c):
@@ -393,10 +392,11 @@
                 to_other(s).start()
 
     def first_step(c):
-        pl.when(c < slots_per + last_b)(lambda: line_in(1, c))
-        pl.when(c < TASKS)(lambda: relay_head(c))
-
-    loop(max(slots_per + last_b, TASKS), first_step)
+        line_in(1, c)
+
+    loop(slots_per + last_b, first_step)
+    came(hall.at[:, 0], h_recv.at[0])
+    loop(TASKS, relay_head)
     for copy in (j_copy, a_copy):
         copy(across, across, 0).wait_recv()
         copy(across, partner, 2).start()
@@ -482,15 +482,12 @@
         x_start(LAYERS, i)
     fbuf[ch] = xs[LAYERS, ch, quarter(ch), :]
 
-    loop(n - 1, lambda i: came(cnt.at[(me + i + 1) % n], c_recv.at[(me + i + 1) % n]))
+    came(cnt.at[pl.ds(0, n - 1)], c_recv.at[0])
     counts = lax.fori_loop(0, n, lambda i, acc: acc + cnt[i], jnp.zeros((8, 128), F32))
     counts = jnp.maximum(counts, 1.0)
 
-    def head_in(t):
-        h_copy(t, partner, partner, 1).wait_recv()
-        h_copy(t, far, partner, 2).wait_recv()
-
-    loop(TASKS, head_in)
+    came(hall.at[:, 0], h_recv.at[1])
+    came(hall.at[:, 0], h_recv.at[2])
     for copy in (j_copy, a_copy):
         copy(partner, partner, 1).wait_recv()
         copy(far, partner, 2).wait_recv()
@@ -506,7 +503,7 @@
 
     def q_copy(t, peer, k):
         rows = pl.ds(pl.multiple_of(peer * HC, HC), HC)
-        return put(gh.at[t, rows, :], ghall.at[ch, t], q_send.at[0], q_recv.at[t, ch], at(chan=peer))
+        return put(gh.at[t, rows, :], ghall.at[ch, t], q_send.at[0], q_recv.at[0], at(chan=peer))
 
     def head_task(t):
         low = hall[t].reshape(4 * HC, C)
@@ -611,13 +608,13 @@
         return put(
             bpart.at[l - 1, i, h, 1 - core],
             bcore.at[l - 1, i, h],
-            bc_send.at[l - 1, i, h],
+            bc_send.at[0],
             bc_recv.at[l - 1, i, h],
             at(chan=partner),
         )
 
     def bx_copy(l, i):
-        return put(bxs.at[l - 1, i], bx.at[l - 1, i], bx_send.at[l - 1, i], bx_recv.at[l - 1, i], at(chan=across))
+        return put(bxs.at[l - 1, i], bx.at[l - 1, i], bx_send.at[0], bx_recv.at[l - 1, i], at(chan=across))
 
     def weight_grads(l):
         lhs = xt[l].reshape(C, PX)
@@ -637,7 +634,7 @@
 
     def l_copy(i):
         dev = (me + i + 1) % n
-        return put(losses.at[2 + me], losses.at[2 + me], l_send.at[0], l_recv.at[me], at(dp=dev))
+        return put(losses.at[2 + me], losses.at[2 + me], l_send.at[0], l_recv.at[0], at(dp=dev))
 
     def head_part(dest):
         rows = hg[pl.ds(pl.multiple_of(dest * piece, 16), piece), :]
@@ -665,14 +662,14 @@
 
     def p_copy(i):
         dest = (me + i + 1) % n
-        return put(psend.at[dest], precv.at[me], p_send.at[0], p_recv.at[me], at(dp=dest))
+        return put(psend.at[dest], precv.at[me], p_send.at[0], p_recv.at[0], at(dp=dest))
 
     def head_grads():
         for i in range(2):
             x_arrive(LAYERS, i)
         for peer in peers:
-            loop(TASKS, lambda t, peer=peer: came(ghall.at[peer, t], q_recv.at[t, peer]))
             came(jrecv.at[peer], s_recv.at[peer])
+        came(ghall.at[pl.ds(0, 3)], q_recv.at[0])
         lhs = [
             jnp.concatenate([ghall[2 * m].reshape(TASKS * HC, 128), ghall[2 * m + 1].reshape(TASKS * HC, 128)], axis=1)
             for m in range(2)
@@ -750,7 +747,7 @@
         return put(ysend.at[zz, k], yrecv.at[zz, k], y_send.at[0], y_recv.at[zz, k], other)
 
     def z_right(zz, k):
-        return put(lsend.at[zz, k], lleft.at[zz, k], z_send.at[0], zl_recv.at[zz, k], right)
+        return put(lsend.at[zz, k], lleft.at[zz, k], z_send.at[0], zr_recv.at[zz + 1, k], right)
 
     def z_left(zz, k):
         return put(lsend.at[zz, k], lright.at[zz, k], z_send.at[0], zr_recv.at[zz, k], left)
@@ -793,7 +790,7 @@
 
         @pl.when((zz >= z) & has_left)
         def _():
-            came(lleft.at[zz, k], zl_recv.at[zz, k])
+            came(lleft.at[zz, k], zr_recv.at[zz + 1, k])
             zsum[...] += read(lleft.at[zz, k])
 
         @pl.when((zz <= z) & has_right)
@@ -827,9 +824,10 @@
         zsum[0:piece, :] = rows
         zsum[piece : piece + SMALL, :] = few
 
+        came(precv.at[pl.ds(0, n - 1)], p_recv.at[0])
+
         def add_piece(i):
             source = (me + i + 1) % n
-            came(precv.at[source], p_recv.at[source])
             one, two = read_head(precv.at[source])
             zsum[0:piece, :] += one
             zsum[piece : piece + SMALL, :] += two
@@ -921,7 +919,7 @@
 
     loop(first_r, own_slot)
 
-    loop(n - 1, lambda i: came(losses.at[2 + (me + i + 1) % n], l_recv.at[(me + i + 1) % n]))
+    came(losses.at[pl.ds(0, n - 1)], l_recv.at[0])
     loss_tile = lax.fori_loop(0, n, lambda i, acc: acc + losses[2 + i], jnp.zeros((8, 128), F32))
     loss_out[0] = jnp.sum(loss_tile[:TASKS, HC : HC + 1])
 
@@ -965,11 +963,8 @@
         f_copy(peer, k).wait_send()
         g_copy(peer, k).wait_send()
         s_copy(peer, k).wait_send()
-    for l in (1, 2):
-        for i in range(2):
-            for h in range(2):
-                bc_copy(l, i, h).wait_send()
-            bx_copy(l, i).wait_send()
+    left_it(bcore, bc_send.at[0])
+    left_it(bxs, bx_send.at[0])
 
 
 def adamw(weight, gradient, moment_one, moment_two, step_rate, one_over, two_over):
@@ -984,7 +979,7 @@
 
 
 def update(
-    over_ref,
+    step_ref,
     conv_g,
     conv_w,
     conv_m,
@@ -1013,7 +1008,9 @@
     scale_out_m,
     scale_out_v,
 ):
-    one_over, two_over = over_ref[0], over_ref[1]
+    steps = jnp.full((8, 128), step_ref[0].astype(F32))
+    one_over = (1.0 / (1.0 - jnp.exp(steps * math.log(beta_one))))[0:1, 0:1]
+    two_over = (1.0 / (1.0 - jnp.exp(steps * math.log(beta_two))))[0:1, 0:1]
 
     def put_all(outs, values):
         for out, value in zip(outs, values):
@@ -1027,7 +1024,7 @@
     @pl.when(pl.program_id(0) == 0)
     def _():
         join_g = small_g[:TASKS, :K, :HC]
-        join = adamw(join_w[...], join_g, join_m[...], join_v[...], 0.4, one_over, two_over)
+        join = adamw(join_w[...], join_g, join_m[...], join_v[...], 0.4, one_over[None], two_over[None])
         put_all((join_out, join_out_m, join_out_v), join)
         scale_g = jnp.concatenate([small_g[t, 24:25, :HC] for t in range(TASKS)], axis=0)
         scale = adamw(scale_w[...], scale_g, scale_m[...], scale_v[...], 0.8, one_over, two_over)
@@ -1114,19 +1111,18 @@
         dma((n * slots_per,)),
         *[dma((1,)) for _ in range(3)],
         dma((1,)), dma((LAYERS + 1, 2, 3)),
-        dma((1,)), dma((TASKS, 3)),
+        dma((1,)), dma((3,)),
         *[dma((3,)) for _ in range(4)],
-        dma((1,)), dma((n,)),
-        dma((1,)), dma((n,)),
+        *[dma((1,)) for _ in range(4)],
         dma((3,)), dma((4,)),
         dma((3,)), dma((4,)),
-        dma((1,)), dma((TASKS, 4)),
-        dma((1,)), dma((n,)),
+        *[dma((1,)) for _ in range(2)],
+        *[dma((1,)) for _ in range(2)],
         dma((3,)), dma((4,)),
-        *[dma((2, 2, 2)) for _ in range(2)],
-        *[dma((2, 2)) for _ in range(2)],
+        dma((1,)), dma((2, 2, 2)),
+        dma((1,)), dma((2, 2)),
         dma((1,)), dma((nz, first_r)),
-        dma((1,)), dma((nz, cargo)), dma((nz, cargo)),
+        dma((1,)), dma((nz + 1, cargo)),
         *[dma((max(last_r, 1),)) for _ in range(2)],
         dma((n,)),
         *[dma((1,)) for _ in range(3)],
@@ -1159,8 +1155,6 @@
         conv_master,
         head_master,
     )
-    step_float = step_count.astype(F32)
-    over = jnp.concatenate([1.0 / (1.0 - beta_one**step_float), 1.0 / (1.0 - beta_two**step_float)])
     conv_rows, head_rows = slots_per * 256, TASKS * HC
     steps = STEPS
 
@@ -1191,7 +1185,7 @@
         + [join_tile] * 3
         + [scale_tile] * 3,
         out_specs=tuple([conv_tile] * 3 + [head_tile] * 3 + [join_tile] * 3 + [scale_tile] * 3),
-    )(over, *flat_conv, *flat_head, small_total, *flat_join, scale_master, scale_first, scale_second)
+    )(step_count, *flat_conv, *flat_head, small_total, *flat_join, scale_master, scale_first, scale_second)
     conv_out = tuple(a.reshape(slots_per, 256, 128) for a in out[0:3])
     head_out = tuple(a.reshape(TASKS, HC, C) for a in out[3:6])
     join_out = tuple(a.transpose(0, 2, 1) for a in out[6:9])

time: 138 us -> 137 us (level)
  no operation moved by 1% of the time
where the time goes in v6:
time: 137 us; the launch traced here: 136 us
  Pallas kernels  133 us (97%)
  between operations  3.04 us (2%)
    pallas_call x1, Pallas kernels, per_device(): pl.pallas_call(functools.partial(kernel, n, slots_per), out_shape=(shape(...  127 us
    pallas_call x1, Pallas kernels, per_device(): pl.pallas_call(update, grid=(steps,), out_shape=tuple([shape((conv_rows,...  5.99 us

profile of v6, /device:TPU:0, one launch (start us, length us, event | category | flops | bytes accessed | tf_op | source)
XLA Modules:
  0.0 135.8 jit_solution(2630841145372289357)
XLA Ops:
  1.3 126.8 %shard_map.282 = (f32[7,256,128]{2,1,0:T(8,128)}, f32[448,512]{1,0:T(8,128)}, f32[8,32,128]{2,1,0:T(8,128)}, f32[1]{0:T(128)}) custom-call(s32[54]{0:T(128)} %slots_ref.1, s32[2,2]{1,0:T(2,128)} %sizes_ref.1, bf16[512,128]{1,0:T(8,128)(2,1)} %bitcast.31, f32[3,2,128]{2,1,0:T(2,128)} %affine_ref.1, s32[2,7,16,16]{3,2,1,0:T(8,128)} %bitcast.32, ...), custom_call_target="tpu_custom_call" | custom-call | tf_op jit(solution)/shard_map/pallas_call | solution.py:1132
  128.1 6.0 %shard_map.283 = (f32[1792,128]{1,0:T(8,128)}, f32[1792,128]{1,0:T(8,128)}, f32[1792,128]{1,0:T(8,128)}, f32[448,512]{1,0:T(8,128)}, f32[448,512]{1,0:T(8,128)},...) custom-call(s32[1]{0:T(128)S(6)} %copy.33.step_ref, ...), custom_call_target="tpu_custom_call" | custom-call | tf_op jit(solution)/shard_map/pallas_call | solution.py:1172

commit v7 on v6

--- a/solution.py
+++ b/solution.py
@@ -56,6 +56,20 @@
 def kernel(
     n,
     slots_per,
+    slots_hbm,
+    sizes_hbm,
+    inputs_hbm,
+    affine_hbm,
+    labels_hbm,
+    kept_hbm,
+    join_hbm,
+    scale_hbm,
+    conv_ref,
+    head_ref,
+    grad_out,
+    head_out,
+    small_out,
+    loss_out,
     slots_ref,
     sizes_ref,
     inputs_ref,
@@ -64,12 +78,6 @@
     kept_ref,
     join_ref,
     scale_ref,
-    conv_ref,
-    head_ref,
-    grad_out,
-    head_out,
-    small_out,
-    loss_out,
     conv_in,
     head_in_ref,
     inv_row,
@@ -199,6 +207,21 @@
     head_copy = pltpu.make_async_copy(head_ref, head_in_ref, in_sem.at[slots_per])
     inv_copy = pltpu.make_async_copy(inv_row, inv_ref, in_sem.at[slots_per + 1])
     loop(slots_per, lambda k: conv_copy(k).start())
+    fetched = (
+        (sizes_hbm, sizes_ref),
+        (inputs_hbm, inputs_ref),
+        (slots_hbm, slots_ref),
+        (affine_hbm, affine_ref),
+        (labels_hbm, labels_ref),
+        (kept_hbm, kept_ref),
+        (join_hbm, join_ref),
+        (scale_hbm, scale_ref),
+    )
+    fetches = [
+        pltpu.make_async_copy(src, dst, in_sem.at[slots_per + 2 + i]) for i, (src, dst) in enumerate(fetched)
+    ]
+    for fetch in fetches:
+        fetch.start()
     head_copy.start()
     barrier = pltpu.get_barrier_semaphore()
 
@@ -285,6 +308,8 @@
 
     loop(first_a, own_a)
     loop(last_b, lambda k: both_ways(base + first_a + k))
+    for fetch in fetches:
+        fetch.wait()
     pixel = lax.broadcasted_iota(jnp.int32, (IMG, 128), 0)
     row_id, col_id = pixel // W, pixel % W
 
@@ -1062,6 +1087,13 @@
     vm, dma = pltpu.VMEM, pltpu.SemaphoreType.DMA
     shape = jax.ShapeDtypeStruct
     scratch = [
+        pltpu.SMEM(unit_slots.shape, jnp.int32),
+        pltpu.SMEM(image_sizes.shape, jnp.int32),
+        vm((PX, 128), BF16),
+        vm(affine.shape, F32),
+        *[vm((2, TASKS, H, W), jnp.int32) for _ in range(2)],
+        vm((TASKS, K, HC), F32),
+        vm((TASKS, HC), F32),
         vm((slots_per, 256, 128), F32),
         vm((TASKS, HC, C), F32),
         vm((8, 128), jnp.int32),
@@ -1107,7 +1139,7 @@
         vm((max(last_r, 1), CHUNK, 128), jnp.int16),
         vm((n, piece + 48, 128), jnp.int16),
         vm((256, 128), F32),
-        dma((slots_per + 2,)),
+        dma((slots_per + 10,)),
         dma((n * slots_per,)),
         *[dma((1,)) for _ in range(3)],
         dma((1,)), dma((LAYERS + 1, 2, 3)),
@@ -1137,7 +1169,7 @@
             shape((8, 32, 128), F32),
             shape((1,), F32),
         ),
-        in_specs=[in_smem] * 2 + [in_vmem] * 6 + [in_hbm] * 2,
+        in_specs=[in_hbm] * 10,
         out_specs=(in_vmem,) * 3 + (in_smem,),
         scratch_shapes=scratch,
         compiler_params=pltpu.CompilerParams(

time: 137 us -> 136 us (level)
  no operation moved by 1% of the time
where the time goes in v7:
time: 136 us; the launch traced here: 135 us
  Pallas kernels  132 us (97%)
  between operations  3.04 us (2%)
    pallas_call x1, Pallas kernels, per_device(): pl.pallas_call(functools.partial(kernel, n, slots_per), out_shape=(shape(...  126 us
    pallas_call x1, Pallas kernels, per_device(): pl.pallas_call(update, grid=(steps,), out_shape=tuple([shape((conv_rows,...  5.99 us

profile of v7, /device:TPU:0, one launch (start us, length us, event | category | flops | bytes accessed | tf_op | source)
XLA Modules:
  0.0 134.8 jit_solution(15900525133109301047)
XLA Ops:
  1.3 125.8 %shard_map.282 = (f32[7,256,128]{2,1,0:T(8,128)}, f32[448,512]{1,0:T(8,128)}, f32[8,32,128]{2,1,0:T(8,128)}, f32[1]{0:T(128)}) custom-call(s32[54]{0:T(128)} %slots_hbm.1, s32[2,2]{1,0:T(2,128)} %sizes_hbm.1, bf16[512,128]{1,0:T(8,128)(2,1)} %bitcast.31, f32[3,2,128]{2,1,0:T(2,128)} %affine_hbm.1, s32[2,7,16,16]{3,2,1,0:T(8,128)} %bitcast.32, ...), custom_call_target="tpu_custom_call" | custom-call | tf_op jit(solution)/shard_map/pallas_call | solution.py:1164
  127.1 6.0 %shard_map.283 = (f32[1792,128]{1,0:T(8,128)}, f32[1792,128]{1,0:T(8,128)}, f32[1792,128]{1,0:T(8,128)}, f32[448,512]{1,0:T(8,128)}, f32[448,512]{1,0:T(8,128)},...) custom-call(s32[1]{0:T(128)S(6)} %copy.33.step_ref, ...), custom_call_target="tpu_custom_call" | custom-call | tf_op jit(solution)/shard_map/pallas_call | solution.py:1204
